TPU v7x, 32 devices: a whole 2x2x4 slice. The times are simulated.
32 devices in a mesh: wide: 8 (over y, x, core), narrow: 4 (over z).
Axes of the slice: x: 2, y: 2, z: 4, core: 2. Of those that a mesh axis runs over, the one named last changes fastest.
Arguments:
- hidden: bfloat16 [2, 2048, 768], P(None, 'wide'), may hold values from -6 to 6
- encoded: bfloat16 [2, 6144, 768], P(None, 'wide'), may hold values from -6 to 6
- token_lengths: int32 [2, 8], replicated, may hold values from 64 to 448, as said below
- frame_counts: int32 [2, 8], replicated, may hold values from 36 to 1500, as said below
- ln_gain: float32 [3, 768], replicated, may hold values from 0.1 to 1.9
- ln_bias: float32 [3, 768], replicated, may hold values from -1.5 to 1.5
- head_bias: float32 [4, 768], P(None, 'narrow'), may hold values from -2.5 to 2.5
- out_bias: float32 [3, 768], replicated, may hold values from -1 to 1
- fc_bias: float32 [3072], P('narrow'), may hold values from -2.5 to 2.5
- self_proj: bfloat16 [3, 768, 768], P(None, 'wide', 'narrow'), may hold values from -0.21875 to 0.21875
- cross_proj: bfloat16 [3, 768, 768], P(None, 'wide', 'narrow'), may hold values from -0.21875 to 0.21875
- out_proj: bfloat16 [2, 768, 768], P(None, 'narrow', 'wide'), may hold values from -1.25 to 1.25
- fc_in: bfloat16 [768, 3072], P('wide', 'narrow'), may hold values from -0.21875 to 0.21875
- fc_out: bfloat16 [3072, 768], P('narrow', 'wide'), may hold values from -0.109375 to 0.109375
- cotangent: bfloat16 [2, 2048, 768], P(None, 'wide'), may hold values from -6 to 6
Outputs:
- output: bfloat16 [2, 2048, 768], P(None, 'wide')
- input_grad: float32 [2, 2048, 768], P(None, 'wide')
- encoded_grad: float32 [2, 6144, 768], P(None, 'wide')
- grad_ln_gain: float32 [3, 768], replicated
- grad_ln_bias: float32 [3, 768], replicated
- grad_head_bias: float32 [4, 768], P(None, 'narrow')
- grad_out_bias: float32 [3, 768], replicated
- grad_fc_bias: float32 [3072], P('narrow')
- grad_self_proj: float32 [3, 768, 768], P(None, 'wide', 'narrow')
- grad_cross_proj: float32 [3, 768, 768], P(None, 'wide', 'narrow')
- grad_out_proj: float32 [2, 768, 768], P(None, 'narrow', 'wide')
- grad_fc_in: float32 [768, 3072], P('wide', 'narrow')
- grad_fc_out: float32 [3072, 768], P('narrow', 'wide')
Inputs may be any that keep to these rules, and one draw needn't show every extreme that they name: `token_lengths`: each row holds the token counts of the 8 items of one micro-batch in packing order; a row sums to 2048, the end of item i lies within (192) / 2 tokens of 256 times (i + 1), and item 2 of every row has 448 tokens. `frame_counts`: each row holds the frame counts of the 8 items of one micro-batch in packing order; items 2k and 2k + 1 together have 3 times their tokens, each item's count differs from 3 times its tokens by at most 156, and item 2 of every row has 1500 frames. So the frames of an item lie within the frame shards of the wide indices from two below the first to two above the last that hold its tokens.
All inputs are finite; a program needn't handle non-finite values.
Results may differ from a plain program's by a relative error of at most 0.03.
Values may be sent and summed in bfloat16 or wider, within the bound.
No kernel may reach another device: no remote copies, remote signals or barrier semaphores. Data moves between devices by JAX's collectives and lax.ppermute only.
A program may use at most 192 MiB of HBM per device.

v0:
```python
from functools import partial

import jax
import jax.numpy as jnp
from jax import lax
from jax.sharding import PartitionSpec as P

HD = 64


epsilon = 1e-05


def from_behind(value, axis, steps):
    count = lax.axis_size(axis)
    initial, last = (max(0, -steps), min(count, count - steps))
    return lax.ppermute(value, axis, [(source, source + steps) for source in range(initial, last)])


def layer_norm(values, gain, offset):
    centre = values - jnp.mean(values, axis=-1, keepdims=True)
    spread = jnp.mean(centre * centre, axis=-1, keepdims=True)
    inverse = lax.rsqrt(spread + epsilon)
    unit_rows = centre * inverse
    return (unit_rows * gain + offset, unit_rows, inverse)


def norm_back(grad_rows, unit_rows, inverse, gain):
    scaled = grad_rows * gain
    centred = scaled - jnp.mean(scaled, axis=-1, keepdims=True)
    return (centred - unit_rows * jnp.mean(scaled * unit_rows, axis=-1, keepdims=True)) * inverse


def owners(places, lengths):
    ends = jnp.cumsum(lengths)
    return jnp.sum((places[:, None] >= ends[None, :]).astype(jnp.int32), axis=1)


def attend_sums(queries, key_rows, value_rows, allowed, scaling):
    raw = (
        jnp.einsum("qhc,khc->hqk", queries, key_rows, preferred_element_type=jnp.float32) * scaling
    )
    weights = jnp.where(allowed[None], jnp.exp(raw), 0.0)
    summed = jnp.einsum(
        "hqk,khc->qhc", weights.astype(jnp.bfloat16), value_rows, preferred_element_type=jnp.float32
    )
    return (summed, jnp.sum(weights, axis=2))


def grad_terms(grad_low, output, denominator):
    grad_float = grad_low.astype(jnp.float32)
    grad_sums = (grad_float / denominator.T[:, :, None]).astype(jnp.bfloat16)
    drift = (jnp.sum(grad_float * output, axis=2) / denominator.T).T
    return (grad_sums, drift)


def attend_grads(queries, key_rows, value_rows, allowed, scaling, grad_sums, drift):
    raw = (
        jnp.einsum("qhc,khc->hqk", queries, key_rows, preferred_element_type=jnp.float32) * scaling
    )
    weights = jnp.where(allowed[None], jnp.exp(raw), 0.0)
    grad_prob = jnp.einsum(
        "qhc,khc->hqk", grad_sums, value_rows, preferred_element_type=jnp.float32
    )
    grad_score = (weights * (grad_prob - drift[:, :, None])).astype(jnp.bfloat16)
    grad_q = (
        jnp.einsum("hqk,khc->qhc", grad_score, key_rows, preferred_element_type=jnp.float32)
        * scaling
    )
    grad_k = (
        jnp.einsum("hqk,qhc->khc", grad_score, queries, preferred_element_type=jnp.float32)
        * scaling
    )
    grad_v = jnp.einsum(
        "hqk,qhc->khc", weights.astype(jnp.bfloat16), grad_sums, preferred_element_type=jnp.float32
    )
    return (grad_q, grad_k, grad_v)


def head_total(partial_rows):
    return lax.psum(partial_rows, "narrow")


def earlier_keys(rows):
    found = []
    current = rows
    for step in range(2):
        current = from_behind(current, "wide", 1)
        found.append(current)
    return jnp.concatenate([found[1], found[0], rows], axis=0)


def frames_near(rows):
    lower = []
    upper = []
    going_down = rows
    going_up = rows
    for step in range(2):
        going_down = from_behind(going_down, "wide", 1)
        going_up = from_behind(going_up, "wide", -1)
        lower.append(going_down)
        upper.append(going_up)
    return jnp.concatenate([lower[1], lower[0], rows, upper[0], upper[1]], axis=0)


def return_prior(farther, nearer):
    carried = farther
    for extra in (nearer, None):
        carried = from_behind(carried.astype(jnp.bfloat16), "wide", -1).astype(carried.dtype)
        if extra is not None:
            carried = carried + extra
    return carried


def return_lower(farther, nearer):
    carried = farther
    for extra in (nearer, None):
        carried = from_behind(carried.astype(jnp.bfloat16), "wide", -1).astype(carried.dtype)
        if extra is not None:
            carried = carried + extra
    return carried


def return_upper(farther, nearer):
    carried = farther
    for extra in (nearer, None):
        carried = from_behind(carried.astype(jnp.bfloat16), "wide", 1).astype(carried.dtype)
        if extra is not None:
            carried = carried + extra
    return carried


def body(
    hidden,
    encoded,
    token_lengths,
    frame_counts,
    ln_gain,
    ln_bias,
    head_bias,
    out_bias,
    fc_bias,
    self_proj,
    cross_proj,
    out_proj,
    fc_in,
    fc_out,
    cotangent,
):
    tok_rows = hidden.shape[1]
    frame_rows = encoded.shape[1]
    width = head_bias.shape[1]
    heads_here = width // HD
    scaling = HD ** (-0.5)
    position = lax.axis_index("wide")
    all_frames = frame_rows * lax.axis_size("wide")
    tok_places = position * tok_rows + jnp.arange(tok_rows, dtype=jnp.int32)
    key_places = position * tok_rows - 2 * tok_rows + jnp.arange(3 * tok_rows, dtype=jnp.int32)
    frame_places = (position - 2) * frame_rows + jnp.arange(5 * frame_rows, dtype=jnp.int32)
    inside = (frame_places >= 0) & (frame_places < all_frames)
    gelu_exact = partial(jax.nn.gelu, approximate=False)
    grad_gain = jnp.zeros(ln_gain.shape, jnp.float32)
    grad_shift = jnp.zeros(ln_bias.shape, jnp.float32)
    grad_heads = jnp.zeros(head_bias.shape, jnp.float32)
    grad_outs = jnp.zeros(out_bias.shape, jnp.float32)
    grad_units = jnp.zeros(fc_bias.shape, jnp.float32)
    shard_sums = (
        jnp.zeros(self_proj.shape, jnp.float32),
        jnp.zeros(cross_proj.shape, jnp.float32),
        jnp.zeros(out_proj.shape, jnp.float32),
        jnp.zeros(fc_in.shape, jnp.float32),
        jnp.zeros(fc_out.shape, jnp.float32),
    )
    outputs = []
    input_grads = []
    frame_grads = []
    for microbatch in range(hidden.shape[0]):
        lengths = token_lengths[microbatch]
        counts = frame_counts[microbatch]
        tok_item = owners(tok_places, lengths)
        key_item = owners(key_places, lengths)
        frame_item = jnp.where(inside, owners(frame_places, counts), -1)
        allowed_self = (
            (key_places[None, :] <= tok_places[:, None])
            & (key_item[None, :] == tok_item[:, None])
            & (key_places[None, :] >= 0)
        )
        allowed_cross = tok_item[:, None] == frame_item[None, :]
        self_w, cross_w, out_w, in_w, back_w = (
            lax.all_gather(self_proj, "wide", axis=1, tiled=True),
            lax.all_gather(cross_proj, "wide", axis=1, tiled=True),
            lax.all_gather(out_proj, "wide", axis=2, tiled=True),
            lax.all_gather(fc_in, "wide", axis=0, tiled=True),
            lax.all_gather(fc_out, "wide", axis=1, tiled=True),
        )
        residual = hidden[microbatch].astype(jnp.float32)
        norm_one, unit_one, inverse_one = layer_norm(residual, ln_gain[0], ln_bias[0])
        low_one = norm_one.astype(jnp.bfloat16)
        self_mixed = jnp.einsum("td,sdw->stw", low_one, self_w, preferred_element_type=jnp.float32)
        query_low = (self_mixed[0] + head_bias[0]).astype(jnp.bfloat16)
        key_low = self_mixed[1].astype(jnp.bfloat16)
        value_low = (self_mixed[2] + head_bias[1]).astype(jnp.bfloat16)
        key_values = jnp.concatenate([key_low, value_low], axis=1)
        joined = earlier_keys(key_values)
        query_heads = query_low.reshape(tok_rows, heads_here, HD)
        key_heads = joined[:, :width].reshape(3 * tok_rows, heads_here, HD)
        value_heads = joined[:, width:].reshape(3 * tok_rows, heads_here, HD)
        self_sum, self_den = attend_sums(query_heads, key_heads, value_heads, allowed_self, scaling)
        self_out = self_sum / self_den.T[:, :, None]
        low_self = self_out.reshape(tok_rows, width).astype(jnp.bfloat16)
        residual_one = residual + (
            head_total(jnp.dot(low_self, out_w[0], preferred_element_type=jnp.float32))
            + out_bias[0]
        )
        norm_two, unit_two, inverse_two = layer_norm(residual_one, ln_gain[1], ln_bias[1])
        low_two = norm_two.astype(jnp.bfloat16)
        cross_heads = (
            (jnp.dot(low_two, cross_w[0], preferred_element_type=jnp.float32) + head_bias[2])
            .astype(jnp.bfloat16)
            .reshape(tok_rows, heads_here, HD)
        )
        frames_low = encoded[microbatch]
        frame_mixed = jnp.einsum(
            "fd,sdw->sfw", frames_low, cross_w[1:], preferred_element_type=jnp.float32
        )
        key_frames = jnp.concatenate(
            [
                frame_mixed[0].astype(jnp.bfloat16),
                (frame_mixed[1] + head_bias[3]).astype(jnp.bfloat16),
            ],
            axis=1,
        )

        def frame_section(whole, section):
            portion = whole[section * frame_rows : (section + 1) * frame_rows]
            key_part = portion[:, :width].reshape(frame_rows, heads_here, HD)
            value_part = portion[:, width:].reshape(frame_rows, heads_here, HD)
            allowed = allowed_cross[:, section * frame_rows : (section + 1) * frame_rows]
            return (allowed, key_part, value_part)

        frame_halo = frames_near(key_frames)
        cross_sum = jnp.zeros((tok_rows, heads_here, HD), jnp.float32)
        cross_den = jnp.zeros((heads_here, tok_rows), jnp.float32)
        for section in range(5):
            allowed, key_part, value_part = frame_section(frame_halo, section)
            part_sum, part_den = attend_sums(cross_heads, key_part, value_part, allowed, scaling)
            cross_sum = cross_sum + part_sum
            cross_den = cross_den + part_den
        cross_out = cross_sum / cross_den.T[:, :, None]
        low_cross = cross_out.reshape(tok_rows, width).astype(jnp.bfloat16)
        residual_two = residual_one + (
            head_total(jnp.dot(low_cross, out_w[1], preferred_element_type=jnp.float32))
            + out_bias[1]
        )
        norm_three, unit_three, inverse_three = layer_norm(residual_two, ln_gain[2], ln_bias[2])
        low_three = norm_three.astype(jnp.bfloat16)
        pre_act = jnp.dot(low_three, in_w, preferred_element_type=jnp.float32) + fc_bias
        low_act = gelu_exact(pre_act).astype(jnp.bfloat16)
        final = residual_two + (
            head_total(jnp.dot(low_act, back_w, preferred_element_type=jnp.float32)) + out_bias[2]
        )
        outputs.append(final.astype(jnp.bfloat16))
        self_w, cross_w, out_w, in_w, back_w = (
            lax.all_gather(self_proj, "wide", axis=1, tiled=True),
            lax.all_gather(cross_proj, "wide", axis=1, tiled=True),
            lax.all_gather(out_proj, "wide", axis=2, tiled=True),
            lax.all_gather(fc_in, "wide", axis=0, tiled=True),
            lax.all_gather(fc_out, "wide", axis=1, tiled=True),
        )
        grad_three = cotangent[microbatch].astype(jnp.float32)
        grad_outs = grad_outs.at[2].add(jnp.sum(grad_three, axis=0))
        low_grad_three = grad_three.astype(jnp.bfloat16)
        back_grad = jnp.einsum(
            "tf,td->fd", low_act, low_grad_three, preferred_element_type=jnp.float32
        )
        grad_act = jnp.einsum(
            "td,fd->tf", low_grad_three, back_w, preferred_element_type=jnp.float32
        )
        gelu_pull = jax.vjp(gelu_exact, pre_act)[1]
        grad_pre = gelu_pull(grad_act)[0].astype(jnp.bfloat16)
        grad_units = grad_units + jnp.sum(grad_pre.astype(jnp.float32), axis=0)
        in_grad = jnp.einsum("td,tf->df", low_three, grad_pre, preferred_element_type=jnp.float32)
        grad_norm_three = head_total(
            jnp.einsum("tf,df->td", grad_pre, in_w, preferred_element_type=jnp.float32)
        )
        grad_gain = grad_gain.at[2].add(jnp.sum(grad_norm_three * unit_three, axis=0))
        grad_shift = grad_shift.at[2].add(jnp.sum(grad_norm_three, axis=0))
        grad_two = grad_three + norm_back(grad_norm_three, unit_three, inverse_three, ln_gain[2])
        grad_outs = grad_outs.at[1].add(jnp.sum(grad_two, axis=0))
        low_grad_two = grad_two.astype(jnp.bfloat16)
        cross_out_grad = jnp.einsum(
            "tw,td->wd", low_cross, low_grad_two, preferred_element_type=jnp.float32
        )
        grad_cross_out = jnp.einsum(
            "td,wd->tw", low_grad_two, out_w[1], preferred_element_type=jnp.float32
        )
        grad_cross_out = grad_cross_out.astype(jnp.bfloat16).reshape(tok_rows, heads_here, HD)
        cross_gsum, cross_drift = grad_terms(grad_cross_out, cross_out, cross_den)
        grad_query_c = jnp.zeros((tok_rows, heads_here, HD), jnp.float32)
        pair_blocks = []
        for section in range(5):
            allowed, key_part, value_part = frame_section(frame_halo, section)
            part_q, part_k, part_v = attend_grads(
                cross_heads, key_part, value_part, allowed, scaling, cross_gsum, cross_drift
            )
            grad_query_c = grad_query_c + part_q
            pair_blocks.append(
                jnp.concatenate(
                    [part_k.reshape(frame_rows, width), part_v.reshape(frame_rows, width)], axis=1
                )
            )
        frame_sum = (
            pair_blocks[2]
            + return_lower(pair_blocks[0], pair_blocks[1])
            + return_upper(pair_blocks[4], pair_blocks[3])
        )
        kv_grads = jnp.stack([frame_sum[:, :width], frame_sum[:, width:]]).astype(jnp.bfloat16)
        cq_grads = grad_query_c.reshape(tok_rows, width).astype(jnp.bfloat16)
        grad_heads = grad_heads.at[2].add(jnp.sum(cq_grads.astype(jnp.float32), axis=0))
        grad_heads = grad_heads.at[3].add(jnp.sum(kv_grads[1].astype(jnp.float32), axis=0))
        cross_grad = jnp.concatenate(
            [
                jnp.einsum("td,tw->dw", low_two, cq_grads, preferred_element_type=jnp.float32)[
                    None
                ],
                jnp.einsum("fd,sfw->sdw", frames_low, kv_grads, preferred_element_type=jnp.float32),
            ],
            axis=0,
        )
        grad_norm_two, grad_frames = (
            lax.psum(
                jnp.einsum(
                    "tw,dw->td", cq_grads, cross_w[0], preferred_element_type=jnp.float32
                ).astype(jnp.bfloat16),
                "narrow",
            ).astype(jnp.float32),
            lax.psum(
                jnp.einsum(
                    "sfw,sdw->fd", kv_grads, cross_w[1:], preferred_element_type=jnp.float32
                ).astype(jnp.bfloat16),
                "narrow",
            ).astype(jnp.float32),
        )
        frame_grads.append(grad_frames)
        grad_gain = grad_gain.at[1].add(jnp.sum(grad_norm_two * unit_two, axis=0))
        grad_shift = grad_shift.at[1].add(jnp.sum(grad_norm_two, axis=0))
        grad_one = grad_two + norm_back(grad_norm_two, unit_two, inverse_two, ln_gain[1])
        grad_outs = grad_outs.at[0].add(jnp.sum(grad_one, axis=0))
        low_grad_one = grad_one.astype(jnp.bfloat16)
        self_out_grad = jnp.einsum(
            "tw,td->wd", low_self, low_grad_one, preferred_element_type=jnp.float32
        )
        grad_self_out = jnp.einsum(
            "td,wd->tw", low_grad_one, out_w[0], preferred_element_type=jnp.float32
        )
        grad_self_out = grad_self_out.astype(jnp.bfloat16).reshape(tok_rows, heads_here, HD)
        self_gsum, self_drift = grad_terms(grad_self_out, self_out, self_den)
        grad_q, grad_k, grad_v = attend_grads(
            query_heads, key_heads, value_heads, allowed_self, scaling, self_gsum, self_drift
        )
        pair_grads = jnp.concatenate(
            [grad_k.reshape(3 * tok_rows, width), grad_v.reshape(3 * tok_rows, width)], axis=1
        )
        own_grads = pair_grads[2 * tok_rows :] + return_prior(
            pair_grads[:tok_rows], pair_grads[tok_rows : 2 * tok_rows]
        )
        self_stack = jnp.stack(
            [grad_q.reshape(tok_rows, width), own_grads[:, :width], own_grads[:, width:]]
        ).astype(jnp.bfloat16)
        grad_heads = grad_heads.at[0].add(jnp.sum(self_stack[0].astype(jnp.float32), axis=0))
        grad_heads = grad_heads.at[1].add(jnp.sum(self_stack[2].astype(jnp.float32), axis=0))
        self_grad = jnp.einsum(
            "td,stw->sdw", low_one, self_stack, preferred_element_type=jnp.float32
        )
        grad_norm_one = head_total(
            jnp.einsum("stw,sdw->td", self_stack, self_w, preferred_element_type=jnp.float32)
        )
        grad_gain = grad_gain.at[0].add(jnp.sum(grad_norm_one * unit_one, axis=0))
        grad_shift = grad_shift.at[0].add(jnp.sum(grad_norm_one, axis=0))
        input_grads.append(grad_one + norm_back(grad_norm_one, unit_one, inverse_one, ln_gain[0]))
        out_grad = jnp.stack([self_out_grad, cross_out_grad])
        shards = (
            lax.psum_scatter(self_grad, "wide", scatter_dimension=1, tiled=True),
            lax.psum_scatter(cross_grad, "wide", scatter_dimension=1, tiled=True),
            lax.psum_scatter(out_grad, "wide", scatter_dimension=2, tiled=True),
            lax.psum_scatter(in_grad, "wide", scatter_dimension=0, tiled=True),
            lax.psum_scatter(back_grad, "wide", scatter_dimension=1, tiled=True),
        )
        shard_sums = jax.tree.map(jnp.add, shard_sums, shards)
    vectors = lax.psum((grad_gain, grad_shift, grad_heads, grad_outs, grad_units), "wide")
    return (
        jnp.stack(outputs),
        jnp.stack(input_grads),
        jnp.stack(frame_grads),
        vectors[0],
        vectors[1],
        vectors[2],
        vectors[3],
        vectors[4],
        shard_sums[0],
        shard_sums[1],
        shard_sums[2],
        shard_sums[3],
        shard_sums[4],
    )


def solution(mesh):
    in_specs = (
        P(None, "wide", None),
        P(None, "wide", None),
        P(),
        P(),
        P(),
        P(),
        P(None, "narrow"),
        P(),
        P("narrow"),
        P(None, "wide", "narrow"),
        P(None, "wide", "narrow"),
        P(None, "narrow", "wide"),
        P("wide", "narrow"),
        P("narrow", "wide"),
        P(None, "wide", None),
    )
    out_specs = (
        P(None, "wide", None),
        P(None, "wide", None),
        P(None, "wide", None),
        P(),
        P(),
        P(None, "narrow"),
        P(),
        P("narrow"),
        P(None, "wide", "narrow"),
        P(None, "wide", "narrow"),
        P(None, "narrow", "wide"),
        P("wide", "narrow"),
        P("narrow", "wide"),
    )
    return jax.shard_map(body, mesh=mesh, in_specs=in_specs, out_specs=out_specs, check_vma=False)
```

profile of v0, /device:TPU:0, one launch (start us, length us, event | category | flops | bytes accessed | tf_op | source)
XLA Modules:
  0.0 830.4 jit_solution(2062097832989884951)
XLA Ops:
  9.1 14.6 %all_gather.12 = bf16[3,768,192]{2,0,1:T(4,128)(2,1)S(1)} all-gather(bf16[3,96,192]{2,0,1:T(4,128)(2,1)S(1)} %copy.61), channel_id=1, replica_groups=mesh['wide'=8,'narrow'=4] {'wide'}, dimensions={1}, use_global_device_ids=true | all-gather | bytes 995328 | tf_op jit(solution)/shard_map/all_gather | solution.py:191
  36.6 20.2 %all_gather.10 = bf16[3,768,192]{2,0,1:T(4,128)(2,1)} all-gather(bf16[3,96,192]{2,0,1:T(4,128)(2,1)S(1)} %copy.57), channel_id=1, replica_groups=mesh['wide'=8,'narrow'=4] {'wide'}, dimensions={1}, use_global_device_ids=true | all-gather | bytes 995328 | tf_op jit(solution)/shard_map/all_gather | solution.py:190
  67.9 5.8 collective-permute-start.6
  83.7 9.5 %all_gather.11 = bf16[2,192,768]{1,0,2:T(2,128)(2,1)S(1)} all-gather(bf16[2,192,96]{1,0,2:T(2,128)(2,1)S(1)} %copy.59), channel_id=1, replica_groups=mesh['wide'=8,'narrow'=4] {'wide'}, dimensions={2}, use_global_device_ids=true | all-gather | bytes 663552 | tf_op jit(solution)/shard_map/all_gather | solution.py:192
  108.5 3.9 collective-permute-start.7
  123.9 5.8 collective-permute-start.3
  134.8 5.0 collective-permute-start.9
  147.9 52.4 %all-reduce.22.cloned.1.call-done = (f32[256,768]{1,0:T(8,128)}, f32[256,768]{1,0:T(8,128)}) async-done(((f32[256,768]{1,0:T(8,128)}, f32[256,768]{1,0:T(8,128)}), (f32[256,768]{1,0:T(8,128)}, f32[256,768]{1,0:T(8,128)})) %all-reduce.22.cloned.1.call-update) | async-done | bytes 1572880 | tf_op jit(solution)/shard_map/psum | solution.py:81
  230.3 67.5 %all-reduce.20.cloned.1.call-done = (f32[256,768]{1,0:T(8,128)}, f32[256,768]{1,0:T(8,128)}) async-done(((f32[256,768]{1,0:T(8,128)}, f32[256,768]{1,0:T(8,128)}), (f32[256,768]{1,0:T(8,128)}, f32[256,768]{1,0:T(8,128)})) %all-reduce.20.cloned.1.call-update) | async-done | bytes 1572880 | tf_op jit(solution)/shard_map/psum | solution.py:81
  301.9 4.7 multiply_convert_fusion.13
  319.0 68.2 %all-reduce.18.cloned.1.call-done = (f32[256,768]{1,0:T(8,128)}, f32[256,768]{1,0:T(8,128)}) async-done(((f32[256,768]{1,0:T(8,128)}, f32[256,768]{1,0:T(8,128)}), (f32[256,768]{1,0:T(8,128)}, f32[256,768]{1,0:T(8,128)})) %all-reduce.18.cloned.1.call-update) | async-done | bytes 1572880 | tf_op jit(solution)/shard_map/psum | solution.py:81
  428.4 3.7 collective-permute-start.22
  441.4 4.3 collective-permute-start.19
  447.3 4.7 collective-permute-start.23
  469.7 4.2 copy.72
  473.9 4.7 reshape.1398
  478.9 124.6 %all-reduce.24.cloned.1.call-done = (bf16[256,768]{1,0:T(8,128)(2,1)}, bf16[256,768]{1,0:T(8,128)(2,1)}, bf16[1,768,768]{2,1,0:T(8,128)(2,1)}, bf16[1,768,768]{2,1,0:T(8,128)(2,1)}) async-done(((bf16[256,768]{1,0:T(8,128)(2,1)}, bf16[256,768]{1,0:T(8,128)(2,1)}, bf16[1,768,768]{2,1,0:T(8,128)(2,1)}, bf16[1,768,768]{2,1,0:T(8,128)(2,1)}), (bf16[256,768]{1,0:T(8,128)(2,1)}, bf16[256,768]{1,0:T(8,128)(2,1)}, ...) | async-done | bytes 3145744 | tf_op jit(solution)/shard_map/psum | solution.py:331
  614.7 3.5 copy.74
  646.7 4.2 copy.70
  650.9 4.7 reshape.1396
  695.0 4.2 maximum_convert_fusion
  702.2 12.2 %reduce-scatter.16.cloned.1.call-done = f32[96,576]{1,0:T(8,128)} async-done(((f32[768,576]{1,0:T(8,128)}), f32[96,576]{1,0:T(8,128)}) %reduce-scatter.16.cloned.1.call-update) | async-done | bytes 221200
  716.3 73.1 %all-reduce.16.cloned.1.call-done = (f32[256,768]{1,0:T(8,128)}, f32[256,768]{1,0:T(8,128)}, f32[256,768]{1,0:T(8,128)}, f32[256,768]{1,0:T(8,128)}) async-done(((f32[256,768]{1,0:T(8,128)}, f32[256,768]{1,0:T(8,128)}, f32[256,768]{1,0:T(8,128)}, f32[256,768]{1,0:T(8,128)}), (f32[256,768]{1,0:T(8,128)}, f32[256,768]{1,0:T(8,128)}, f32[256,768]{1,0:T(8,128)}, ...) | async-done | bytes 3145744 | tf_op jit(solution)/shard_map/psum | solution.py:81
  792.4 25.3 %all-reduce.4 = (f32[3,768]{1,0:T(4,128)}, f32[3,768]{1,0:T(4,128)}, f32[4,192]{1,0:T(4,128)}, f32[3,768]{1,0:T(4,128)}, f32[768]{0:T(1024)}) all-reduce(f32[3,768]{1,0:T(4,128)S(1)} %scatter-add.95, f32[3,768]{1,0:T(4,128)S(1)} %scatter-add.105, f32[4,192]{1,0:T(4,128)S(1)} %copy-done.205, ...), channel_id=1, replica_groups=mesh['wide'=8,'narrow'=4] {'wide'}, use_global_device_ids=true, to_apply=%region_70.71 | all-reduce | flops 8448 | bytes 67584 | tf_op jit(solution)/shard_map/psum | solution.py:390
  (940 shorter events, 280.3 us)
Async XLA Ops:
  8.0 192.2 %all-reduce.22.cloned.1.call-start = ((), (), s32[]{:S(2)}) async-start(), calls=%async_computation.15 | async-start | bytes 3145728 | tf_op jit(solution)/shard_map/psum | solution.py:81
  31.5 90.7 %collective-permute-start.2 = (bf16[768,384]{0,1:T(8,128)(2,1)}, bf16[768,384]{0,1:T(8,128)(2,1)}, u32[]{:S(2)}, u32[]{:S(2)}) collective-permute-start(bf16[768,384]{0,1:T(8,128)(2,1)} %pad_maximum_fusion.2), channel_id=1, source_target_pairs={{0,4},{4,8},{8,12},{12,16},{16,20},{20,24},{24,28},{1,5},{5,9},{9,... | collective-permute-start | bytes 1769480 | tf_op jit(solution)/shard_map/ppermute | solution.py:17
  34.5 95.2 %collective-permute-start.4 = (bf16[768,384]{0,1:T(8,128)(2,1)}, bf16[768,384]{0,1:T(8,128)(2,1)}, u32[]{:S(2)}, u32[]{:S(2)}) collective-permute-start(bf16[768,384]{0,1:T(8,128)(2,1)} %pad_maximum_fusion.2), channel_id=1, source_target_pairs={{4,0},{8,4},{12,8},{16,12},{20,16},{24,20},{28,24},{5,1},{9,5},{13... | collective-permute-start | bytes 1769480 | tf_op jit(solution)/shard_map/ppermute | solution.py:17
  64.3 39.9 %collective-permute-start = (bf16[256,384]{0,1:T(8,128)(2,1)}, bf16[256,384]{0,1:T(8,128)(2,1)}, u32[]{:S(2)}, u32[]{:S(2)}) collective-permute-start(bf16[256,384]{0,1:T(8,128)(2,1)} %pad_maximum_fusion.18), channel_id=1, source_target_pairs={{0,4},{4,8},{8,12},{12,16},{16,20},{20,24},{24,28},{1,5},{5,9},{9,... | collective-permute-start | bytes 589832 | tf_op jit(solution)/shard_map/ppermute | solution.py:17
  67.9 39.1 %collective-permute-start.6 = (bf16[256,384]{0,1:T(8,128)(2,1)}, bf16[256,384]{0,1:T(8,128)(2,1)}, u32[]{:S(2)}, u32[]{:S(2)}) collective-permute-start(bf16[256,384]{0,1:T(8,128)(2,1)} %pad_maximum_fusion.19), channel_id=1, source_target_pairs={{0,4},{4,8},{8,12},{12,16},{16,20},{20,24},{24,28},{1,5},{5,9},{9,... | collective-permute-start | bytes 589832 | tf_op jit(solution)/shard_map/ppermute | solution.py:17
  74.6 58.3 %collective-permute-start.8 = (bf16[768,384]{0,1:T(8,128)(2,1)}, bf16[768,384]{0,1:T(8,128)(2,1)}, u32[]{:S(2)}, u32[]{:S(2)}) collective-permute-start(bf16[768,384]{0,1:T(8,128)(2,1)} %pad_maximum_fusion.3), channel_id=1, source_target_pairs={{0,4},{4,8},{8,12},{12,16},{16,20},{20,24},{24,28},{1,5},{5,9},{9,... | collective-permute-start | bytes 1769480 | tf_op jit(solution)/shard_map/ppermute | solution.py:17
  107.1 32.7 %collective-permute-start.10 = (bf16[768,384]{0,1:T(8,128)(2,1)}, bf16[768,384]{0,1:T(8,128)(2,1)}, u32[]{:S(2)}, u32[]{:S(2)}) collective-permute-start(bf16[768,384]{0,1:T(8,128)(2,1)} %pad_maximum_fusion.3), channel_id=1, source_target_pairs={{4,0},{8,4},{12,8},{16,12},{20,16},{24,20},{28,24},{5,1},{9,5},{13... | collective-permute-start | bytes 1769480 | tf_op jit(solution)/shard_map/ppermute | solution.py:17
  122.1 175.7 %all-reduce.20.cloned.1.call-start = ((), (), s32[]{:S(2)}) async-start(), calls=%async_computation.14 | async-start | bytes 3145728 | tf_op jit(solution)/shard_map/psum | solution.py:81
  123.9 19.0 %collective-permute-start.3 = (bf16[768,384]{0,1:T(8,128)(2,1)}, bf16[768,384]{0,1:T(8,128)(2,1)S(1)}, u32[]{:S(2)}, u32[]{:S(2)}) collective-permute-start(bf16[768,384]{0,1:T(8,128)(2,1)} %collective-permute-done.2), channel_id=1, source_target_pairs={{0,4},{4,8},{8,12},{12,16},{16,20},{20,24},{24,28},{1,5},{5,9},{9,... | collective-permute-start | bytes 1769480 | tf_op jit(solution)/shard_map/ppermute | solution.py:17
  229.1 72.7 %all-gather.3.cloned.1.call-start = ((), (), s32[]{:S(2)}) async-start(), calls=%async_computation.5 | async-start | bytes 1327104 | tf_op jit(solution)/shard_map/all_gather | solution.py:193
  229.7 80.3 %all-gather.5.cloned.1.call-start = ((), (), s32[]{:S(2)}) async-start(), calls=%async_computation.6 | async-start | bytes 1327104 | tf_op jit(solution)/shard_map/all_gather | solution.py:194
  230.3 157.0 %all-reduce.18.cloned.1.call-start = ((), (), s32[]{:S(2)}) async-start(), calls=%async_computation.13 | async-start | bytes 3145728 | tf_op jit(solution)/shard_map/psum | solution.py:81
  318.5 285.0 %all-reduce.24.cloned.1.call-start = ((), (), s32[]{:S(2)}) async-start(), calls=%async_computation.16 | async-start | bytes 6291456 | tf_op jit(solution)/shard_map/psum | solution.py:331
  421.1 18.7 %collective-permute-start.16 = (bf16[768,384]{0,1:T(8,128)(2,1)S(1)}, bf16[768,384]{0,1:T(8,128)(2,1)S(1)}, u32[]{:S(2)}, u32[]{:S(2)}) collective-permute-start(bf16[768,384]{0,1:T(8,128)(2,1)S(1)} %pad_maximum_fusion.4), channel_id=1, source_target_pairs={{4,0},{8,4},{12,8},{16,12},{20,16},{24,20},{28,24},{5,1},{9,5},{13... | collective-permute-start | bytes 1769480 | tf_op jit(solution)/shard_map/ppermute | solution.py:17
  422.8 18.5 %collective-permute-start.18 = (bf16[768,384]{0,1:T(8,128)(2,1)S(1)}, bf16[768,384]{0,1:T(8,128)(2,1)S(1)}, u32[]{:S(2)}, u32[]{:S(2)}) collective-permute-start(bf16[768,384]{0,1:T(8,128)(2,1)S(1)} %pad_maximum_fusion.5), channel_id=1, source_target_pairs={{0,4},{4,8},{8,12},{12,16},{16,20},{20,24},{24,28},{1,5},{5,9},{9,... | collective-permute-start | bytes 1769480 | tf_op jit(solution)/shard_map/ppermute | solution.py:17
  426.7 18.9 %collective-permute-start.20 = (bf16[768,384]{0,1:T(8,128)(2,1)S(1)}, bf16[768,384]{0,1:T(8,128)(2,1)S(1)}, u32[]{:S(2)}, u32[]{:S(2)}) collective-permute-start(bf16[768,384]{0,1:T(8,128)(2,1)S(1)} %pad_maximum_fusion.7), channel_id=1, source_target_pairs={{4,0},{8,4},{12,8},{16,12},{20,16},{24,20},{28,24},{5,1},{9,5},{13... | collective-permute-start | bytes 1769480 | tf_op jit(solution)/shard_map/ppermute | solution.py:17
  428.4 18.7 %collective-permute-start.22 = (bf16[768,384]{0,1:T(8,128)(2,1)S(1)}, bf16[768,384]{0,1:T(8,128)(2,1)S(1)}, u32[]{:S(2)}, u32[]{:S(2)}) collective-permute-start(bf16[768,384]{0,1:T(8,128)(2,1)S(1)} %pad_maximum_fusion.8), channel_id=1, source_target_pairs={{0,4},{4,8},{8,12},{12,16},{16,20},{20,24},{24,28},{1,5},{5,9},{9,... | collective-permute-start | bytes 1769480 | tf_op jit(solution)/shard_map/ppermute | solution.py:17
  439.9 13.1 %collective-permute-start.17 = (bf16[768,384]{0,1:T(8,128)(2,1)S(1)}, bf16[768,384]{0,1:T(8,128)(2,1)S(1)}, u32[]{:S(2)}, u32[]{:S(2)}) collective-permute-start(bf16[768,384]{0,1:T(8,128)(2,1)S(1)} %fusion.8), channel_id=1, source_target_pairs={{4,0},{8,4},{12,8},{16,12},{20,16},{24,20},{28,24},{5,1},{9,5},{13... | collective-permute-start | bytes 1769480 | tf_op jit(solution)/shard_map/ppermute | solution.py:17
  459.3 218.8 %reduce-scatter.18.cloned.1.call-start = ((), (), s32[]{:S(2)}) async-start(), calls=%async_computation.10 | async-start | bytes 2211840
  478.6 221.7 %reduce-scatter.20.cloned.1.call-start = ((), (), s32[]{:S(2)}) async-start(), calls=%async_computation.11 | async-start | bytes 1327104
  632.9 81.6 %reduce-scatter.16.cloned.1.call-start = ((), (), s32[]{:S(2)}) async-start(), calls=%async_computation.9 | async-start | bytes 2211840
  655.7 133.8 %all-reduce.16.cloned.1.call-start = ((), (), s32[]{:S(2)}) async-start(), calls=%async_computation.12 | async-start | bytes 6291456 | tf_op jit(solution)/shard_map/psum | solution.py:81
  663.8 159.1 %reduce-scatter.12.cloned.1.call-start = ((), (), s32[]{:S(2)}) async-start(), calls=%async_computation.7 | async-start | bytes 2654208 | tf_op jit(solution)/shard_map/reduce_scatter | solution.py:386
  668.3 154.6 %reduce-scatter.14.cloned.1.call-start = ((), (), s32[]{:S(2)}) async-start(), calls=%async_computation.8 | async-start | bytes 2654208 | tf_op jit(solution)/shard_map/reduce_scatter | solution.py:387
  (289 other events, 1646.2 us)
Sparse Core Ops, SparseCore 0:
  122.2 78.0 all-reduce.21
  229.2 68.5 all-reduce.19
  318.7 68.5 all-reduce.17
  459.4 144.0 all-reduce.23
  663.9 125.5 all-reduce.15
Sparse Core Ops, SparseCore 1:
  231.5 22.9 all-gather.2
  256.2 23.9 all-gather.4
  478.7 62.5 reduce-scatter.17
  633.0 37.8 reduce-scatter.19
  674.3 40.1 reduce-scatter.15
  718.8 42.3 reduce-scatter.11
  764.9 42.4 reduce-scatter.13
where the time goes:
time: 843 us; the launch traced here: 830 us
  waiting for transfers between devices  405 us (48%)
  local copies, waits for them, and re-layouts  117 us (14%)
  matrix products  104 us (12%)
  blocking collectives  69.7 us (8%)
  starting transfers between devices  64.6 us (8%)
  other arithmetic  51.7 us (6%)
  between operations  19 us (2%)
    psum x4, waiting for transfers between devices, head_total(): return lax.psum(partial_rows, 'narrow')  261 us
    psum x1, waiting for transfers between devices, body(): lax.psum(jnp.einsum('tw,dw->td', cq_grads, cross_w[0], preferred_element_...  125 us
    unnamed x573, local copies, waits for them, and re-layouts  77.1 us
    ppermute x24, starting transfers between devices, from_behind(): lax.ppermute(value, axis, [(source, source + steps) for source in range(i...  63.2 us
    psum x1, blocking collectives, body(): lax.psum((grad_gain, grad_shift, grad_heads, grad_outs, grad_units), 'wide')  25.3 us
    all_gather x1, blocking collectives, body(): lax.all_gather(self_proj, 'wide', axis=1, tiled=True)  20.2 us
  transfers between devices with their start and end apart: 36, of which 11 were waited for; matrix products, arithmetic and copies ran while one was open for 21% of the time, Pallas kernels for 0%

commit v1 on v0

v1 whole, which is shorter than its diff:
```python
from functools import partial

import jax
import jax.numpy as jnp
from jax import lax
from jax.experimental import pallas as pl
from jax.experimental.pallas import tpu as pltpu
from jax.sharding import PartitionSpec as P

HD = 64
LANES = 128
MAXLEN = 448
JITTER = 156
EPSILON = 1e-05
F32 = jnp.float32
BF16 = jnp.bfloat16
NN = (((1,), (0,)), ((), ()))
NT = (((1,), (1,)), ((), ()))
TN = (((0,), (0,)), ((), ()))
AXES = ("wide", "narrow")


def mm(left, right, dims=NN):
    return lax.dot_general(left, right, dims, preferred_element_type=F32)


def normalise(values):
    centre = values - jnp.mean(values, axis=-1, keepdims=True)
    spread = jnp.mean(centre * centre, axis=-1, keepdims=True)
    inverse = lax.rsqrt(spread + EPSILON)
    return centre * inverse, inverse


def norm_back(grad_rows, unit_rows, inverse, gain):
    scaled = grad_rows * gain
    centred = scaled - jnp.mean(scaled, axis=-1, keepdims=True)
    return (centred - unit_rows * jnp.mean(scaled * unit_rows, axis=-1, keepdims=True)) * inverse


def erf(x):
    x = jnp.clip(x, -3.832506856900711, 3.832506856900711)
    x2 = x * x
    top = x2 * 0.00022905065861350646 + 0.0034082910107109506
    top = top * x2 + 0.050955695062380861
    top = top * x2 + 0.18520832239976145
    top = top * x2 + 1.128379143519084
    low = x2 * -1.1791602954361697e-7 + 0.000023547966471313185
    low = low * x2 + 0.0010179625278914885
    low = low * x2 + 0.014070470171167667
    low = low * x2 + 0.11098505178285362
    low = low * x2 + 0.49746925110067538
    low = low * x2 + 1.0
    return x * top / low


def fetch(scalars, blocks, whole, sems):
    rows = blocks[0].shape[0]
    here = scalars[0]
    copies = []
    for j, block in enumerate(blocks):
        at = pl.multiple_of(rows * jnp.bitwise_xor(here, j), rows)
        copies.append(pltpu.make_async_copy(block, whole.at[pl.ds(at, rows), :], sems.at[j]))
    for copy in copies:
        copy.start()
    return copies


def first_half(shape):
    return lax.broadcasted_iota(jnp.int32, shape, len(shape) - 1) < HD


def self_forward(
    scalars, hidden, gains, shifts, biases, w0, w1, w2, w3,
    norm_out, q_out, k_out, v_out, o_out, den_out, part_out, whole, sems,
):
    copies = fetch(scalars, (w0, w1, w2, w3), whole, sems)
    rows = hidden.shape[0]
    pairs = q_out.shape[0]
    cols = pairs * LANES
    unit, _ = normalise(hidden[...].astype(F32))
    norm = (unit * gains[0:1, :] + shifts[0:1, :]).astype(BF16)
    norm_out[...] = norm
    lo, hi = scalars[1], scalars[2]
    place = lax.broadcasted_iota(jnp.int32, (rows, 1), 0)
    valid = (place >= lo) & (place < hi)
    for copy in copies:
        copy.wait()
    query = (mm(norm, whole[:, :cols]) + biases[0:1, :]).astype(BF16).astype(F32)
    query = jnp.where(valid, query * HD ** -0.5, 0.0).astype(BF16)
    key = mm(norm, whole[:, cols : 2 * cols]).astype(BF16)
    value = (mm(norm, whole[:, 2 * cols : 3 * cols]) + biases[1:2, :]).astype(BF16)
    for p in range(pairs):
        q_out[p] = query[:, p * LANES : (p + 1) * LANES]
        k_out[p] = key[:, p * LANES : (p + 1) * LANES]
        v_out[p] = value[:, p * LANES : (p + 1) * LANES]
    q_place = lax.broadcasted_iota(jnp.int32, (rows, rows), 0)
    k_place = lax.broadcasted_iota(jnp.int32, (rows, rows), 1)
    allowed = (k_place <= q_place) & (k_place >= lo)
    half = first_half((rows, LANES))
    zero = jnp.zeros((), BF16)

    def one_pair(p, carry):
        q_pair, k_pair, v_pair = q_out[p], k_out[p], v_out[p]
        outs, dens = [], []
        for keep in (half, jnp.logical_not(half)):
            raw = mm(jnp.where(keep, q_pair, zero), k_pair, NT)
            weights = jnp.where(allowed, jnp.exp(raw), 0.0)
            total = jnp.sum(weights, axis=1, keepdims=True)
            total = jnp.where(total > 0.0, total, 1.0)
            outs.append(mm(weights.astype(BF16), v_pair) / total)
            dens.append(jnp.broadcast_to(total, (rows, LANES)))
        o_out[p] = jnp.where(half, outs[0], outs[1])
        den_out[p] = jnp.where(half, dens[0], dens[1])
        return carry

    lax.fori_loop(0, pairs, one_pair, 0)
    low = jnp.concatenate([o_out[p] for p in range(pairs)], axis=1).astype(BF16)
    part_out[...] = mm(low, whole[:, 3 * cols :], NT).astype(BF16)


def frame_project(scalars, frames, biases, w0, w1, w2, w3, k_out, v_out, whole, sems):
    copies = fetch(scalars, (w0, w1, w2, w3), whole, sems)
    pairs = k_out.shape[0]
    cols = pairs * LANES
    for copy in copies:
        copy.wait()
    key = mm(frames[...], whole[:, cols : 2 * cols]).astype(BF16)
    for p in range(pairs):
        k_out[p] = key[:, p * LANES : (p + 1) * LANES]
    value = (mm(frames[...], whole[:, 2 * cols : 3 * cols]) + biases[3:4, :]).astype(BF16)
    for p in range(pairs):
        v_out[p] = value[:, p * LANES : (p + 1) * LANES]


def cross_forward(
    scalars, hidden, mine, other, gains, shifts, outs_bias, biases, k_all, v_all, w0, w1, w2, w3,
    resid_out, norm_out, q_out, o_out, den_out, part_out, whole, sems,
):
    copies = fetch(scalars, (w0, w1, w2, w3), whole, sems)
    rows = hidden.shape[0]
    pairs = q_out.shape[0]
    cols = pairs * LANES
    summed = mine[...].astype(F32) + other[...].astype(F32)
    resid = hidden[...].astype(F32) + (summed + outs_bias[0:1, :])
    resid_out[...] = resid
    unit, _ = normalise(resid)
    norm = (unit * gains[1:2, :] + shifts[1:2, :]).astype(BF16)
    norm_out[...] = norm
    place = lax.broadcasted_iota(jnp.int32, (rows, 1), 0)
    valid = (place >= scalars[1]) & (place < scalars[2])
    for copy in copies:
        copy.wait()
    query = (mm(norm, whole[:, :cols]) + biases[2:3, :]).astype(BF16).astype(F32)
    query = jnp.where(valid, query * HD ** -0.5, 0.0).astype(BF16)
    for p in range(pairs):
        q_out[p] = query[:, p * LANES : (p + 1) * LANES]
    frame = lax.broadcasted_iota(jnp.int32, (1, k_all.shape[1]), 1)
    allowed = (frame >= scalars[3]) & (frame < scalars[4])
    half = first_half((rows, LANES))
    zero = jnp.zeros((), BF16)

    def one_pair(p, carry):
        q_pair, k_pair, v_pair = q_out[p], k_all[p], v_all[p]
        outs, dens = [], []
        for keep in (half, jnp.logical_not(half)):
            raw = mm(jnp.where(keep, q_pair, zero), k_pair, NT)
            weights = jnp.where(allowed, jnp.exp(raw), 0.0)
            total = jnp.sum(weights, axis=1, keepdims=True)
            outs.append(mm(weights.astype(BF16), v_pair) / total)
            dens.append(jnp.broadcast_to(total, (rows, LANES)))
        o_out[p] = jnp.where(half, outs[0], outs[1])
        den_out[p] = jnp.where(half, dens[0], dens[1])
        return carry

    lax.fori_loop(0, pairs, one_pair, 0)
    low = jnp.concatenate([o_out[p] for p in range(pairs)], axis=1).astype(BF16)
    part_out[...] = mm(low, whole[:, 3 * cols :], NT).astype(BF16)


CHUNK = 256


def unit_forward(
    scalars, resid, mine, other, gains, shifts, outs_bias, fc_bias, cotangent,
    a0, a1, a2, a3, d0, d1, d2, d3,
    resid_out, norm_out, act_out, pre_out, part_out, back_out, sum_out,
    whole_in, whole_back, sems_in, sems_back,
):
    copies = fetch(scalars, (a0, a1, a2, a3), whole_in, sems_in)
    copies += fetch(scalars, (d0, d1, d2, d3), whole_back, sems_back)
    summed = mine[...].astype(F32) + other[...].astype(F32)
    resid_two = resid[...] + (summed + outs_bias[1:2, :])
    resid_out[...] = resid_two
    unit, _ = normalise(resid_two)
    norm_out[...] = (unit * gains[2:3, :] + shifts[2:3, :]).astype(BF16)
    for copy in copies:
        copy.wait()

    def one_chunk(j, carry):
        at = pl.ds(pl.multiple_of(j * CHUNK, CHUNK), CHUNK)
        pre = mm(norm_out[...], whole_in[:, at]) + fc_bias[:, at]
        cdf = 0.5 * (1.0 + erf(pre * 0.7071067811865476))
        act_out[:, at] = (pre * cdf).astype(BF16)
        slope = cdf + pre * (jnp.exp(-0.5 * pre * pre) * 0.3989422804014327)
        grad = (slope * mm(cotangent[...], whole_back[:, at])).astype(BF16)
        pre_out[:, at] = grad
        sum_out[:, at] = jnp.sum(grad.astype(F32), axis=0, keepdims=True)
        return carry

    lax.fori_loop(0, act_out.shape[1] // CHUNK, one_chunk, 0)
    back_out[...] = mm(pre_out[...], whole_in[...], NT).astype(BF16)
    part_out[...] = mm(act_out[...], whole_back[...], NT).astype(BF16)


def finish_output(scalars, resid, mine, other, outs_bias, out):
    rows = resid.shape[0]
    place = lax.broadcasted_iota(jnp.int32, (rows, 1), 0)
    valid = (place >= scalars[1]) & (place < scalars[2])
    summed = mine[...].astype(F32) + other[...].astype(F32)
    total = resid[...] + (summed + outs_bias[2:3, :])
    out[...] = jnp.where(valid, total, 0.0).astype(BF16)


def column_sum(values):
    return jnp.sum(values, axis=0, keepdims=True)


def cross_backward(
    scalars, resid, cotangent, mine, other, gains, q_all, k_all, v_all, o_all, den_all,
    w0, w1, w2, w3,
    grad_out, low_out, att_out, dq_out, dk_out, dv_out, part_out, sums_out, heads_out,
    drop, whole, sems,
):
    copies = fetch(scalars, (w0, w1, w2, w3), whole, sems)
    rows = resid.shape[0]
    pairs = q_all.shape[0]
    cols = pairs * LANES
    unit, inverse = normalise(resid[...])
    grad_norm = mine[...].astype(F32) + other[...].astype(F32)
    top = cotangent[...].astype(F32)
    grad = top + norm_back(grad_norm, unit, inverse, gains[2:3, :])
    sums_out[0:1, :] = column_sum(grad_norm * unit)
    sums_out[1:2, :] = column_sum(grad_norm)
    sums_out[2:3, :] = column_sum(top)
    sums_out[3:4, :] = column_sum(grad)
    grad_out[...] = grad
    low = grad.astype(BF16)
    low_out[...] = low
    for p in range(pairs):
        att_out[:, p * LANES : (p + 1) * LANES] = o_all[p].astype(BF16)
    for copy in copies:
        copy.wait()
    attended = mm(low, whole[:, 3 * cols :]).astype(BF16)
    for p in range(pairs):
        drop[p] = attended[:, p * LANES : (p + 1) * LANES]
    count = k_all.shape[1]
    frame = lax.broadcasted_iota(jnp.int32, (count, 1), 0)
    allowed = (frame >= scalars[3]) & (frame < scalars[4])
    attend_back(pairs, rows, allowed, drop, q_all, k_all, v_all, o_all, den_all, dq_out, dk_out, dv_out)
    dq = jnp.concatenate([dq_out[p] for p in range(pairs)], axis=1)
    part_out[...] = mm(dq, whole[:, :cols], NT).astype(BF16)
    for p in range(pairs):
        heads_out[0:1, p * LANES : (p + 1) * LANES] = column_sum(dq_out[p].astype(F32))
        heads_out[1:2, p * LANES : (p + 1) * LANES] = column_sum(dv_out[p].astype(F32))


def attend_back(pairs, rows, allowed, drop, q_all, k_all, v_all, o_all, den_all, dq_out, dk_out, dv_out):
    count = k_all.shape[1]
    half = first_half((count, LANES))
    zero = jnp.zeros((), BF16)
    upper = lax.broadcasted_iota(jnp.int32, (LANES, rows), 0) < HD

    def one_pair(p, carry):
        q_pair, k_pair, v_pair = q_all[p], k_all[p], v_all[p]
        grad = drop[p].astype(F32)
        den = den_all[p]
        grad_sums = (grad / den).astype(BF16)
        drift_all = (grad * o_all[p] / den).T
        found = []
        for t in range(2):
            keep = half if t == 0 else jnp.logical_not(half)
            drift = jnp.sum(drift_all[t * HD : (t + 1) * HD, :], axis=0, keepdims=True)
            raw = mm(jnp.where(keep, k_pair, zero), q_pair, NT)
            weights = jnp.where(allowed, jnp.exp(raw), 0.0)
            prob = mm(jnp.where(keep, v_pair, zero), grad_sums, NT)
            score = (weights * (prob - drift)).astype(BF16)
            found.append(
                (
                    mm(k_pair, score, TN),
                    mm(score, q_pair),
                    mm(weights.astype(BF16), grad_sums),
                )
            )
        dq_out[p] = (jnp.where(upper, found[0][0], found[1][0]).T * HD ** -0.5).astype(BF16)
        dk_out[p] = jnp.where(half, found[0][1], found[1][1]).astype(dk_out.dtype)
        dv_out[p] = jnp.where(half, found[0][2], found[1][2]).astype(dv_out.dtype)
        return carry

    lax.fori_loop(0, pairs, one_pair, 0)


def self_backward(
    scalars, resid, top, mine, other, gains, q_all, k_all, v_all, o_all, den_all,
    w0, w1, w2, w3,
    grad_out, low_out, att_out, dq_out, dk_out, dv_out, part_out, sums_out, heads_out,
    drop, whole, sems,
):
    copies = fetch(scalars, (w0, w1, w2, w3), whole, sems)
    rows = resid.shape[0]
    pairs = q_all.shape[0]
    cols = pairs * LANES
    unit, inverse = normalise(resid[...])
    grad_norm = mine[...].astype(F32) + other[...].astype(F32)
    grad = top[...] + norm_back(grad_norm, unit, inverse, gains[1:2, :])
    sums_out[0:1, :] = column_sum(grad_norm * unit)
    sums_out[1:2, :] = column_sum(grad_norm)
    sums_out[2:3, :] = column_sum(grad)
    grad_out[...] = grad
    low = grad.astype(BF16)
    low_out[...] = low
    for p in range(pairs):
        att_out[:, p * LANES : (p + 1) * LANES] = o_all[p].astype(BF16)
    for copy in copies:
        copy.wait()
    attended = mm(low, whole[:, 3 * cols :]).astype(BF16)
    for p in range(pairs):
        drop[p] = attended[:, p * LANES : (p + 1) * LANES]
    k_place = lax.broadcasted_iota(jnp.int32, (rows, rows), 0)
    q_place = lax.broadcasted_iota(jnp.int32, (rows, rows), 1)
    allowed = (k_place <= q_place) & (k_place >= scalars[1])
    attend_back(pairs, rows, allowed, drop, q_all, k_all, v_all, o_all, den_all, dq_out, dk_out, dv_out)
    total = jnp.zeros((rows, part_out.shape[1]), F32)
    for index, piece in enumerate((dq_out, dk_out, dv_out)):
        joined = jnp.concatenate([piece[p] for p in range(pairs)], axis=1)
        total = total + mm(joined, whole[:, index * cols : (index + 1) * cols], NT)
    part_out[...] = total.astype(BF16)
    for p in range(pairs):
        heads_out[0:1, p * LANES : (p + 1) * LANES] = column_sum(dq_out[p].astype(F32))
        heads_out[1:2, p * LANES : (p + 1) * LANES] = column_sum(dv_out[p].astype(F32))


def input_backward(hidden, top, mine, other, gains, out, sums_out):
    unit, inverse = normalise(hidden[...].astype(F32))
    grad_norm = mine[...].astype(F32) + other[...].astype(F32)
    grad = top[...] + norm_back(grad_norm, unit, inverse, gains[0:1, :])
    sums_out[0:1, :] = column_sum(grad_norm * unit)
    sums_out[1:2, :] = column_sum(grad_norm)
    out[...] = grad.astype(BF16)


def frame_backward(scalars, dk_all, dv_all, w0, w1, w2, w3, out, whole, sems):
    copies = fetch(scalars, (w0, w1, w2, w3), whole, sems)
    pairs = dk_all.shape[0]
    cols = pairs * LANES
    dk = jnp.concatenate([dk_all[p] for p in range(pairs)], axis=1)
    dv = jnp.concatenate([dv_all[p] for p in range(pairs)], axis=1)
    for copy in copies:
        copy.wait()
    total = mm(dk, whole[:, cols : 2 * cols], NT) + mm(dv, whole[:, 2 * cols : 3 * cols], NT)
    out[...] = total.astype(BF16)


def weight_grads(layout, scalars, *refs):
    count = 1 + max(max(pair) for pair in layout)
    operands = refs[:count]
    outs = refs[count : count + 4]
    whole, sems = refs[count + 4 :]
    at = 0
    for left, right in layout:
        ref = operands[right]
        if len(ref.shape) == 3:
            grads = jnp.concatenate([ref[p] for p in range(ref.shape[0])], axis=1)
        else:
            grads = ref[...]
        size = grads.shape[1]
        whole[:, at : at + size] = mm(operands[left][...], grads, TN).astype(BF16)
        at += size
    rows = outs[0].shape[0]
    copies = []
    for j, out in enumerate(outs):
        start = pl.multiple_of(rows * jnp.bitwise_xor(scalars[0], j), rows)
        copies.append(pltpu.make_async_copy(whole.at[pl.ds(start, rows), :], out, sems.at[j]))
    for copy in copies:
        copy.start()
    for copy in copies:
        copy.wait()


SMEM = pl.BlockSpec(memory_space=pltpu.SMEM)
VMEM = pl.BlockSpec(memory_space=pltpu.VMEM)
ANY = pl.BlockSpec(memory_space=pl.ANY)


def shape(dims, dtype):
    return jax.ShapeDtypeStruct(tuple(dims), dtype)


def kernel_call(kernel, name, operands, spaces, outs, out_spaces=None, scratch=()):
    return pl.pallas_call(
        kernel,
        out_shape=tuple(outs),
        in_specs=list(spaces),
        out_specs=tuple(out_spaces or [VMEM] * len(outs)),
        scratch_shapes=list(scratch),
        compiler_params=pltpu.CompilerParams(vmem_limit_bytes=56 * 1024 * 1024),
        name=name,
    )(*operands)


def body(
    hidden, encoded, token_lengths, frame_counts, ln_gain, ln_bias, head_bias, out_bias, fc_bias,
    self_proj, cross_proj, out_proj, fc_in, fc_out, cotangent,
):
    wide = lax.axis_size("wide")
    depth = lax.axis_size("narrow")
    tok_rows, width = hidden.shape[1:]
    frame_rows = encoded.shape[1]
    swing = (MAXLEN - tok_rows) // 2
    ratio = frame_rows // tok_rows
    near = ratio * swing
    far = frame_rows - near
    assert far >= near + JITTER and far + near == frame_rows and depth == 4 and hidden.shape[0] == 2
    rows = tok_rows + 2 * swing
    frames = near + frame_rows + far
    shard = width // wide
    heads_cols = head_bias.shape[1]
    cols = 2 * heads_cols
    pairs = cols // LANES
    units = 2 * fc_bias.shape[0]

    w = lax.axis_index("wide")
    n = lax.axis_index("narrow")
    chip = w // 2
    core = w % 2
    batch = n // 2
    odd = n % 2
    item = 2 * chip + odd
    relay = wide == 8

    def move(value, rule):
        pairs_list = []
        for ws in range(wide):
            for ns in range(depth):
                target = rule(ws, ns)
                if target is not None and 0 <= target[0] < wide:
                    pairs_list.append((ws * depth + ns, target[0] * depth + target[1]))
        return lax.ppermute(value, AXES, pairs_list)

    def swap(value):
        return move(value, lambda a, z: (a ^ 1, z))

    def pick(value, index):
        return lax.dynamic_index_in_dim(value, index, 0, keepdims=False)

    def ordered(own, partner):
        return jnp.where(
            core == 0,
            jnp.concatenate([own, partner], axis=0),
            jnp.concatenate([partner, own], axis=0),
        )

    def halo(piece):
        def rule(target, a, z):
            if z % 2 == 0 and a % 2 == 1:
                return (a + 1 + target, z)
            if z % 2 == 1 and a % 2 == 0:
                return (a - 2 + target, z)
            return None

        found = [move(piece, partial(rule, target)) for target in range(2)]
        return jnp.where(core == 0, found[0], found[1])

    def window(own, margin, size, step):
        edge = jnp.where(odd == 0, own[-margin:], own[:margin])
        side = halo(edge)
        joined = jnp.concatenate([side, ordered(own, swap(own)), side], axis=0)
        return lax.dynamic_slice_in_dim(joined, odd * step, size, 0)

    hidden_rows = window(pick(hidden, batch), swing, rows, tok_rows)
    lengths = pick(token_lengths, batch)
    counts = pick(frame_counts, batch)
    items = jnp.arange(lengths.shape[0], dtype=jnp.int32)
    tok_lo = jnp.sum(jnp.where(items < item, lengths, 0)) - (tok_rows * item - swing)
    tok_hi = tok_lo + jnp.sum(jnp.where(items == item, lengths, 0))
    frame_start = frame_rows * item - jnp.where(odd == 0, near, far)
    frame_lo = jnp.sum(jnp.where(items < item, counts, 0)) - frame_start
    frame_hi = frame_lo + jnp.sum(jnp.where(items == item, counts, 0))
    here = chip if relay else jnp.zeros((), jnp.int32)
    scalars = jnp.stack([here, tok_lo, tok_hi, frame_lo, frame_hi]).astype(jnp.int32)

    def group(stack, out):
        parts = [stack[0], stack[1], stack[2], out.T]
        return jnp.concatenate(parts, axis=1)

    pieces = [
        group(self_proj, out_proj[0]),
        group(cross_proj, out_proj[1]),
        fc_in,
        fc_out.T,
    ]
    sizes = [piece.shape[1] for piece in pieces]
    own_piece = jnp.concatenate(pieces, axis=1)
    partner_piece = move(own_piece, lambda a, z: (a ^ 1, z) if a % 2 != z // 2 else None)
    chip_piece = ordered(own_piece, partner_piece)

    def spread(value):
        def rule(step, a, z):
            return (a, z ^ step) if a % 2 == z // 2 else None

        got = [None] + [move(value, partial(rule, step)) for step in (1, 2, 3)]
        same = jnp.where(core == batch, value, got[2])
        across = jnp.where(core == batch, got[1], got[3])
        return jnp.where(odd == 0, same, across), jnp.where(odd == 0, across, same)

    def gathered(index):
        start = sum(sizes[:index])
        first, second = spread(chip_piece[:, start : start + sizes[index]])
        splits = 4 if index < 2 else 1
        joined = jnp.stack(
            [x.reshape(2 * shard, splits, -1) for x in (first, second)], axis=2
        ).reshape(2 * shard, 2 * sizes[index])
        if relay:
            half = shard
            side_x = move(joined, lambda a, z: (a ^ 2, z))
            side_y = move(joined, lambda a, z: (a ^ 4, z))
            far_one = move(side_y[:half], lambda a, z: (a ^ 2, z))
            far_two = move(side_x[half:], lambda a, z: (a ^ 4, z))
            return [joined, side_x, side_y, jnp.concatenate([far_one, far_two], axis=0)]
        groups = [list(range(k, wide, 2)) for k in range(2)]
        full = lax.all_gather(joined, "wide", axis=0, tiled=True, axis_index_groups=groups)
        return [full[width // 4 * j : width // 4 * (j + 1)] for j in range(4)]

    bias_vector = jnp.concatenate([head_bias.reshape(-1), fc_bias])
    all_bias = lax.all_gather(bias_vector, "narrow", axis=0, tiled=False)
    core_bias = lax.dynamic_slice_in_dim(all_bias, 2 * core, 2, 0)
    biases = jnp.swapaxes(core_bias[:, : head_bias.size].reshape(2, 4, heads_cols), 0, 1).reshape(4, cols)
    fc_biases = core_bias[:, head_bias.size :].reshape(1, units)

    self_w = gathered(0)
    cross_w = gathered(1)
    in_w = gathered(2)
    back_w = gathered(3)

    frame_window = window(pick(encoded, batch), near, frames, 2 * near)
    place = jnp.arange(rows, dtype=jnp.int32)[:, None]
    valid = (place >= tok_lo) & (place < tok_hi)
    top_rows = jnp.where(
        valid, window(pick(cotangent, batch), swing, rows, tok_rows), jnp.zeros((), BF16)
    )

    act_shape = shape((rows, width), BF16)
    wide_f32 = shape((rows, width), F32)
    head_b = shape((pairs, rows, LANES), BF16)
    head_f = shape((pairs, rows, LANES), F32)
    frame_b = shape((pairs, frames, LANES), BF16)
    weight_scratch = [pltpu.VMEM((width, 4 * cols), BF16), pltpu.SemaphoreType.DMA((4,))]

    low_one, self_q, self_k, self_v, self_o, self_den, part = kernel_call(
        self_forward,
        "self_forward",
        (scalars, hidden_rows, ln_gain, ln_bias, biases, *self_w),
        [SMEM] + [VMEM] * 4 + [ANY] * 4,
        [act_shape, head_b, head_b, head_b, head_f, head_f, act_shape],
        scratch=weight_scratch,
    )
    other = swap(part)
    cross_k, cross_v = kernel_call(
        frame_project,
        "frame_project",
        (scalars, frame_window, biases, *cross_w),
        [SMEM] + [VMEM] * 2 + [ANY] * 4,
        [frame_b, frame_b],
        scratch=weight_scratch,
    )
    resid_one, low_two, cross_q, cross_o, cross_den, part_two = kernel_call(
        cross_forward,
        "cross_forward",
        (scalars, hidden_rows, part, other, ln_gain, ln_bias, out_bias, biases, cross_k, cross_v, *cross_w),
        [SMEM] + [VMEM] * 9 + [ANY] * 4,
        [wide_f32, act_shape, head_b, head_f, head_f, act_shape],
        scratch=weight_scratch,
    )
    other_two = swap(part_two)
    resid_two, low_three, low_act, grad_pre, part_three, back_three, unit_sums = kernel_call(
        unit_forward,
        "unit_forward",
        (scalars, resid_one, part_two, other_two, ln_gain, ln_bias, out_bias, fc_biases, top_rows, *in_w, *back_w),
        [SMEM] + [VMEM] * 8 + [ANY] * 8,
        [
            wide_f32, act_shape, shape((rows, units), BF16), shape((rows, units), BF16),
            act_shape, act_shape, shape((1, units), F32),
        ],
        scratch=[weight_scratch[0]] * 2 + [weight_scratch[1]] * 2,
    )
    other_back = swap(back_three)
    other_three = swap(part_three)
    grad_block = [shape((width // 4, 4 * cols), BF16)] * 4

    def grads_of(layout, name, *operands):
        return kernel_call(
            partial(weight_grads, layout),
            name,
            (scalars, *operands),
            [SMEM] + [VMEM] * len(operands),
            grad_block,
            [ANY] * 4,
            scratch=weight_scratch,
        )

    back_grads = grads_of(((0, 1),), "back_grads", top_rows, low_act)
    in_grads = grads_of(((0, 1),), "in_grads", low_three, grad_pre)
    final = kernel_call(
        finish_output,
        "finish_output",
        (scalars, resid_two, part_three, other_three, out_bias),
        [SMEM] + [VMEM] * 4,
        [act_shape],
    )[0]
    sums_shape = shape((8, width), F32)
    heads_shape = shape((8, cols), F32)
    drop_scratch = [pltpu.VMEM((pairs, rows, LANES), BF16)]
    grad_two, low_grad_two, low_cross, cq_grad, ck_grad, cv_grad, back_two, sums_two, heads_two = kernel_call(
        cross_backward,
        "cross_backward",
        (scalars, resid_two, top_rows, back_three, other_back, ln_gain, cross_q, cross_k, cross_v, cross_o, cross_den, *cross_w),
        [SMEM] + [VMEM] * 10 + [ANY] * 4,
        [wide_f32, act_shape, shape((rows, cols), BF16), head_b, frame_b, frame_b, act_shape, sums_shape, heads_shape],
        scratch=drop_scratch + weight_scratch,
    )
    other_back_two = swap(back_two)
    frame_part = kernel_call(
        frame_backward,
        "frame_backward",
        (scalars, ck_grad, cv_grad, *cross_w),
        [SMEM] + [VMEM] * 2 + [ANY] * 4,
        [shape((frames, width), BF16)],
        scratch=weight_scratch,
    )[0]
    cross_grads = grads_of(
        ((0, 1), (2, 3), (2, 4), (5, 6)),
        "cross_grads",
        low_two, cq_grad, frame_window, ck_grad, cv_grad, low_grad_two, low_cross,
    )
    grad_one, low_grad_one, low_self, sq_grad, sk_grad, sv_grad, back_one, sums_one, heads_one = kernel_call(
        self_backward,
        "self_backward",
        (scalars, resid_one, grad_two, back_two, other_back_two, ln_gain, self_q, self_k, self_v, self_o, self_den, *self_w),
        [SMEM] + [VMEM] * 10 + [ANY] * 4,
        [wide_f32, act_shape, shape((rows, cols), BF16), head_b, head_b, head_b, act_shape, sums_shape, heads_shape],
        scratch=drop_scratch + weight_scratch,
    )
    other_back_one = swap(back_one)
    self_grads = grads_of(
        ((0, 1), (0, 2), (0, 3), (4, 5)),
        "self_grads",
        low_one, sq_grad, sk_grad, sv_grad, low_grad_one, low_self,
    )
    input_rows, sums_zero = kernel_call(
        input_backward,
        "input_backward",
        (hidden_rows, grad_one, back_one, other_back_one, ln_gain),
        [VMEM] * 5,
        [act_shape, sums_shape],
    )

    main = core == odd

    def to_slices(middle, before, after):
        def head_rule(a, z):
            if a % 2 == z % 2:
                return None
            return (a, z ^ 1) if z % 2 == 1 else (a - 2, z ^ 1)

        def tail_rule(a, z):
            if a % 2 == z % 2:
                return None
            return (a, z ^ 1) if z % 2 == 0 else (a + 2, z ^ 1)

        from_above = move(before, head_rule)
        from_below = move(after, tail_rule)
        gap = jnp.zeros((middle.shape[0] - before.shape[0], middle.shape[1]), middle.dtype)
        lower = jnp.concatenate([gap, from_above], axis=0)
        gap = jnp.zeros((middle.shape[0] - after.shape[0], middle.shape[1]), middle.dtype)
        return middle + lower + jnp.concatenate([from_below, gap], axis=0)

    def to_copies(block, dtype):
        def rule(step, a, z):
            return (a, z ^ step) if a % 2 == z % 2 else None

        got = [None] + [move(block, partial(rule, step)) for step in (1, 2, 3)]
        near_copy = jnp.where(main, block, got[1]).astype(dtype)
        far_copy = jnp.where(main, got[2], got[3]).astype(dtype)
        return jnp.stack([jnp.where(batch == 0, near_copy, far_copy), jnp.where(batch == 0, far_copy, near_copy)])

    def token_output(block, dtype):
        mid = block[swing : swing + tok_rows]
        return to_copies(to_slices(mid, block[:swing], block[swing + tok_rows :]), dtype)

    output = token_output(final, BF16)
    input_grad = token_output(input_rows, F32)

    lead = jnp.where(odd == 0, near, far)
    mid_part = lax.dynamic_slice_in_dim(frame_part, lead, frame_rows, 0)
    outer_part = jnp.where(
        odd == 0,
        jnp.concatenate([frame_part[:near], frame_part[near + frame_rows :]], axis=0),
        jnp.concatenate([frame_part[far + frame_rows :], frame_part[:far]], axis=0),
    )
    kept = jnp.where(main, mid_part, outer_part)
    given = jnp.where(main, outer_part, mid_part)
    half_sum = (kept.astype(F32) + swap(given).astype(F32)).astype(BF16)

    def frame_cross_rule(a, z):
        if a % 2 == z % 2:
            return None
        return (a - 2, z ^ 1) if z % 2 == 0 else (a + 2, z ^ 1)

    def frame_pair_rule(a, z):
        return None if a % 2 == z % 2 else (a, z ^ 1)

    from_near = move(half_sum[:near], frame_cross_rule)
    from_far = move(half_sum[near:], frame_pair_rule)
    first_rows = jnp.concatenate([from_far, jnp.zeros((frame_rows - far, width), BF16)], axis=0)
    last_rows = jnp.concatenate([jnp.zeros((frame_rows - near, width), BF16), from_near], axis=0)
    odd_first = jnp.concatenate([jnp.zeros((frame_rows - far, width), BF16), from_far], axis=0)
    odd_last = jnp.concatenate([from_near, jnp.zeros((frame_rows - near, width), BF16)], axis=0)
    extra = jnp.where(odd == 1, first_rows + last_rows, odd_first + odd_last)
    encoded_grad = to_copies(half_sum + extra, F32)

    def scattered(blocks, index):
        half = shard
        if relay:
            got_x = move(blocks[3][half:], lambda a, z: (a ^ 2, z))
            got_y = move(blocks[3][:half], lambda a, z: (a ^ 4, z))
            to_x = jnp.concatenate([(blocks[1][:half].astype(F32) + got_y.astype(F32)).astype(BF16), blocks[1][half:]], axis=0)
            to_y = jnp.concatenate([blocks[2][:half], (blocks[2][half:].astype(F32) + got_x.astype(F32)).astype(BF16)], axis=0)
            from_x = move(to_x, lambda a, z: (a ^ 2, z))
            from_y = move(to_y, lambda a, z: (a ^ 4, z))
            total = blocks[0].astype(F32) + from_x.astype(F32) + from_y.astype(F32)
        else:
            groups = [list(range(k, wide, 2)) for k in range(2)]
            total = lax.psum_scatter(
                jnp.concatenate(blocks, axis=0), "wide", scatter_dimension=0, tiled=True, axis_index_groups=groups
            ).astype(F32)
        splits = 4 if index < 2 else 1
        parts = total.astype(BF16).reshape(2 * shard, splits, 2, -1)
        parts = [parts[:, :, k].reshape(2 * shard, -1) for k in range(2)]
        same = jnp.where(odd == 0, parts[0], parts[1])
        across = jnp.where(odd == 0, parts[1], parts[0])

        def rule(step, a, z):
            return (a, z ^ step) if a % 2 == (z ^ step) // 2 else None

        got = [move(across if step != 2 else same, partial(rule, step)) for step in (1, 2, 3)]
        summed = same.astype(F32) + got[0].astype(F32) + got[1].astype(F32) + got[2].astype(F32)
        keep = jnp.where(core == 0, summed[:shard], summed[shard:])
        give = jnp.where(core == 0, summed[shard:], summed[:shard])
        passed = move(give, lambda a, z: (a ^ 1, z) if a % 2 == z // 2 else None)
        return jnp.where(core == batch, keep, passed)

    grad_back = scattered(back_grads, 3)
    grad_in = scattered(in_grads, 2)
    grad_cross = scattered(cross_grads, 1)
    grad_self = scattered(self_grads, 0)

    def unpacked(grad):
        stack = jnp.stack([grad[:, heads_cols * k : heads_cols * (k + 1)] for k in range(3)])
        return stack, grad[:, 3 * heads_cols :].T

    grad_self_proj, grad_out_one = unpacked(grad_self)
    grad_cross_proj, grad_out_two = unpacked(grad_cross)

    only = jnp.where(core == 0, 1.0, 0.0)
    head_rows = jnp.stack([heads_one[0], heads_one[1], heads_two[0], heads_two[1]])
    head_full = lax.dynamic_update_slice(
        jnp.zeros((4, depth * heads_cols), F32), head_rows, (0, cols * core)
    )
    unit_full = lax.dynamic_update_slice(jnp.zeros((1, 2 * units), F32), unit_sums, (0, units * core))
    vectors = jnp.concatenate(
        [
            jnp.stack([sums_zero[0], sums_one[0], sums_two[0], sums_zero[1], sums_one[1], sums_two[1], sums_one[2], sums_two[3], sums_two[2]]).reshape(-1) * only,
            head_full.reshape(-1),
            unit_full.reshape(-1),
        ]
    )
    vectors = lax.psum(vectors, AXES)
    grad_gain = vectors[: 3 * width].reshape(3, width)
    grad_shift = vectors[3 * width : 6 * width].reshape(3, width)
    grad_outs = vectors[6 * width : 9 * width].reshape(3, width)
    grad_heads = vectors[9 * width : 9 * width + 4 * depth * heads_cols].reshape(4, depth * heads_cols)
    grad_heads = lax.dynamic_slice_in_dim(grad_heads, heads_cols * n, heads_cols, 1)
    grad_units = vectors[9 * width + 4 * depth * heads_cols :]
    grad_units = lax.dynamic_slice_in_dim(grad_units, units // 2 * n, units // 2, 0)
    return (
        output,
        input_grad,
        encoded_grad,
        grad_gain,
        grad_shift,
        grad_heads,
        grad_outs,
        grad_units,
        grad_self_proj,
        grad_cross_proj,
        jnp.stack([grad_out_one, grad_out_two]),
        grad_in,
        grad_back.T,
    )


def solution(mesh):
    in_specs = (
        P(None, "wide", None),
        P(None, "wide", None),
        P(),
        P(),
        P(),
        P(),
        P(None, "narrow"),
        P(),
        P("narrow"),
        P(None, "wide", "narrow"),
        P(None, "wide", "narrow"),
        P(None, "narrow", "wide"),
        P("wide", "narrow"),
        P("narrow", "wide"),
        P(None, "wide", None),
    )
    out_specs = (
        P(None, "wide", None),
        P(None, "wide", None),
        P(None, "wide", None),
        P(),
        P(),
        P(None, "narrow"),
        P(),
        P("narrow"),
        P(None, "wide", "narrow"),
        P(None, "wide", "narrow"),
        P(None, "narrow", "wide"),
        P("wide", "narrow"),
        P("narrow", "wide"),
    )
    return jax.shard_map(body, mesh=mesh, in_specs=in_specs, out_specs=out_specs, check_vma=False)
```

time: 843 us -> 604 us (0.72)
  the two profiles are of different devices: /device:TPU:0 before, /device:TPU:12 now
where the time goes in v1:
time: 604 us; the launch traced here: 597 us
  starting transfers between devices  156 us (26%)
  waiting for transfers between devices  138 us (23%)
  Pallas kernels  109 us (18%)
  other arithmetic  73.3 us (12%)
  local copies, waits for them, and re-layouts  63.9 us (11%)
  blocking collectives  51.8 us (9%)
    ppermute x92, starting transfers between devices, move(): return lax.ppermute(value, AXES, pairs_list)  156 us
    ppermute x92, waiting for transfers between devices, move(): return lax.ppermute(value, AXES, pairs_list)  138 us
    pallas_call x13, Pallas kernels, kernel_call(): pl.pallas_call(kernel, out_shape=tuple(outs), in_specs=list(spaces), out_...  109 us
    psum x1, blocking collectives, body(): vectors = lax.psum(vectors, AXES)  39.1 us
    all_gather x1, blocking collectives, body(): all_bias = lax.all_gather(bias_vector, 'narrow', axis=0, tiled=False)  12.7 us
  transfers between devices with their start and end apart: 92, of which 21 were waited for; matrix products, arithmetic and copies ran while one was open for 20% of the time, Pallas kernels for 15%

profile of v1, /device:TPU:12, one launch (start us, length us, event | category | flops | bytes accessed | tf_op | source)
XLA Modules:
  0.0 597.5 jit_solution(9700426094084340599)
XLA Ops:
  10.7 12.7 %all-gather.1 = f32[4,1,1536]{2,1,0:T(1,128)S(1)} all-gather(f32[1,1,1536]{2,1,0:T(1,128)S(1)} %reshape.163), channel_id=2, replica_groups=mesh['wide'=8,'narrow'=4] {'narrow'}, dimensions={0}, use_global_device_ids=true | all-gather | bytes 30720 | tf_op jit(solution)/shard_map/all_gather | solution.py:534
  71.2 6.5 %collective-permute-done.26 = bf16[192,768]{1,0:T(8,128)(2,1)S(1)} collective-permute-done((bf16[192,768]{1,0:T(8,128)(2,1)S(1)}, bf16[192,768]{1,0:T(8,128)(2,1)S(1)}, u32[]{:S(2)}, u32[]{:S(2)}) %collective-permute-start.26) | collective-permute-done | bytes 294944 | tf_op jit(solution)/shard_map/ppermute | solution.py:447
  115.6 18.3 %collective-permute-done.7.w1 = bf16[192,1536]{1,0:T(8,128)(2,1)S(1)} collective-permute-done((bf16[192,1536]{1,0:T(8,128)(2,1)S(1)}, bf16[192,1536]{1,0:T(8,128)(2,1)S(1)}, u32[]{:S(2)}, u32[]{:S(2)}) %collective-permute-start.7) | collective-permute-done | bytes 589856 | tf_op jit(solution)/shard_map/ppermute | solution.py:447
  133.9 6.3 %collective-permute-start.36 = (bf16[192,1536]{1,0:T(8,128)(2,1)S(1)}, bf16[192,1536]{1,0:T(8,128)(2,1)S(1)}, u32[]{:S(2)}, u32[]{:S(2)}) collective-permute-start(bf16[192,1536]{1,0:T(8,128)(2,1)S(1)} %bitcast.127), channel_id=1, source_target_pairs={{0,8},{1,9},{2,10},{3,11},{4,12},{5,13},{6,14},{7,15},{8,0},{9,1},... | collective-permute-start | bytes 1769480 | tf_op jit(solution)/shard_map/ppermute | solution.py:447
  152.4 7.8 %self_forward.1 = (bf16[448,768]{1,0:T(8,128)(2,1)}, bf16[3,448,128]{2,1,0:T(8,128)(2,1)}, bf16[3,448,128]{2,1,0:T(8,128)(2,1)}, bf16[3,448,128]{2,1,0:T(8,128)(...) custom-call(s32[5]{0:T(128)} %stack.102.scalars, bf16[448,768]{1,0:T(8,128)(2,1)} %fusion.10.hidden, ...), custom_call_target="tpu_custom_call" | custom-call | tf_op jit(solution)/shard_map/self_forward/pallas_call | solution.py:399
  169.0 5.8 collective-permute-done.20
  177.8 7.0 %frame_project.1 = (bf16[3,1536,128]{2,1,0:T(8,128)(2,1)}, bf16[3,1536,128]{2,1,0:T(8,128)(2,1)}) custom-call(s32[5]{0:T(128)} %stack.102.scalars, bf16[1536,768]{1,0:T(8,128)(2,1)} %fusion.3.frames.refs_2_, f32[4,384]{1,0:T(4,128)} %reshape.150.biases, bf16[192,1536]{1,0:T(8,128)(2,1)} %copy-done.1, bf16[192,1536]{1,0:T(8,128)(2,1)} %copy-done.3, ...), custom_call_target="tpu_custom_call" | custom-call | tf_op jit(solution)/shard_map/frame_project/pallas_call | solution.py:399
  184.9 11.2 %cross_forward.1 = (f32[448,768]{1,0:T(8,128)}, bf16[448,768]{1,0:T(8,128)(2,1)}, bf16[3,448,128]{2,1,0:T(8,128)(2,1)}, f32[3,448,128]{2,1,0:T(8,128)}, f32[3,44...) custom-call(s32[5]{0:T(128)} %stack.102.scalars, bf16[448,768]{1,0:T(8,128)(2,1)} %fusion.10.hidden, ...), custom_call_target="tpu_custom_call" | custom-call | tf_op jit(solution)/shard_map/cross_forward/pallas_call | solution.py:399
  200.0 14.0 %unit_forward.1 = (f32[448,768]{1,0:T(8,128)}, bf16[448,768]{1,0:T(8,128)(2,1)}, bf16[448,1536]{1,0:T(8,128)(2,1)}, bf16[448,1536]{1,0:T(8,128)(2,1)}, bf16[448,...) custom-call(s32[5]{0:T(128)} %stack.102.scalars, f32[448,768]{1,0:T(8,128)} %get-tuple-element.74.resid, ...), custom_call_target="tpu_custom_call" | custom-call | tf_op jit(solution)/shard_map/unit_forward/pallas_call | solution.py:399
  243.4 21.7 %cross_backward.1 = (f32[448,768]{1,0:T(8,128)}, bf16[448,768]{1,0:T(8,128)(2,1)}, bf16[448,384]{1,0:T(8,128)(2,1)}, bf16[3,448,128]{2,1,0:T(8,128)(2,1)}, bf16[...) custom-call(s32[5]{0:T(128)} %stack.102.scalars, ...), custom_call_target="tpu_custom_call" | custom-call | tf_op jit(solution)/shard_map/cross_backward/pallas_call | solution.py:399
  265.2 7.9 %cross_grads.1 = (bf16[192,1536]{1,0:T(8,128)(2,1)}, bf16[192,1536]{1,0:T(8,128)(2,1)}, bf16[192,1536]{1,0:T(8,128)(2,1)}, bf16[192,1536]{1,0:T(8,128)(2,1)}) custom-call(s32[5]{0:T(128)} %stack.102.scalars, bf16[448,768]{1,0:T(8,128)(2,1)} %get-tuple-element.110.refs_0_, bf16[3,448,128]{2,1,0:T(8,128)(2,1)} %get-tuple-element.111.refs_1_, ...), custom_call_target="tpu_custom_call" | custom-call | tf_op jit(solution)/shard_map/cross_grads/pallas_call | solution.py:399
  277.8 7.3 %frame_backward.1 = bf16[1536,768]{1,0:T(8,128)(2,1)} custom-call(s32[5]{0:T(128)} %stack.102.scalars, bf16[3,1536,128]{2,1,0:T(8,128)(2,1)} %get-tuple-element.92.dk_all.refs_3_, bf16[3,1536,128]{2,1,0:T(8,128)(2,1)} %get-tuple-element.93.dv_all.refs_4_, bf16[192,1536]{1,0:T(8,128)(2,1)} %copy-done.1, bf16[192,1536]{1,0:T(8,128)(2,1)} %copy-done.3, ...), custom_call_target="tpu_custom_call" | custom-call | tf_op jit(solution)/shard_map/frame_backward/pallas_call | solution.py:399
  307.9 5.0 collective-permute-start.88
  331.0 5.8 collective-permute-done.89
  336.8 5.8 collective-permute-start.47
  348.8 5.7 collective-permute-done.43
  357.4 13.3 %collective-permute-done.45 = bf16[256,768]{1,0:T(8,128)(2,1)S(1)} collective-permute-done((bf16[256,768]{1,0:T(8,128)(2,1)S(1)}, bf16[256,768]{1,0:T(8,128)(2,1)S(1)}, u32[]{:S(2)}, u32[]{:S(2)}) %collective-permute-start.45) | collective-permute-done | bytes 393248 | tf_op jit(solution)/shard_map/ppermute | solution.py:447
  375.7 11.6 %self_backward.1 = (f32[448,768]{1,0:T(8,128)}, bf16[448,768]{1,0:T(8,128)(2,1)}, bf16[448,384]{1,0:T(8,128)(2,1)}, bf16[3,448,128]{2,1,0:T(8,128)(2,1)}, bf16[3...) custom-call(s32[5]{0:T(128)} %stack.102.scalars, ...), custom_call_target="tpu_custom_call" | custom-call | tf_op jit(solution)/shard_map/self_backward/pallas_call | solution.py:399
  387.4 5.0 self_grads.1
  432.9 6.3 %collective-permute-start.55 = (bf16[480,768]{1,0:T(8,128)(2,1)}, bf16[480,768]{1,0:T(8,128)(2,1)}, u32[]{:S(2)}, u32[]{:S(2)}) collective-permute-start(bf16[480,768]{1,0:T(8,128)(2,1)} %slice.499), channel_id=1, source_target_pairs={{1,0},{3,2},{4,5},{6,7},{9,8},{11,10},{12,13},{14,15},{17,16},{19,... | collective-permute-start | bytes 2211848 | tf_op jit(solution)/shard_map/ppermute | solution.py:447
  444.1 39.1 %psum.7 = f32[13056]{0:T(1024)S(1)} all-reduce(f32[13056]{0:T(1024)S(1)} %pad_maximum_fusion.20), channel_id=1, replica_groups=mesh['wide'=8,'narrow'=4] {'wide','narrow'}, use_global_device_ids=true, to_apply=%region_4.5 | all-reduce | flops 13056 | bytes 104448 | tf_op jit(solution)/shard_map/psum | solution.py:786
  512.4 7.2 %collective-permute-done.65 = bf16[192,768]{1,0:T(8,128)(2,1)S(1)} collective-permute-done((bf16[192,768]{1,0:T(8,128)(2,1)S(1)}, bf16[192,768]{1,0:T(8,128)(2,1)S(1)}, u32[]{:S(2)}, u32[]{:S(2)}) %collective-permute-start.65) | collective-permute-done | bytes 294944 | tf_op jit(solution)/shard_map/ppermute | solution.py:447
  529.9 7.4 %collective-permute-start.67 = (f32[96,768]{1,0:T(8,128)S(1)}, f32[96,768]{1,0:T(8,128)S(1)}, u32[]{:S(2)}, u32[]{:S(2)}) collective-permute-start(f32[96,768]{1,0:T(8,128)S(1)} %slice_select_fusion.3), channel_id=1, source_target_pairs={{0,4},{1,5},{6,2},{7,3},{8,12},{9,13},{14,10},{15,11},{16,20},{17,... | collective-permute-start | bytes 884744 | tf_op jit(solution)/shard_map/ppermute | solution.py:447
  546.8 46.1 %collective-permute-done.59 = bf16[768,768]{1,0:T(8,128)(2,1)} collective-permute-done((bf16[768,768]{1,0:T(8,128)(2,1)S(1)}, bf16[768,768]{1,0:T(8,128)(2,1)}, u32[]{:S(2)}, u32[]{:S(2)}) %collective-permute-start.59) | collective-permute-done | bytes 1179680 | tf_op jit(solution)/shard_map/ppermute | solution.py:447
  (510 shorter events, 306.9 us)
Async XLA Ops:
  5.3 51.0 %collective-permute-start.2 = (bf16[256,768]{1,0:T(8,128)(2,1)S(1)}, bf16[256,768]{1,0:T(8,128)(2,1)S(1)}, u32[]{:S(2)}, u32[]{:S(2)}) collective-permute-start(bf16[256,768]{1,0:T(8,128)(2,1)S(1)} %dynamic-slice_bitcast_fusion.2), channel_id=1, source_target_pairs={{0,4},{1,5},{2,6},{3,7},{4,0},{5,1},{6,2},{7,3},{8,12},{9,13},{10,... | collective-permute-start | bytes 1179656 | tf_op jit(solution)/shard_map/ppermute | solution.py:447
  7.2 34.6 %collective-permute-start = (bf16[96,768]{1,0:T(8,128)(2,1)}, bf16[96,768]{1,0:T(8,128)(2,1)}, u32[]{:S(2)}, u32[]{:S(2)}) collective-permute-start(bf16[96,768]{1,0:T(8,128)(2,1)} %fusion.14), channel_id=1, source_target_pairs={{4,8},{6,10},{9,1},{11,3},{12,16},{14,18},{17,9},{19,11},{20,24},{... | collective-permute-start | bytes 442376 | tf_op jit(solution)/shard_map/ppermute | solution.py:447
  80.9 30.6 %collective-permute-start.14 = (bf16[768,768]{1,0:T(8,128)(2,1)}, bf16[768,768]{1,0:T(8,128)(2,1)}, u32[]{:S(2)}, u32[]{:S(2)}) collective-permute-start(bf16[768,768]{1,0:T(8,128)(2,1)} %dynamic-slice_bitcast_fusion), channel_id=1, source_target_pairs={{0,4},{1,5},{2,6},{3,7},{4,0},{5,1},{6,2},{7,3},{8,12},{9,13},{10,... | collective-permute-start | bytes 3538952 | tf_op jit(solution)/shard_map/ppermute | solution.py:447
  104.5 35.7 %collective-permute-start.19 = (bf16[192,1536]{1,0:T(8,128)(2,1)S(1)}, bf16[192,1536]{1,0:T(8,128)(2,1)S(1)}, u32[]{:S(2)}, u32[]{:S(2)}) collective-permute-start(bf16[192,1536]{1,0:T(8,128)(2,1)S(1)} %reshape.152.w0), channel_id=1, source_target_pairs={{0,16},{1,17},{2,18},{3,19},{4,20},{5,21},{6,22},{7,23},{8,24},{9,... | collective-permute-start | bytes 1769480 | tf_op jit(solution)/shard_map/ppermute | solution.py:447
  105.9 36.5 %collective-permute-start.18 = (bf16[192,1536]{1,0:T(8,128)(2,1)S(1)}, bf16[192,1536]{1,0:T(8,128)(2,1)S(1)}, u32[]{:S(2)}, u32[]{:S(2)}) collective-permute-start(bf16[192,1536]{1,0:T(8,128)(2,1)S(1)} %reshape.152.w0), channel_id=1, source_target_pairs={{0,8},{1,9},{2,10},{3,11},{4,12},{5,13},{6,14},{7,15},{8,0},{9,1},... | collective-permute-start | bytes 1769480 | tf_op jit(solution)/shard_map/ppermute | solution.py:447
  110.3 50.1 %collective-permute-start.37 = (bf16[192,1536]{1,0:T(8,128)(2,1)S(1)}, bf16[192,1536]{1,0:T(8,128)(2,1)S(1)}, u32[]{:S(2)}, u32[]{:S(2)}) collective-permute-start(bf16[192,1536]{1,0:T(8,128)(2,1)S(1)} %bitcast.126), channel_id=1, source_target_pairs={{0,16},{1,17},{2,18},{3,19},{4,20},{5,21},{6,22},{7,23},{8,24},{9,... | collective-permute-start | bytes 1769480 | tf_op jit(solution)/shard_map/ppermute | solution.py:447
  111.4 32.5 %collective-permute-start.9 = (bf16[96,1536]{1,0:T(8,128)(2,1)S(1)}, bf16[96,1536]{1,0:T(8,128)(2,1)S(1)}, u32[]{:S(2)}, u32[]{:S(2)}) collective-permute-start(bf16[96,1536]{1,0:T(8,128)(2,1)S(1)} %slice.480), channel_id=1, source_target_pairs={{0,8},{1,9},{2,10},{3,11},{4,12},{5,13},{6,14},{7,15},{8,0},{9,1},... | collective-permute-start | bytes 884744 | tf_op jit(solution)/shard_map/ppermute | solution.py:447
  165.3 32.2 %collective-permute-start.38 = (bf16[96,1536]{1,0:T(8,128)(2,1)S(1)}, bf16[96,1536]{1,0:T(8,128)(2,1)S(1)}, u32[]{:S(2)}, u32[]{:S(2)}) collective-permute-start(bf16[96,1536]{1,0:T(8,128)(2,1)S(1)} %slice.490), channel_id=1, source_target_pairs={{0,8},{1,9},{2,10},{3,11},{4,12},{5,13},{6,14},{7,15},{8,0},{9,1},... | collective-permute-start | bytes 884744 | tf_op jit(solution)/shard_map/ppermute | solution.py:447
  168.4 29.1 %collective-permute-start.39 = (bf16[96,1536]{1,0:T(8,128)(2,1)S(1)}, bf16[96,1536]{1,0:T(8,128)(2,1)S(1)}, u32[]{:S(2)}, u32[]{:S(2)}) collective-permute-start(bf16[96,1536]{1,0:T(8,128)(2,1)S(1)} %slice.491), channel_id=1, source_target_pairs={{0,16},{1,17},{2,18},{3,19},{4,20},{5,21},{6,22},{7,23},{8,24},{9,... | collective-permute-start | bytes 884744 | tf_op jit(solution)/shard_map/ppermute | solution.py:447
  232.7 56.8 %collective-permute-start.40 = (bf16[448,768]{1,0:T(8,128)(2,1)S(1)}, bf16[448,768]{1,0:T(8,128)(2,1)S(1)}, u32[]{:S(2)}, u32[]{:S(2)}) collective-permute-start(bf16[448,768]{1,0:T(8,128)(2,1)S(1)} %copy-done.38), channel_id=1, source_target_pairs={{0,4},{1,5},{2,6},{3,7},{4,0},{5,1},{6,2},{7,3},{8,12},{9,13},{10,... | collective-permute-start | bytes 2064392 | tf_op jit(solution)/shard_map/ppermute | solution.py:447
  235.2 68.9 %collective-permute-start.85 = (bf16[192,1536]{1,0:T(8,128)(2,1)}, bf16[192,1536]{1,0:T(8,128)(2,1)}, u32[]{:S(2)}, u32[]{:S(2)}) collective-permute-start(bf16[192,1536]{1,0:T(8,128)(2,1)} %pad_maximum_fusion.15), channel_id=1, source_target_pairs={{0,8},{1,9},{2,10},{3,11},{4,12},{5,13},{6,14},{7,15},{8,0},{9,1},... | collective-permute-start | bytes 1769480 | tf_op jit(solution)/shard_map/ppermute | solution.py:447
  239.2 65.4 %collective-permute-start.87 = (bf16[192,1536]{1,0:T(8,128)(2,1)}, bf16[192,1536]{1,0:T(8,128)(2,1)}, u32[]{:S(2)}, u32[]{:S(2)}) collective-permute-start(bf16[192,1536]{1,0:T(8,128)(2,1)} %pad_maximum_fusion.16), channel_id=1, source_target_pairs={{0,16},{1,17},{2,18},{3,19},{4,20},{5,21},{6,22},{7,23},{8,24},{9,... | collective-permute-start | bytes 1769480 | tf_op jit(solution)/shard_map/ppermute | solution.py:447
  242.0 71.0 %collective-permute-start.77 = (bf16[192,1536]{1,0:T(8,128)(2,1)}, bf16[192,1536]{1,0:T(8,128)(2,1)}, u32[]{:S(2)}, u32[]{:S(2)}) collective-permute-start(bf16[192,1536]{1,0:T(8,128)(2,1)} %pad_maximum_fusion.13), channel_id=1, source_target_pairs={{0,8},{1,9},{2,10},{3,11},{4,12},{5,13},{6,14},{7,15},{8,0},{9,1},... | collective-permute-start | bytes 1769480 | tf_op jit(solution)/shard_map/ppermute | solution.py:447
  313.0 29.7 %collective-permute-start.90 = (bf16[192,768]{1,0:T(8,128)(2,1)}, bf16[192,768]{1,0:T(8,128)(2,1)}, u32[]{:S(2)}, u32[]{:S(2)}) collective-permute-start(bf16[192,768]{1,0:T(8,128)(2,1)} %get-tuple-element.195), channel_id=1, source_target_pairs={{2,1},{3,0},{4,7},{5,6},{10,9},{11,8},{12,15},{13,14},{18,17},{19,... | collective-permute-start | bytes 884744 | tf_op jit(solution)/shard_map/ppermute | solution.py:447
  336.8 37.0 %collective-permute-start.47 = (bf16[448,768]{1,0:T(8,128)(2,1)S(1)}, bf16[448,768]{1,0:T(8,128)(2,1)S(1)}, u32[]{:S(2)}, u32[]{:S(2)}) collective-permute-start(bf16[448,768]{1,0:T(8,128)(2,1)S(1)} %copy-done.41), channel_id=1, source_target_pairs={{0,4},{1,5},{2,6},{3,7},{4,0},{5,1},{6,2},{7,3},{8,12},{9,13},{10,... | collective-permute-start | bytes 2064392 | tf_op jit(solution)/shard_map/ppermute | solution.py:447
  342.6 77.9 %collective-permute-start.54 = (bf16[768,768]{1,0:T(8,128)(2,1)}, bf16[768,768]{1,0:T(8,128)(2,1)}, u32[]{:S(2)}, u32[]{:S(2)}) collective-permute-start(bf16[768,768]{1,0:T(8,128)(2,1)} %broadcast_select_fusion.2), channel_id=1, source_target_pairs={{0,4},{1,5},{2,6},{3,7},{4,0},{5,1},{6,2},{7,3},{8,12},{9,13},{10,... | collective-permute-start | bytes 3538952 | tf_op jit(solution)/shard_map/ppermute | solution.py:447
  354.5 48.5 %collective-permute-start.69 = (bf16[192,1536]{1,0:T(8,128)(2,1)}, bf16[192,1536]{1,0:T(8,128)(2,1)}, u32[]{:S(2)}, u32[]{:S(2)}) collective-permute-start(bf16[192,1536]{1,0:T(8,128)(2,1)} %pad_maximum_fusion.11), channel_id=1, source_target_pairs={{0,8},{1,9},{2,10},{3,11},{4,12},{5,13},{6,14},{7,15},{8,0},{9,1},... | collective-permute-start | bytes 1769480 | tf_op jit(solution)/shard_map/ppermute | solution.py:447
  356.1 47.0 %collective-permute-start.71 = (bf16[192,1536]{1,0:T(8,128)(2,1)}, bf16[192,1536]{1,0:T(8,128)(2,1)}, u32[]{:S(2)}, u32[]{:S(2)}) collective-permute-start(bf16[192,1536]{1,0:T(8,128)(2,1)} %pad_maximum_fusion.12), channel_id=1, source_target_pairs={{0,16},{1,17},{2,18},{3,19},{4,20},{5,21},{6,22},{7,23},{8,24},{9,... | collective-permute-start | bytes 1769480 | tf_op jit(solution)/shard_map/ppermute | solution.py:447
  403.0 36.1 %collective-permute-start.48 = (bf16[448,768]{1,0:T(8,128)(2,1)}, bf16[448,768]{1,0:T(8,128)(2,1)}, u32[]{:S(2)}, u32[]{:S(2)}) collective-permute-start(bf16[448,768]{1,0:T(8,128)(2,1)} %get-tuple-element.90.mine), channel_id=1, source_target_pairs={{0,4},{1,5},{2,6},{3,7},{4,0},{5,1},{6,2},{7,3},{8,12},{9,13},{10,... | collective-permute-start | bytes 2064392 | tf_op jit(solution)/shard_map/ppermute | solution.py:447
  420.5 75.2 %collective-permute-start.61 = (bf16[192,1536]{1,0:T(8,128)(2,1)}, bf16[192,1536]{1,0:T(8,128)(2,1)}, u32[]{:S(2)}, u32[]{:S(2)}) collective-permute-start(bf16[192,1536]{1,0:T(8,128)(2,1)} %pad_maximum_fusion.9), channel_id=1, source_target_pairs={{0,8},{1,9},{2,10},{3,11},{4,12},{5,13},{6,14},{7,15},{8,0},{9,1},... | collective-permute-start | bytes 1769480 | tf_op jit(solution)/shard_map/ppermute | solution.py:447
  424.7 71.0 %collective-permute-start.63 = (bf16[192,1536]{1,0:T(8,128)(2,1)}, bf16[192,1536]{1,0:T(8,128)(2,1)}, u32[]{:S(2)}, u32[]{:S(2)}) collective-permute-start(bf16[192,1536]{1,0:T(8,128)(2,1)} %pad_maximum_fusion.10), channel_id=1, source_target_pairs={{0,16},{1,17},{2,18},{3,19},{4,20},{5,21},{6,22},{7,23},{8,24},{9,... | collective-permute-start | bytes 1769480 | tf_op jit(solution)/shard_map/ppermute | solution.py:447
  430.2 62.6 %collective-permute-start.75 = (f32[96,768]{1,0:T(8,128)S(1)}, f32[96,768]{1,0:T(8,128)S(1)}, u32[]{:S(2)}, u32[]{:S(2)}) collective-permute-start(f32[96,768]{1,0:T(8,128)S(1)} %slice_select_fusion.2), channel_id=1, source_target_pairs={{0,4},{1,5},{6,2},{7,3},{8,12},{9,13},{14,10},{15,11},{16,20},{17,... | collective-permute-start | bytes 884744 | tf_op jit(solution)/shard_map/ppermute | solution.py:447
  432.9 90.9 %collective-permute-start.55 = (bf16[480,768]{1,0:T(8,128)(2,1)}, bf16[480,768]{1,0:T(8,128)(2,1)}, u32[]{:S(2)}, u32[]{:S(2)}) collective-permute-start(bf16[480,768]{1,0:T(8,128)(2,1)} %slice.499), channel_id=1, source_target_pairs={{1,0},{3,2},{4,5},{6,7},{9,8},{11,10},{12,13},{14,15},{17,16},{19,... | collective-permute-start | bytes 2211848 | tf_op jit(solution)/shard_map/ppermute | solution.py:447
  528.6 64.3 %collective-permute-start.59 = (bf16[768,768]{1,0:T(8,128)(2,1)S(1)}, bf16[768,768]{1,0:T(8,128)(2,1)}, u32[]{:S(2)}, u32[]{:S(2)}) collective-permute-start(bf16[768,768]{1,0:T(8,128)(2,1)S(1)} %select_add_fusion), channel_id=1, source_target_pairs={{0,3},{2,1},{5,6},{7,4},{8,11},{10,9},{13,14},{15,12},{16,19},{18,... | collective-permute-start | bytes 3538952 | tf_op jit(solution)/shard_map/ppermute | solution.py:447
  (150 other events, 1712.7 us)

commit v2 on v1

v2 whole, which is shorter than its diff:
```python
from functools import partial

import jax
import jax.numpy as jnp
from jax import lax
from jax.experimental import pallas as pl
from jax.experimental.pallas import tpu as pltpu
from jax.sharding import PartitionSpec as P

HD = 64
LANES = 128
MAXLEN = 448
JITTER = 156
EPSILON = 1e-05
F32 = jnp.float32
BF16 = jnp.bfloat16
NN = (((1,), (0,)), ((), ()))
NT = (((1,), (1,)), ((), ()))
TN = (((0,), (0,)), ((), ()))
AXES = ("wide", "narrow")


def mm(left, right, dims=NN):
    return lax.dot_general(left, right, dims, preferred_element_type=F32)


def normalise(values):
    centre = values - jnp.mean(values, axis=-1, keepdims=True)
    spread = jnp.mean(centre * centre, axis=-1, keepdims=True)
    inverse = lax.rsqrt(spread + EPSILON)
    return centre * inverse, inverse


def norm_back(grad_rows, unit_rows, inverse, gain):
    scaled = grad_rows * gain
    centred = scaled - jnp.mean(scaled, axis=-1, keepdims=True)
    return (centred - unit_rows * jnp.mean(scaled * unit_rows, axis=-1, keepdims=True)) * inverse


def erf(x):
    x = jnp.clip(x, -3.832506856900711, 3.832506856900711)
    x2 = x * x
    top = x2 * 0.00022905065861350646 + 0.0034082910107109506
    top = top * x2 + 0.050955695062380861
    top = top * x2 + 0.18520832239976145
    top = top * x2 + 1.128379143519084
    low = x2 * -1.1791602954361697e-7 + 0.000023547966471313185
    low = low * x2 + 0.0010179625278914885
    low = low * x2 + 0.014070470171167667
    low = low * x2 + 0.11098505178285362
    low = low * x2 + 0.49746925110067538
    low = low * x2 + 1.0
    return x * top / low


def fetch(scalars, blocks, whole, sems, mixed=False, column=0):
    rows = whole.shape[1] // 8
    copies = []
    for group in range(2):
        for chip in range(4):
            for half in range(2):
                first = (2 * group + half) * rows
                if len(blocks) == 4:
                    source, place = blocks[chip], jnp.bitwise_xor(scalars[0], chip)
                else:
                    source, place = blocks[0], chip
                    first += 4 * chip * rows
                    if mixed:
                        core = scalars[5]
                        first = 4 * jnp.bitwise_xor(core, half) + 2 * core + jnp.bitwise_xor(scalars[6], group)
                        first = pl.multiple_of(rows * (8 * chip + first), rows)
                at = 2 * rows * place + rows * jnp.bitwise_xor(scalars[5], half)
                copies.append(
                    pltpu.make_async_copy(
                        source.at[pl.ds(first, rows), pl.ds(column, whole.shape[2])],
                        whole.at[group, pl.ds(pl.multiple_of(at, rows), rows), :],
                        sems.at[len(copies)],
                    )
                )
    for copy in copies:
        copy.start()
    return copies


def first_half(shape):
    return lax.broadcasted_iota(jnp.int32, shape, len(shape) - 1) < HD


def lay_window(scalars, own, partner, halo, out, margin, other):
    size = own.shape[0]
    odd = scalars[6]
    main = scalars[7] == 1
    before = jnp.where(odd == 0, margin, other)
    out[pl.ds(pl.multiple_of(before, 32), size), :] = jnp.where(main, own[...], partner[...])
    near_side = jnp.where(main, partner[:other, :], own[:other, :])
    far_side = jnp.where(main, partner[size - other :, :], own[size - other :, :])

    @pl.when(odd == 0)
    def _():
        out[:margin, :] = halo[...]
        out[margin + size :, :] = near_side

    @pl.when(odd == 1)
    def _():
        out[other + size :, :] = halo[...]
        out[:other, :] = far_side


def valid_rows(scalars, rows):
    place = lax.broadcasted_iota(jnp.int32, (rows, 1), 0)
    return (place >= scalars[1]) & (place < scalars[2])


def both(first, second, at, size):
    return jnp.concatenate([first[:, at : at + size], second[:, at : at + size]], axis=1)


def bias_row(biases, at, size):
    parts = biases[:, at : at + size].astype(F32)
    rows = [parts[8 * g : 8 * g + 1] + parts[8 * g + 2 : 8 * g + 3] + parts[8 * g + 4 : 8 * g + 5] for g in range(2)]
    return jnp.concatenate(rows, axis=1)


def halves(refs, cols):
    joined = jnp.concatenate([refs[p] for p in range(refs.shape[0])], axis=1)
    return joined[:, :cols], joined[:, cols:]


def by_pairs(values, out):
    for p in range(out.shape[0]):
        out[p] = values[:, p * LANES : (p + 1) * LANES]


def attend(pairs, rows, allowed, guard, q_all, k_all, v_all, o_out, den_out):
    half = first_half((rows, LANES))
    zero = jnp.zeros((), BF16)

    def one_pair(p, carry):
        q_pair, k_pair, v_pair = q_all[p], k_all[p], v_all[p]
        outs, dens = [], []
        for keep in (half, jnp.logical_not(half)):
            raw = mm(jnp.where(keep, q_pair, zero), k_pair, NT)
            weights = jnp.where(allowed, jnp.exp(raw), 0.0)
            total = jnp.sum(weights, axis=1, keepdims=True)
            if guard:
                total = jnp.where(total > 0.0, total, 1.0)
            outs.append(mm(weights.astype(BF16), v_pair) / total)
            dens.append(jnp.broadcast_to(total, (rows, LANES)))
        o_out[p] = jnp.where(half, outs[0], outs[1])
        den_out[p] = jnp.where(half, dens[0], dens[1])
        return carry

    lax.fori_loop(0, pairs, one_pair, 0)


def out_product(o_all, whole, cols):
    first, second = halves(o_all, cols)
    first, second = first.astype(BF16), second.astype(BF16)
    return mm(first, whole[0, :, 3 * cols :], NT) + mm(second, whole[1, :, 3 * cols :], NT)


def self_forward(
    scalars, own, partner, halo, gains, shifts, biases, w0, w1, w2, w3,
    hidden_out, norm_out, q_out, k_out, v_out, o_out, den_out, part_out, whole, sems,
):
    copies = fetch(scalars, (w0, w1, w2, w3), whole, sems)
    rows = hidden_out.shape[0]
    pairs = q_out.shape[0]
    cols = pairs * LANES // 2
    margin = halo.shape[0]
    lay_window(scalars, own, partner, halo, hidden_out, margin, margin)
    unit, _ = normalise(hidden_out[...].astype(F32))
    norm = (unit * gains[0:1, :] + shifts[0:1, :]).astype(BF16)
    norm_out[...] = norm
    valid = valid_rows(scalars, rows)
    for copy in copies:
        copy.wait()
    first = mm(norm, whole[0, :, : 3 * cols])
    second = mm(norm, whole[1, :, : 3 * cols])
    query = (both(first, second, 0, cols) + bias_row(biases, 0 * cols, cols)).astype(BF16).astype(F32)
    by_pairs(jnp.where(valid, query * HD ** -0.5, 0.0).astype(BF16), q_out)
    by_pairs(both(first, second, cols, cols).astype(BF16), k_out)
    by_pairs((both(first, second, 2 * cols, cols) + bias_row(biases, 1 * cols, cols)).astype(BF16), v_out)
    q_place = lax.broadcasted_iota(jnp.int32, (rows, rows), 0)
    k_place = lax.broadcasted_iota(jnp.int32, (rows, rows), 1)
    allowed = (k_place <= q_place) & (k_place >= scalars[1])
    attend(pairs, rows, allowed, True, q_out, k_out, v_out, o_out, den_out)
    part_out[...] = out_product(o_out, whole, cols).astype(BF16)


def frame_project(
    mixed, scalars, own, partner, halo, biases, w0, frame_out, k_out, v_out, whole, sems
):
    copies = fetch(scalars, (w0,), whole, sems, mixed)
    pairs = k_out.shape[0]
    cols = pairs * LANES // 2
    margin = halo.shape[0]
    lay_window(scalars, own, partner, halo, frame_out, margin, own.shape[0] - margin)
    for copy in copies:
        copy.wait()
    first = mm(frame_out[...], whole[0, :, cols : 3 * cols])
    second = mm(frame_out[...], whole[1, :, cols : 3 * cols])
    by_pairs(both(first, second, 0, cols).astype(BF16), k_out)
    by_pairs((both(first, second, cols, cols) + bias_row(biases, 3 * cols, cols)).astype(BF16), v_out)


def cross_forward(
    mixed, scalars, hidden, mine, other, gains, shifts, outs_bias, biases, k_all, v_all, w0,
    resid_out, norm_out, q_out, o_out, den_out, part_out, whole, sems,
):
    copies = fetch(scalars, (w0,), whole, sems, mixed)
    rows = hidden.shape[0]
    pairs = q_out.shape[0]
    cols = pairs * LANES // 2
    summed = mine[...].astype(F32) + other[...].astype(F32)
    resid = hidden[...].astype(F32) + (summed + outs_bias[0:1, :])
    resid_out[...] = resid
    unit, _ = normalise(resid)
    norm = (unit * gains[1:2, :] + shifts[1:2, :]).astype(BF16)
    norm_out[...] = norm
    valid = valid_rows(scalars, rows)
    for copy in copies:
        copy.wait()
    query = jnp.concatenate([mm(norm, whole[0, :, :cols]), mm(norm, whole[1, :, :cols])], axis=1)
    query = (query + bias_row(biases, 2 * cols, cols)).astype(BF16).astype(F32)
    by_pairs(jnp.where(valid, query * HD ** -0.5, 0.0).astype(BF16), q_out)
    frame = lax.broadcasted_iota(jnp.int32, (1, k_all.shape[1]), 1)
    allowed = (frame >= scalars[3]) & (frame < scalars[4])
    attend(pairs, rows, allowed, False, q_out, k_all, v_all, o_out, den_out)
    part_out[...] = out_product(o_out, whole, cols).astype(BF16)


CHUNK = 256


def unit_forward(
    mixed, scalars, resid, mine, other, gains, shifts, outs_bias, fc_bias, own, partner, halo,
    w0,
    resid_out, norm_out, top_out, act_out, pre_out, part_out, back_out, sum_out, whole, sems,
):
    copies = fetch(scalars, (w0,), whole, sems, mixed, whole.shape[1])
    margin = halo.shape[0]
    lay_window(scalars, own, partner, halo, top_out, margin, margin)
    valid = valid_rows(scalars, resid.shape[0])
    top_out[...] = jnp.where(valid, top_out[...], jnp.zeros((), BF16))
    summed = mine[...].astype(F32) + other[...].astype(F32)
    resid_two = resid[...] + (summed + outs_bias[1:2, :])
    resid_out[...] = resid_two
    unit, _ = normalise(resid_two)
    norm_out[...] = (unit * gains[2:3, :] + shifts[2:3, :]).astype(BF16)
    for copy in copies:
        copy.wait()
    units = act_out.shape[1] // 2
    steps = units // CHUNK

    def one_chunk(j, carry):
        group = j // steps
        at_in = pl.ds(pl.multiple_of((j - group * steps) * CHUNK, CHUNK), CHUNK)
        at_back = pl.ds(pl.multiple_of(units + (j - group * steps) * CHUNK, CHUNK), CHUNK)
        at = pl.ds(pl.multiple_of(j * CHUNK, CHUNK), CHUNK)
        parts = fc_bias[:, at_in].astype(F32)
        parts = jnp.where(group == 0, parts[:8], parts[8:])
        pre = mm(norm_out[...], whole[group, :, at_in]) + (parts[1:2] + parts[3:4] + parts[5:6])
        cdf = 0.5 * (1.0 + erf(pre * 0.7071067811865476))
        act_out[:, at] = (pre * cdf).astype(BF16)
        slope = cdf + pre * (jnp.exp(-0.5 * pre * pre) * 0.3989422804014327)
        grad = (slope * mm(top_out[...], whole[group, :, at_back])).astype(BF16)
        pre_out[:, at] = grad
        sum_out[:, at] = jnp.sum(grad.astype(F32), axis=0, keepdims=True)
        return carry

    lax.fori_loop(0, 2 * steps, one_chunk, 0)
    back_out[...] = (
        mm(pre_out[:, :units], whole[0, :, :units], NT) + mm(pre_out[:, units:], whole[1, :, :units], NT)
    ).astype(BF16)
    part_out[...] = (
        mm(act_out[:, :units], whole[0, :, units:], NT) + mm(act_out[:, units:], whole[1, :, units:], NT)
    ).astype(BF16)


def send_rows(scalars, total, mid_out, pair_out, cross_out):
    margin = pair_out.shape[0]
    size = mid_out.shape[0]
    odd = scalars[6] == 1
    low = total.astype(BF16)
    head = low[:margin]
    tail = low[margin + size :]
    mid_out[...] = low[margin : margin + size]
    pair_out[...] = jnp.where(odd, head, tail)
    cross_out[...] = jnp.where(odd, tail, head)


def finish_output(scalars, resid, mine, other, outs_bias, mid_out, pair_out, cross_out):
    summed = mine[...].astype(F32) + other[...].astype(F32)
    total = resid[...] + (summed + outs_bias[2:3, :])
    total = jnp.where(valid_rows(scalars, resid.shape[0]), total, 0.0)
    send_rows(scalars, total, mid_out, pair_out, cross_out)


def column_sum(values):
    return jnp.sum(values, axis=0, keepdims=True)


def attend_back(pairs, rows, allowed, drop, q_all, k_all, v_all, o_all, den_all, dq_out, dk_out, dv_out):
    count = k_all.shape[1]
    half = first_half((count, LANES))
    zero = jnp.zeros((), BF16)
    upper = lax.broadcasted_iota(jnp.int32, (LANES, rows), 0) < HD

    def one_pair(p, carry):
        q_pair, k_pair, v_pair = q_all[p], k_all[p], v_all[p]
        grad = drop[p].astype(F32)
        den = den_all[p]
        grad_sums = (grad / den).astype(BF16)
        drift_all = (grad * o_all[p] / den).T
        found = []
        for t in range(2):
            keep = half if t == 0 else jnp.logical_not(half)
            drift = jnp.sum(drift_all[t * HD : (t + 1) * HD, :], axis=0, keepdims=True)
            raw = mm(jnp.where(keep, k_pair, zero), q_pair, NT)
            weights = jnp.where(allowed, jnp.exp(raw), 0.0)
            prob = mm(jnp.where(keep, v_pair, zero), grad_sums, NT)
            score = (weights * (prob - drift)).astype(BF16)
            found.append(
                (
                    mm(k_pair, score, TN),
                    mm(score, q_pair),
                    mm(weights.astype(BF16), grad_sums),
                )
            )
        dq_out[p] = (jnp.where(upper, found[0][0], found[1][0]).T * HD ** -0.5).astype(BF16)
        dk_out[p] = jnp.where(half, found[0][1], found[1][1]).astype(dk_out.dtype)
        dv_out[p] = jnp.where(half, found[0][2], found[1][2]).astype(dv_out.dtype)
        return carry

    lax.fori_loop(0, pairs, one_pair, 0)


def open_gradient(grad, whole, o_all, grad_out, low_out, att_out, drop, copies):
    pairs = drop.shape[0]
    cols = pairs * LANES // 2
    grad_out[...] = grad
    low = grad.astype(BF16)
    low_out[...] = low
    for p in range(pairs):
        att_out[:, p * LANES : (p + 1) * LANES] = o_all[p].astype(BF16)
    for copy in copies:
        copy.wait()
    first = mm(low, whole[0, :, 3 * cols :]).astype(BF16)
    second = mm(low, whole[1, :, 3 * cols :]).astype(BF16)
    by_pairs(jnp.concatenate([first, second], axis=1), drop)


def head_sums(dq_out, dv_out, heads_out):
    for p in range(dq_out.shape[0]):
        heads_out[0:1, p * LANES : (p + 1) * LANES] = column_sum(dq_out[p].astype(F32))
        heads_out[1:2, p * LANES : (p + 1) * LANES] = column_sum(dv_out[p].astype(F32))


def cross_backward(
    mixed, scalars, resid, cotangent, mine, other, gains, q_all, k_all, v_all, o_all, den_all,
    w0,
    grad_out, low_out, att_out, dq_out, dk_out, dv_out, part_out, sums_out, heads_out,
    drop, whole, sems,
):
    copies = fetch(scalars, (w0,), whole, sems, mixed)
    rows = resid.shape[0]
    pairs = q_all.shape[0]
    cols = pairs * LANES // 2
    unit, inverse = normalise(resid[...])
    grad_norm = mine[...].astype(F32) + other[...].astype(F32)
    top = cotangent[...].astype(F32)
    grad = top + norm_back(grad_norm, unit, inverse, gains[2:3, :])
    sums_out[0:1, :] = column_sum(grad_norm * unit)
    sums_out[1:2, :] = column_sum(grad_norm)
    sums_out[2:3, :] = column_sum(top)
    sums_out[3:4, :] = column_sum(grad)
    open_gradient(grad, whole, o_all, grad_out, low_out, att_out, drop, copies)
    frame = lax.broadcasted_iota(jnp.int32, (k_all.shape[1], 1), 0)
    allowed = (frame >= scalars[3]) & (frame < scalars[4])
    attend_back(pairs, rows, allowed, drop, q_all, k_all, v_all, o_all, den_all, dq_out, dk_out, dv_out)
    first, second = halves(dq_out, cols)
    part_out[...] = (mm(first, whole[0, :, :cols], NT) + mm(second, whole[1, :, :cols], NT)).astype(BF16)
    head_sums(dq_out, dv_out, heads_out)


def self_backward(
    scalars, resid, top, mine, other, gains, q_all, k_all, v_all, o_all, den_all,
    w0, w1, w2, w3,
    grad_out, low_out, att_out, dq_out, dk_out, dv_out, part_out, sums_out, heads_out,
    drop, whole, sems,
):
    copies = fetch(scalars, (w0, w1, w2, w3), whole, sems)
    rows = resid.shape[0]
    pairs = q_all.shape[0]
    cols = pairs * LANES // 2
    unit, inverse = normalise(resid[...])
    grad_norm = mine[...].astype(F32) + other[...].astype(F32)
    grad = top[...] + norm_back(grad_norm, unit, inverse, gains[1:2, :])
    sums_out[0:1, :] = column_sum(grad_norm * unit)
    sums_out[1:2, :] = column_sum(grad_norm)
    sums_out[2:3, :] = column_sum(grad)
    open_gradient(grad, whole, o_all, grad_out, low_out, att_out, drop, copies)
    k_place = lax.broadcasted_iota(jnp.int32, (rows, rows), 0)
    q_place = lax.broadcasted_iota(jnp.int32, (rows, rows), 1)
    allowed = (k_place <= q_place) & (k_place >= scalars[1])
    attend_back(pairs, rows, allowed, drop, q_all, k_all, v_all, o_all, den_all, dq_out, dk_out, dv_out)
    pieces = [halves(piece, cols) for piece in (dq_out, dk_out, dv_out)]
    total = jnp.zeros((rows, part_out.shape[1]), F32)
    for group in range(2):
        joined = jnp.concatenate([piece[group] for piece in pieces], axis=1)
        total = total + mm(joined, whole[group, :, : 3 * cols], NT)
    part_out[...] = total.astype(BF16)
    head_sums(dq_out, dv_out, heads_out)


def input_backward(
    scalars, hidden, top, mine, other, gains, sums_one, sums_two, heads_one, heads_two, unit_sums,
    mid_out, pair_out, cross_out, vec_out,
):
    unit, inverse = normalise(hidden[...].astype(F32))
    grad_norm = mine[...].astype(F32) + other[...].astype(F32)
    grad = top[...] + norm_back(grad_norm, unit, inverse, gains[0:1, :])
    send_rows(scalars, grad, mid_out, pair_out, cross_out)
    heads = [heads_one[0:1, :], heads_one[1:2, :], heads_two[0:1, :], heads_two[1:2, :]]
    cols = heads[0].shape[1] // 2
    units = unit_sums.shape[1] // 2
    own = jnp.concatenate([row[:, :cols] for row in heads], axis=1)
    rest = jnp.concatenate([row[:, cols:] for row in heads], axis=1)
    own_units, rest_units = unit_sums[:, :units], unit_sums[:, units:]
    odd = scalars[6] == 1
    rows = [
        column_sum(grad_norm * unit), sums_one[0:1, :], sums_two[0:1, :],
        column_sum(grad_norm), sums_one[1:2, :], sums_two[1:2, :],
        sums_one[2:3, :], sums_two[3:4, :], sums_two[2:3, :],
        jnp.where(odd, rest, own), jnp.where(odd, rest_units, own_units),
        jnp.where(odd, own, rest), jnp.where(odd, own_units, rest_units),
    ]
    for k, row in enumerate(rows):
        vec_out[k : k + 1, :] = row
    vec_out[len(rows) :, :] = jnp.zeros((vec_out.shape[0] - len(rows), vec_out.shape[1]), F32)


def frame_backward(mixed, scalars, dk_all, dv_all, w0, kept_out, given_out, total, whole, sems):
    copies = fetch(scalars, (w0,), whole, sems, mixed)
    pairs = dk_all.shape[0]
    cols = pairs * LANES // 2
    size = kept_out.shape[0]
    frames = dk_all.shape[1]
    near = (frames - size) * 3 // 8
    far = frames - size - near
    keys = halves(dk_all, cols)
    values = halves(dv_all, cols)
    for copy in copies:
        copy.wait()
    for group in range(2):
        joined = jnp.concatenate([keys[group], values[group]], axis=1)
        part = mm(joined, whole[group, :, cols : 3 * cols], NT)
        total[...] = part if group == 0 else total[...] + part
    odd = scalars[6]
    main = scalars[7] == 1
    lead = pl.multiple_of(jnp.where(odd == 0, near, far), 32)
    near_at = pl.multiple_of(jnp.where(odd == 0, 0, far + size), 32)
    far_at = pl.multiple_of(jnp.where(odd == 0, near + size, 0), 32)
    mid = total[pl.ds(lead, size), :].astype(BF16)
    near_part = total[pl.ds(near_at, near), :].astype(BF16)
    far_part = total[pl.ds(far_at, far), :].astype(BF16)

    @pl.when(main)
    def _():
        kept_out[...] = mid
        given_out[:near, :] = near_part
        given_out[near:, :] = far_part

    @pl.when(jnp.logical_not(main))
    def _():
        given_out[...] = mid
        kept_out[:near, :] = near_part
        kept_out[near:, :] = far_part


def send_grads(scalars, whole, out, sems, extra=None):
    rows = whole.shape[1] // 8
    added = 0 if extra is None else extra.shape[0]
    copies = []
    for chip in range(4):
        start = chip * (4 * rows + added)
        for group in range(2):
            for half in range(2):
                at = 2 * rows * chip + rows * jnp.bitwise_xor(scalars[5], half)
                copies.append(
                    pltpu.make_async_copy(
                        whole.at[group, pl.ds(pl.multiple_of(at, rows), rows), :],
                        out.at[pl.ds(start + (2 * group + half) * rows, rows), :],
                        sems.at[len(copies)],
                    )
                )
        if added:
            copies.append(
                pltpu.make_async_copy(extra, out.at[pl.ds(start + 4 * rows, added), :], sems.at[len(copies)])
            )
    for copy in copies:
        copy.start()
    for copy in copies:
        copy.wait()


def unit_grads(scalars, norm, pre, top, act, out, whole, sems):
    units = pre.shape[1] // 2
    for group in range(2):
        at = slice(group * units, (group + 1) * units)
        whole[group, :, :units] = mm(norm[...], pre[:, at], TN).astype(BF16)
        whole[group, :, units:] = mm(top[...], act[:, at], TN).astype(BF16)
    send_grads(scalars, whole, out, sems)


def cross_grads(scalars, norm, frames, low, att, dq, dk, dv, vectors, out, low_vectors, whole, sems):
    low_vectors[...] = vectors[...].astype(BF16)
    cols = att.shape[1] // 2
    parts = [halves(piece, cols) for piece in (dq, dk, dv)]
    for group in range(2):
        at = slice(group * cols, (group + 1) * cols)
        joined = jnp.concatenate([parts[1][group], parts[2][group]], axis=1)
        found = [mm(norm[...], parts[0][group], TN), mm(frames[...], joined, TN), mm(low[...], att[:, at], TN)]
        whole[group] = jnp.concatenate(found, axis=1).astype(BF16)
    send_grads(scalars, whole, out, sems, low_vectors)


def self_grads(scalars, norm, low, att, dq, dk, dv, out, whole, sems):
    cols = att.shape[1] // 2
    parts = [halves(piece, cols) for piece in (dq, dk, dv)]
    for group in range(2):
        at = slice(group * cols, (group + 1) * cols)
        joined = jnp.concatenate([part[group] for part in parts], axis=1)
        found = [mm(norm[...], joined, TN), mm(low[...], att[:, at], TN)]
        whole[group] = jnp.concatenate(found, axis=1).astype(BF16)
    send_grads(scalars, whole, out, sems)


SMEM = pl.BlockSpec(memory_space=pltpu.SMEM)
VMEM = pl.BlockSpec(memory_space=pltpu.VMEM)
ANY = pl.BlockSpec(memory_space=pl.ANY)


def shape(dims, dtype):
    return jax.ShapeDtypeStruct(tuple(dims), dtype)


def kernel_call(kernel, name, cost, operands, spaces, outs, out_spaces=None, scratch=()):
    return pl.pallas_call(
        kernel,
        out_shape=tuple(outs),
        in_specs=list(spaces),
        out_specs=tuple(out_spaces or [VMEM] * len(outs)),
        scratch_shapes=list(scratch),
        compiler_params=pltpu.CompilerParams(vmem_limit_bytes=56 * 1024 * 1024),
        cost_estimate=pl.CostEstimate(flops=int(cost * 1e9), transcendentals=0, bytes_accessed=1 << 20),
        name=name,
    )(*operands)


def body(
    hidden, encoded, token_lengths, frame_counts, ln_gain, ln_bias, head_bias, out_bias, fc_bias,
    self_proj, cross_proj, out_proj, fc_in, fc_out, cotangent,
):
    wide = lax.axis_size("wide")
    depth = lax.axis_size("narrow")
    tok_rows, width = hidden.shape[1:]
    frame_rows = encoded.shape[1]
    swing = (MAXLEN - tok_rows) // 2
    ratio = frame_rows // tok_rows
    near = ratio * swing
    far = frame_rows - near
    assert far >= near + JITTER and 8 * near == 3 * frame_rows
    assert depth == 4 and hidden.shape[0] == 2
    rows = tok_rows + 2 * swing
    frames = near + frame_rows + far
    shard = width // wide
    block = 2 * shard
    head_cols = head_bias.shape[1]
    cols = 2 * head_cols
    pairs = cols // LANES
    hidden_units = fc_bias.shape[0]
    units = 2 * hidden_units

    w = lax.axis_index("wide")
    n = lax.axis_index("narrow")
    chip = w // 2
    core = w % 2
    batch = n // 2
    odd = n % 2
    item = 2 * chip + odd
    main = core == odd
    home = core == batch
    relay = wide == 8

    def move(value, rule):
        pairs_list = []
        for ws in range(wide):
            for ns in range(depth):
                target = rule(ws, ns)
                if target is not None and 0 <= target[0] < wide:
                    pairs_list.append((ws * depth + ns, target[0] * depth + target[1]))
        return lax.ppermute(value, AXES, pairs_list)

    def swap(value):
        return move(value, lambda a, z: (a ^ 1, z))

    def after(value, *events):
        return lax.optimization_barrier((value, *events))[0]

    def pick(value, index):
        return lax.dynamic_index_in_dim(value, index, 0, keepdims=False)

    bias_vector = jnp.concatenate([head_bias.reshape(-1), fc_bias])
    bias_high = lax.reduce_precision(bias_vector, 8, 7)
    bias_rest = bias_vector - bias_high
    bias_middle = lax.reduce_precision(bias_rest, 8, 7)
    bias_parts = jnp.stack([bias_high, bias_middle, bias_rest - bias_middle]).astype(BF16)
    bias_parts = jnp.concatenate([bias_parts.reshape(6, width), jnp.zeros((2, width), BF16)], axis=0)

    def group(stack, out):
        return jnp.concatenate([stack[0], stack[1], stack[2], out.T], axis=1)

    def away(value):
        return move(value, lambda a, z: (a ^ 1, z) if a % 2 != z // 2 else None)

    def two_groups(value):
        opposite = move(value, lambda a, z: (a, z ^ 2) if a % 2 == z // 2 else None)
        same = jnp.where(home, value, opposite)
        return same, move(same, lambda a, z: (a, z ^ 1))

    groups = [list(range(k, wide, 2)) for k in range(2)]

    def in_quarters(joined):
        if relay:
            return lax.all_gather(joined, "wide", axis=0, tiled=True, axis_index_groups=groups)
        size = joined.shape[1]
        full = lax.all_gather(joined.reshape(2, 2, shard, size), "wide", axis_index_groups=groups)
        full = jnp.where(core == 0, full, full[:, :, ::-1])
        full = jnp.swapaxes(full, 0, 1).reshape(2, 4, width // 4, size)
        return jnp.swapaxes(full, 0, 1).reshape(-1, size)

    def between_chips(joined, *events):
        if relay:
            joined = after(joined, *events)
            return [joined] + [move(joined, partial(lambda k, a, z: (a ^ k, z), 2 * k)) for k in (1, 2, 3)]
        full = in_quarters(joined)
        return [full[j * width // 2 : (j + 1) * width // 2] for j in range(4)]

    def edge(value, margin):
        start = jnp.where(odd == 0, value.shape[1] - margin, 0)
        return lax.dynamic_slice(value, (batch, start, 0), (1, margin, width))[0]

    def halo_rule(a, z):
        if a % 2 == z % 2:
            return None
        return (a + 1, z) if z % 2 == 0 else (a - 1, z)

    edges = jnp.concatenate([edge(hidden, swing), edge(cotangent, swing), edge(encoded, near)], axis=0)
    halo = move(edges, halo_rule)
    halo = jnp.where(main, halo, move(halo, lambda a, z: (a ^ 1, z) if a % 2 == z % 2 else None))
    hidden_halo, top_halo, frame_halo = halo[:swing], halo[swing : 2 * swing], halo[2 * swing :]

    rest_piece = jnp.concatenate([group(cross_proj, out_proj[1]), fc_in, fc_out.T], axis=1)
    if relay:
        rest_w = lax.all_gather(rest_piece, AXES, axis=0, tiled=True)
    else:
        rest_here = jnp.concatenate([rest_piece, away(rest_piece)], axis=0)
        rest_w = in_quarters(jnp.concatenate(two_groups(rest_here), axis=0))
    self_piece = group(self_proj, out_proj[0])
    self_got = two_groups(jnp.concatenate([self_piece, away(self_piece), bias_parts], axis=0))
    self_own = after(jnp.concatenate([x[:block] for x in self_got], axis=0), halo)
    self_w = between_chips(self_own)
    biases = jnp.concatenate([x[block:] for x in self_got], axis=0)

    own_hidden = pick(hidden, batch)
    own_top = pick(after(cotangent, self_own), batch)
    own_frames = pick(after(encoded, self_own), batch)
    token_lengths = after(token_lengths, self_own)
    lengths = pick(token_lengths, batch)
    counts = pick(frame_counts, batch)
    items = jnp.arange(lengths.shape[0], dtype=jnp.int32)
    tok_lo = jnp.sum(jnp.where(items < item, lengths, 0)) - (tok_rows * item - swing)
    tok_hi = tok_lo + jnp.sum(jnp.where(items == item, lengths, 0))
    frame_start = frame_rows * item - jnp.where(odd == 0, near, far)
    frame_lo = jnp.sum(jnp.where(items < item, counts, 0)) - frame_start
    frame_hi = frame_lo + jnp.sum(jnp.where(items == item, counts, 0))
    nothing = jnp.zeros((), jnp.int32)
    here, order = (chip, core) if relay else (nothing, nothing)
    scalars = jnp.stack(
        [here, tok_lo, tok_hi, frame_lo, frame_hi, order, odd, main.astype(jnp.int32)]
    ).astype(jnp.int32)

    low_shape = shape((rows, width), BF16)
    wide_f32 = shape((rows, width), F32)
    head_b = shape((pairs, rows, LANES), BF16)
    head_f = shape((pairs, rows, LANES), F32)
    frame_b = shape((pairs, frames, LANES), BF16)
    att_shape = shape((rows, cols), BF16)
    frame_full = shape((frames, width), BF16)
    sems = pltpu.SemaphoreType.DMA((20,))
    head_scratch = [pltpu.VMEM((2, width, width), BF16), sems]
    unit_scratch = [pltpu.VMEM((2, width, 2 * hidden_units), BF16), sems]

    hidden_rows, low_one, self_q, self_k, self_v, self_o, self_den, part = kernel_call(
        self_forward, "self_forward", 8,
        (scalars, own_hidden, swap(own_hidden), hidden_halo, ln_gain, ln_bias, biases, *self_w),
        [SMEM] + [VMEM] * 6 + [ANY] * 4,
        [low_shape, low_shape, head_b, head_b, head_b, head_f, head_f, low_shape],
        scratch=head_scratch,
    )
    frame_window, cross_k, cross_v = kernel_call(
        partial(frame_project, relay), "frame_project", 7,
        (scalars, own_frames, swap(own_frames), after(frame_halo, part), biases, rest_w),
        [SMEM] + [VMEM] * 4 + [ANY],
        [frame_full, frame_b, frame_b],
        scratch=head_scratch,
    )
    resid_one, low_two, cross_q, cross_o, cross_den, part_two = kernel_call(
        partial(cross_forward, relay), "cross_forward", 11,
        (scalars, hidden_rows, part, swap(part), ln_gain, ln_bias, out_bias, biases, cross_k, cross_v, rest_w),
        [SMEM] + [VMEM] * 9 + [ANY],
        [wide_f32, low_shape, head_b, head_f, head_f, low_shape],
        scratch=head_scratch,
    )
    act_shape = shape((rows, units), BF16)
    resid_two, low_three, top_rows, low_act, grad_pre, part_three, back_three, unit_sums = kernel_call(
        partial(unit_forward, relay), "unit_forward", 14,
        (scalars, resid_one, part_two, swap(part_two), ln_gain, ln_bias, out_bias, biases, own_top, swap(own_top), top_halo, rest_w),
        [SMEM] + [VMEM] * 10 + [ANY],
        [wide_f32, low_shape, low_shape, act_shape, act_shape, low_shape, low_shape, shape((1, units), F32)],
        scratch=unit_scratch,
    )
    other_back = swap(back_three)
    other_three = swap(part_three)

    def between_back(grads):
        if relay:
            return lax.psum_scatter(grads, "wide", scatter_dimension=0, tiled=True, axis_index_groups=groups)
        size = grads.shape[1]
        full = jnp.swapaxes(grads.reshape(4, 2, width // 4, size), 0, 1).reshape(2, wide // 2, 2, shard, size)
        full = jnp.swapaxes(jnp.where(core == 0, full, full[:, :, ::-1]), 0, 1)
        total = lax.psum_scatter(full, "wide", scatter_dimension=0, axis_index_groups=groups)
        return total.reshape(2 * block, size)

    def from_opposite(paired):
        return move(paired, lambda a, z: (a, z ^ 2) if a % 2 != z // 2 else None)

    def to_owner(paired, opposite):
        summed = paired.astype(F32) + opposite.astype(F32)
        passed = move(summed[shard:], lambda a, z: (a ^ 1, z) if a % 2 == z // 2 else None)
        return jnp.where(home, summed[:shard], passed)

    def grads_of(kernel, name, cost, size, scratch, *operands, added=0):
        return kernel_call(
            kernel, name, cost, (scalars, *operands),
            [SMEM] + [VMEM] * len(operands),
            [shape((2 * width + 4 * added, size), BF16)],
            [ANY],
            scratch=scratch,
        )[0]

    grads_unit = grads_of(
        unit_grads, "unit_grads", 9, 2 * hidden_units, unit_scratch, low_three, grad_pre, top_rows, low_act
    )
    unit_total = between_back(grads_unit)
    sums_shape = shape((8, width), F32)
    heads_shape = shape((8, cols), F32)
    drop_scratch = [pltpu.VMEM((pairs, rows, LANES), BF16)]
    grad_two, low_grad_two, low_cross, cq_grad, ck_grad, cv_grad, back_two, sums_two, heads_two = kernel_call(
        partial(cross_backward, relay), "cross_backward", 21,
        (scalars, resid_two, top_rows, back_three, after(other_back, grads_unit), ln_gain, cross_q, cross_k, cross_v, cross_o, cross_den, rest_w),
        [SMEM] + [VMEM] * 10 + [ANY],
        [wide_f32, low_shape, att_shape, head_b, frame_b, frame_b, low_shape, sums_shape, heads_shape],
        scratch=drop_scratch + head_scratch,
    )
    def cross_rule(a, z):
        if a % 2 == z % 2:
            return None
        return (a - 2, z ^ 1) if z % 2 == 0 else (a + 2, z ^ 1)

    def pair_rule(a, z):
        return None if a % 2 == z % 2 else (a, z ^ 1)

    def from_main(value, step):
        return move(value, lambda a, z: (a, z ^ step) if a % 2 == z % 2 else None)

    def per_batch(near_copy, far_copy, dtype):
        near_copy, far_copy = near_copy.astype(dtype), far_copy.astype(dtype)
        return jnp.stack(
            [jnp.where(batch == 0, near_copy, far_copy), jnp.where(batch == 0, far_copy, near_copy)]
        )

    def token_block(mid, from_pair, from_cross):
        above = jnp.where(odd == 1, from_pair, from_cross)
        below = jnp.where(odd == 1, from_cross, from_pair)
        return jnp.concatenate([mid[:swing] + above, mid[swing:-swing], mid[-swing:] + below], axis=0)

    edge_shape = shape((swing, width), BF16)
    slice_shapes = [shape((tok_rows, width), BF16), edge_shape, edge_shape]
    out_mid, out_pair, out_cross = kernel_call(
        finish_output, "finish_output", 3,
        (scalars, resid_two, part_three, after(other_three, grad_two), out_bias),
        [SMEM] + [VMEM] * 4,
        slice_shapes,
    )
    grad_one, low_grad_one, low_self, sq_grad, sk_grad, sv_grad, back_one, sums_one, heads_one = kernel_call(
        self_backward, "self_backward", 12,
        (scalars, resid_one, grad_two, back_two, after(swap(back_two), out_mid), ln_gain, self_q, self_k, self_v, self_o, self_den, *self_w),
        [SMEM] + [VMEM] * 10 + [ANY] * 4,
        [wide_f32, low_shape, att_shape, head_b, head_b, head_b, low_shape, sums_shape, heads_shape],
        scratch=drop_scratch + head_scratch,
    )
    kept, given = kernel_call(
        partial(frame_backward, relay), "frame_backward", 7,
        (scalars, after(ck_grad, back_one), cv_grad, rest_w),
        [SMEM] + [VMEM] * 2 + [ANY],
        [shape((frame_rows, width), BF16)] * 2,
        scratch=[pltpu.VMEM((frames, width), F32)] + head_scratch,
    )
    in_mid, in_pair, in_cross, vectors = kernel_call(
        input_backward, "input_backward", 4,
        (scalars, hidden_rows, grad_one, back_one, after(swap(back_one), kept), ln_gain, sums_one, sums_two, heads_one, heads_two, unit_sums),
        [SMEM] + [VMEM] * 10,
        slice_shapes + [shape((16, width), F32)],
    )
    grads_self = grads_of(
        self_grads, "self_grads", 5, width, head_scratch,
        after(low_one, in_mid), low_grad_one, low_self, sq_grad, sk_grad, sv_grad,
    )
    self_total = between_back(after(grads_self, unit_total))
    half_sum = (kept.astype(F32) + swap(given).astype(F32)).astype(BF16)
    half_sum = after(half_sum, grads_self)
    from_pair = move(jnp.concatenate([half_sum[near:], in_pair, out_pair], axis=0), pair_rule)
    from_cross = move(jnp.concatenate([half_sum[:near], in_cross, out_cross], axis=0), cross_rule)
    added = vectors.shape[0]
    grads_cross = grads_of(
        cross_grads, "cross_grads", 8, width, [pltpu.VMEM((added, width), BF16)] + head_scratch,
        low_two, frame_window, low_grad_two, low_cross, after(cq_grad, half_sum), ck_grad, cv_grad, vectors,
        added=added,
    )
    extra = jnp.where(
        odd == 1,
        jnp.concatenate([from_pair[:far], from_cross[:near]], axis=0),
        jnp.concatenate([from_cross[:near], from_pair[:far]], axis=0),
    )
    frame_block = after(half_sum + extra, grads_cross)
    token_rows = jnp.concatenate(
        [
            token_block(in_mid, from_pair[far:-swing], from_cross[near:-swing]),
            token_block(out_mid, from_pair[-swing:], from_cross[-swing:]),
        ],
        axis=0,
    )
    frame_opposite = from_main(frame_block, 2)
    frame_beside = from_main(frame_block, 1)
    if relay:
        cross_total = between_back(after(grads_cross, self_total, frame_beside))
    else:
        parts = grads_cross.reshape(4, -1, width)[:, : width // 2].reshape(-1, width)
        cross_total = jnp.concatenate(
            [between_back(parts), jnp.zeros((added, width), BF16)], axis=0
        )
    early = jnp.concatenate([unit_total, self_total], axis=1)
    early_across = move(after(early[block:], frame_beside), lambda a, z: (a, z ^ 1))
    early_paired = (early[:block].astype(F32) + early_across.astype(F32)).astype(BF16)
    token_rows = after(token_rows, frame_opposite)
    frame_third = from_main(frame_opposite, 1)
    token_opposite = from_main(token_rows, 2)
    token_beside = from_main(token_rows, 1)
    early_opposite = from_opposite(early_paired)
    cross_total = after(cross_total, early_paired)
    cross_across = move(cross_total[block:], lambda a, z: (a, z ^ 1))
    cross_paired = (cross_total[:block].astype(F32) + cross_across[:block].astype(F32)).astype(BF16)
    if relay:
        vectors = cross_total[2 * block :].astype(F32) + cross_across[block:].astype(F32)
        vectors = vectors + move(vectors, lambda a, z: (a, z ^ 2))
    else:
        vectors = lax.psum(lax.psum(vectors, "narrow"), "wide", axis_index_groups=groups)
    token_third = from_main(after(token_opposite, cross_paired), 1)
    cross_opposite = from_opposite(cross_paired)
    grad_early = to_owner(early_paired, after(early_opposite, cross_paired))
    grad_unit, grad_self = grad_early[:, : 2 * hidden_units], grad_early[:, 2 * hidden_units :]
    grad_cross = to_owner(cross_paired, cross_opposite)

    def copied(first, last, value, opposite, beside, third, dtype):
        near_copy = jnp.where(main, value[first:last], beside[first:last])
        far_copy = jnp.where(main, opposite[first:last], third[first:last])
        return per_batch(near_copy, far_copy, dtype)

    encoded_grad = copied(0, frame_rows, frame_block, frame_opposite, frame_beside, frame_third, F32)
    tokens = (token_rows, token_opposite, token_beside, token_third)
    input_grad = copied(0, tok_rows, *tokens, F32)
    output = copied(tok_rows, 2 * tok_rows, *tokens, BF16)

    def unpacked(grad):
        stack = jnp.stack([grad[:, head_cols * k : head_cols * (k + 1)] for k in range(3)])
        return stack, grad[:, 3 * head_cols :].T

    grad_self_proj, grad_out_one = unpacked(grad_self)
    grad_cross_proj, grad_out_two = unpacked(grad_cross)

    mine = lax.dynamic_slice_in_dim(vectors, 9 + 2 * odd, 2, 0)
    mine = jnp.where(home, mine, swap(mine))
    return (
        output,
        input_grad,
        encoded_grad,
        vectors[:3],
        vectors[3:6],
        mine[0].reshape(4, head_cols),
        vectors[6:9],
        mine[1],
        grad_self_proj,
        grad_cross_proj,
        jnp.stack([grad_out_one, grad_out_two]),
        grad_unit[:, :hidden_units],
        grad_unit[:, hidden_units:].T,
    )


def solution(mesh):
    in_specs = (
        P(None, "wide", None),
        P(None, "wide", None),
        P(),
        P(),
        P(),
        P(),
        P(None, "narrow"),
        P(),
        P("narrow"),
        P(None, "wide", "narrow"),
        P(None, "wide", "narrow"),
        P(None, "narrow", "wide"),
        P("wide", "narrow"),
        P("narrow", "wide"),
        P(None, "wide", None),
    )
    out_specs = (
        P(None, "wide", None),
        P(None, "wide", None),
        P(None, "wide", None),
        P(),
        P(),
        P(None, "narrow"),
        P(),
        P("narrow"),
        P(None, "wide", "narrow"),
        P(None, "wide", "narrow"),
        P(None, "narrow", "wide"),
        P("wide", "narrow"),
        P("narrow", "wide"),
    )
    return jax.shard_map(body, mesh=mesh, in_specs=in_specs, out_specs=out_specs, check_vma=False)
```

time: 604 us -> 413 us (0.68)
  the two profiles are of different devices: /device:TPU:12 before, /device:TPU:0 now
where the time goes in v2:
time: 413 us; the launch traced here: 407 us
  waiting for transfers between devices  133 us (32%)
  Pallas kernels  114 us (28%)
  starting transfers between devices  89.5 us (22%)
  local copies, waits for them, and re-layouts  28.4 us (7%)
  other arithmetic  24.8 us (6%)
  between operations  17.5 us (4%)
    pallas_call x12, Pallas kernels, kernel_call(): pl.pallas_call(kernel, out_shape=tuple(outs), in_specs=list(spaces), out_...  114 us
    ppermute x34, waiting for transfers between devices, move(): return lax.ppermute(value, AXES, pairs_list)  107 us
    ppermute x34, starting transfers between devices, move(): return lax.ppermute(value, AXES, pairs_list)  88.9 us
    all_gather x1, waiting for transfers between devices, body(): rest_w = lax.all_gather(rest_piece, AXES, axis=0, tiled=True)  25.3 us
    unnamed x79, local copies, waits for them, and re-layouts  12.7 us
    another operation x6, other arithmetic, per_batch(): jnp.stack([jnp.where(batch == 0, near_copy, far_copy), jnp.where(batch ==...  9.32 us
  transfers between devices with their start and end apart: 38, of which 17 were waited for; matrix products, arithmetic and copies ran while one was open for 9% of the time, Pallas kernels for 20%

profile of v2, /device:TPU:0, one launch (start us, length us, event | category | flops | bytes accessed | tf_op | source)
XLA Modules:
  0.0 407.0 jit_solution(7523198093256397707)
XLA Ops:
  22.3 6.0 %collective-permute-start.1 = (bf16[200,768]{1,0:T(8,128)(2,1)}, bf16[200,768]{1,0:T(8,128)(2,1)}, u32[]{:S(2)}, u32[]{:S(2)}) collective-permute-start(bf16[200,768]{1,0:T(8,128)(2,1)} %maximum_maximum_fusion), channel_id=1, source_target_pairs={{0,2},{1,3},{6,4},{7,5},{8,10},{9,11},{14,12},{15,13},{16,18},{17,... | collective-permute-start | bytes 921608 | tf_op jit(solution)/shard_map/ppermute | solution.py:604
  36.5 5.4 %collective-permute-start.2 = (bf16[200,768]{1,0:T(8,128)(2,1)S(1)}, bf16[200,768]{1,0:T(8,128)(2,1)}, u32[]{:S(2)}, u32[]{:S(2)}) collective-permute-start(bf16[200,768]{1,0:T(8,128)(2,1)S(1)} %broadcast_select_fusion.3), channel_id=1, source_target_pairs={{0,1},{1,0},{2,3},{3,2},{4,5},{5,4},{6,7},{7,6},{8,9},{9,8},{10,11... | collective-permute-start | bytes 921608 | tf_op jit(solution)/shard_map/ppermute | solution.py:604
  41.9 8.3 %collective-permute-done.2 = bf16[200,768]{1,0:T(8,128)(2,1)} collective-permute-done((bf16[200,768]{1,0:T(8,128)(2,1)S(1)}, bf16[200,768]{1,0:T(8,128)(2,1)}, u32[]{:S(2)}, u32[]{:S(2)}) %collective-permute-start.2) | collective-permute-done | bytes 307232 | tf_op jit(solution)/shard_map/ppermute | solution.py:604
  60.9 6.7 %collective-permute-start.10 = (bf16[768,768]{1,0:T(8,128)(2,1)}, bf16[768,768]{1,0:T(8,128)(2,1)S(1)}, u32[]{:S(2)}, u32[]{:S(2)}) collective-permute-start(bf16[768,768]{1,0:T(8,128)(2,1)} %dynamic-slice_bitcast_fusion.own), channel_id=1, source_target_pairs={{0,4},{1,5},{2,6},{3,7},{4,0},{5,1},{6,2},{7,3},{8,12},{9,13},{10,... | collective-permute-start | bytes 3538952 | tf_op jit(solution)/shard_map/ppermute | solution.py:604
  74.3 7.3 %collective-permute-done.8.w3 = bf16[384,768]{1,0:T(8,128)(2,1)} collective-permute-done((bf16[384,768]{1,0:T(8,128)(2,1)}, bf16[384,768]{1,0:T(8,128)(2,1)}, u32[]{:S(2)}, u32[]{:S(2)}) %collective-permute-start.8) | collective-permute-done | bytes 589856 | tf_op jit(solution)/shard_map/ppermute | solution.py:604
  81.6 8.3 %self_forward.1 = (bf16[448,768]{1,0:T(8,128)(2,1)}, bf16[448,768]{1,0:T(8,128)(2,1)}, bf16[3,448,128]{2,1,0:T(8,128)(2,1)}, bf16[3,448,128]{2,1,0:T(8,128)(2,1)...) custom-call(s32[8]{0:T(128)} %stack.107.scalars, ...), custom_call_target="tpu_custom_call" | custom-call | flops 8000000000 | bytes 1048576 | tf_op jit(solution)/shard_map/self_forward/pallas_call | solution.py:550
  89.9 15.4 %collective-permute-start.9 = (bf16[448,768]{1,0:T(8,128)(2,1)}, bf16[448,768]{1,0:T(8,128)(2,1)S(1)}, u32[]{:S(2)}, u32[]{:S(2)}) collective-permute-start(bf16[448,768]{1,0:T(8,128)(2,1)} %get-tuple-element.89.mine), channel_id=1, source_target_pairs={{0,4},{1,5},{2,6},{3,7},{4,0},{5,1},{6,2},{7,3},{8,12},{9,13},{10,... | collective-permute-start | bytes 2064392 | tf_op jit(solution)/shard_map/ppermute | solution.py:604
  106.2 25.3 %all-gather.2.cloned.1.call-done.w0 = bf16[3072,2304]{1,0:T(8,128)(2,1)} async-done(((bf16[96,2304]{1,0:T(8,128)(2,1)}), bf16[3072,2304]{1,0:T(8,128)(2,1)}) %all-gather.2.cloned.1.call-update) | async-done | bytes 14155792 | tf_op jit(solution)/shard_map/all_gather | solution.py:667
  131.5 7.9 %frame_project.1 = (bf16[1536,768]{1,0:T(8,128)(2,1)}, bf16[3,1536,128]{2,1,0:T(8,128)(2,1)}, bf16[3,1536,128]{2,1,0:T(8,128)(2,1)}) custom-call(s32[8]{0:T(128)} %stack.107.scalars, bf16[768,768]{1,0:T(8,128)(2,1)} %dynamic-slice_bitcast_fusion.own, bf16[768,768]{1,0:T(8,128)(2,1)} %copy-done.24, bf16[288,768]{1,0:T(8,128)(2,1)} %slice.267.halo, ...), custom_call_target="tpu_custom_call" | custom-call | flops 7000000000 | bytes 1048576 | tf_op jit(solution)/shard_map/frame_project/pallas_call | solution.py:550
  140.3 11.6 %cross_forward.1 = (f32[448,768]{1,0:T(8,128)}, bf16[448,768]{1,0:T(8,128)(2,1)}, bf16[3,448,128]{2,1,0:T(8,128)(2,1)}, f32[3,448,128]{2,1,0:T(8,128)}, f32[3,44...) custom-call(s32[8]{0:T(128)} %stack.107.scalars, bf16[448,768]{1,0:T(8,128)(2,1)} %get-tuple-element.88.hidden, ...), custom_call_target="tpu_custom_call" | custom-call | flops 11000000512 | bytes 1048576 | tf_op jit(solution)/shard_map/cross_forward/pallas_call | solution.py:550
  155.6 14.3 %unit_forward.1 = (f32[448,768]{1,0:T(8,128)}, bf16[448,768]{1,0:T(8,128)(2,1)}, bf16[448,768]{1,0:T(8,128)(2,1)}, bf16[448,1536]{1,0:T(8,128)(2,1)}, bf16[448,1...) custom-call(s32[8]{0:T(128)} %stack.107.scalars, ...), custom_call_target="tpu_custom_call" | custom-call | flops 14000000000 | bytes 1048576 | tf_op jit(solution)/shard_map/unit_forward/pallas_call | solution.py:550
  169.9 7.2 %unit_grads.1 = bf16[1536,1536]{1,0:T(8,128)(2,1)} custom-call(s32[8]{0:T(128)} %stack.107.scalars, bf16[448,768]{1,0:T(8,128)(2,1)} %get-tuple-element.100.norm, bf16[448,1536]{1,0:T(8,128)(2,1)} %get-tuple-element.101.pre, bf16[448,768]{1,0:T(8,128)(2,1)} %get-tuple-element.98.top.cotangent, bf16[448,1536]{1,0:T(8,128)(2,1)} %get-tuple-element.102.act), custom_call_target="tpu_custom_call" | custom-call | flops 8999999488 | bytes 1048576 | tf_op jit(solution)/shard_map/unit_grads/pallas_call | solution.py:550
  181.2 22.7 %cross_backward.1 = (f32[448,768]{1,0:T(8,128)}, bf16[448,768]{1,0:T(8,128)(2,1)}, bf16[448,384]{1,0:T(8,128)(2,1)}, bf16[3,448,128]{2,1,0:T(8,128)(2,1)}, bf16[...) custom-call(s32[8]{0:T(128)} %stack.107.scalars, ...), custom_call_target="tpu_custom_call" | custom-call | flops 20999999488 | bytes 1048576 | tf_op jit(solution)/shard_map/cross_backward/pallas_call | solution.py:550
  209.0 12.3 %self_backward.1 = (f32[448,768]{1,0:T(8,128)}, bf16[448,768]{1,0:T(8,128)(2,1)}, bf16[448,384]{1,0:T(8,128)(2,1)}, bf16[3,448,128]{2,1,0:T(8,128)(2,1)}, bf16[3...) custom-call(s32[8]{0:T(128)} %stack.107.scalars, ...), custom_call_target="tpu_custom_call" | custom-call | flops 12000000000 | bytes 1048576 | tf_op jit(solution)/shard_map/self_backward/pallas_call | solution.py:550
  221.6 8.8 %frame_backward.1 = (bf16[768,768]{1,0:T(8,128)(2,1)}, bf16[768,768]{1,0:T(8,128)(2,1)}) custom-call(s32[8]{0:T(128)} %stack.107.scalars, bf16[3,1536,128]{2,1,0:T(8,128)(2,1)} %get-tuple-element.121.dk_all.dk, bf16[3,1536,128]{2,1,0:T(8,128)(2,1)} %get-tuple-element.122.dv_all.dv, bf16[3072,2304]{1,0:T(8,128)(2,1)} %all-gather.2.cloned.1.call-done.w0), custom_call_target="tpu_custom_call" | custom-call | flops 7000000000 | bytes 1048576 | tf_op jit(solution)/shard_map/frame_backward/pallas_call | solution.py:550
  235.4 5.2 %self_grads.1 = bf16[1536,768]{1,0:T(8,128)(2,1)} custom-call(s32[8]{0:T(128)} %stack.107.scalars, bf16[448,768]{1,0:T(8,128)(2,1)} %get-tuple-element.133.norm, bf16[448,768]{1,0:T(8,128)(2,1)} %get-tuple-element.134.low, bf16[448,384]{1,0:T(8,128)(2,1)} %get-tuple-element.135.att, bf16[3,448,128]{2,1,0:T(8,128)(2,1)} %get-tuple-element.136.dq, ...), custom_call_target="tpu_custom_call" | custom-call | flops 5000000000 | bytes 1048576 | tf_op jit(solution)/shard_map/self_grads/pallas_call | solution.py:550
  250.4 8.8 %cross_grads.1 = bf16[1600,768]{1,0:T(8,128)(2,1)} custom-call(s32[8]{0:T(128)} %stack.107.scalars, bf16[448,768]{1,0:T(8,128)(2,1)} %get-tuple-element.144.norm, bf16[1536,768]{1,0:T(8,128)(2,1)} %get-tuple-element.145.frames, bf16[448,768]{1,0:T(8,128)(2,1)} %get-tuple-element.146.low, bf16[448,384]{1,0:T(8,128)(2,1)} %get-tuple-element.147.att, ...), custom_call_target="tpu_custom_call" | custom-call | flops 8000000000 | bytes 1048576 | tf_op jit(solution)/shard_map/cross_grads/pallas_call | solution.py:550
  259.2 4.7 %collective-permute-done.18 = bf16[672,768]{1,0:T(8,128)(2,1)S(1)} collective-permute-done((bf16[672,768]{1,0:T(8,128)(2,1)}, bf16[672,768]{1,0:T(8,128)(2,1)S(1)}, u32[]{:S(2)}, u32[]{:S(2)}) %collective-permute-start.18) | collective-permute-done | bytes 1032224 | tf_op jit(solution)/shard_map/ppermute | solution.py:604
  264.6 11.5 %collective-permute-start.23 = (bf16[768,768]{1,0:T(8,128)(2,1)S(1)}, bf16[768,768]{1,0:T(8,128)(2,1)}, u32[]{:S(2)}, u32[]{:S(2)}) collective-permute-start(bf16[768,768]{1,0:T(8,128)(2,1)S(1)} %fusion.2), channel_id=1, source_target_pairs={{0,1},{2,3},{5,4},{7,6},{8,9},{10,11},{13,12},{15,14},{16,17},{18,... | collective-permute-start | bytes 3538952 | tf_op jit(solution)/shard_map/ppermute | solution.py:604
  276.2 12.7 %collective-permute-done.23 = bf16[768,768]{1,0:T(8,128)(2,1)} collective-permute-done((bf16[768,768]{1,0:T(8,128)(2,1)S(1)}, bf16[768,768]{1,0:T(8,128)(2,1)}, u32[]{:S(2)}, u32[]{:S(2)}) %collective-permute-start.23) | collective-permute-done | bytes 1179680 | tf_op jit(solution)/shard_map/ppermute | solution.py:604
  298.6 19.2 %collective-permute-done.20 = bf16[768,768]{1,0:T(8,128)(2,1)} collective-permute-done((bf16[768,768]{1,0:T(8,128)(2,1)S(1)}, bf16[768,768]{1,0:T(8,128)(2,1)}, u32[]{:S(2)}, u32[]{:S(2)}) %collective-permute-start.20) | collective-permute-done | bytes 1179680 | tf_op jit(solution)/shard_map/ppermute | solution.py:604
  327.0 12.0 %collective-permute-done.24 = bf16[192,2304]{1,0:T(8,128)(2,1)S(1)} collective-permute-done((bf16[192,2304]{1,0:T(8,128)(2,1)S(1)}, bf16[192,2304]{1,0:T(8,128)(2,1)S(1)}, u32[]{:S(2)}, u32[]{:S(2)}) %collective-permute-start.24) | collective-permute-done | bytes 884768 | tf_op jit(solution)/shard_map/ppermute | solution.py:604
  341.6 7.1 %collective-permute-done.27 = bf16[768,768]{1,0:T(8,128)(2,1)} collective-permute-done((bf16[768,768]{1,0:T(8,128)(2,1)}, bf16[768,768]{1,0:T(8,128)(2,1)}, u32[]{:S(2)}, u32[]{:S(2)}) %collective-permute-start.27) | collective-permute-done | bytes 1179680 | tf_op jit(solution)/shard_map/ppermute | solution.py:604
  353.1 17.9 %collective-permute-done.25 = bf16[208,768]{1,0:T(8,128)(2,1)S(1)} collective-permute-done((bf16[208,768]{1,0:T(8,128)(2,1)S(1)}, bf16[208,768]{1,0:T(8,128)(2,1)S(1)}, u32[]{:S(2)}, u32[]{:S(2)}) %collective-permute-start.25) | collective-permute-done | bytes 319520 | tf_op jit(solution)/shard_map/ppermute | solution.py:604
  (221 shorter events, 122.9 us)
Async XLA Ops:
  7.2 124.3 %all-gather.2.cloned.1.call-start = ((), (), s32[]{:S(2)}) async-start(), calls=%async_computation.3 | async-start | bytes 14598144 | tf_op jit(solution)/shard_map/all_gather | solution.py:667
  11.1 229.6 %reduce-scatter.4.cloned.1.call-start = ((), (), s32[]{:S(2)}) async-start(), calls=%async_computation.4 | async-start | bytes 5898240 | tf_op jit(solution)/shard_map/reduce_scatter | solution.py:740
  12.4 15.9 %collective-permute-start.3 = (bf16[480,768]{1,0:T(8,128)(2,1)S(1)}, bf16[480,768]{1,0:T(8,128)(2,1)}, u32[]{:S(2)}, u32[]{:S(2)}) collective-permute-start(bf16[480,768]{1,0:T(8,128)(2,1)S(1)} %pad_maximum_fusion.4), channel_id=1, source_target_pairs={{4,8},{6,10},{9,5},{11,7},{12,16},{14,18},{17,13},{19,15},{20,24},... | collective-permute-start | bytes 2211848 | tf_op jit(solution)/shard_map/ppermute | solution.py:604
  28.2 23.8 %collective-permute-start.4 = (bf16[480,768]{1,0:T(8,128)(2,1)}, bf16[480,768]{1,0:T(8,128)(2,1)}, u32[]{:S(2)}, u32[]{:S(2)}) collective-permute-start(bf16[480,768]{1,0:T(8,128)(2,1)} %collective-permute-done.3), channel_id=1, source_target_pairs={{0,4},{2,6},{5,1},{7,3},{8,12},{10,14},{13,9},{15,11},{16,20},{18,... | collective-permute-start | bytes 2211848 | tf_op jit(solution)/shard_map/ppermute | solution.py:604
  53.3 21.0 %collective-permute-start.6 = (bf16[384,768]{1,0:T(8,128)(2,1)}, bf16[384,768]{1,0:T(8,128)(2,1)}, u32[]{:S(2)}, u32[]{:S(2)}) collective-permute-start(bf16[384,768]{1,0:T(8,128)(2,1)} %pad_maximum_fusion.6.w0), channel_id=1, source_target_pairs={{0,8},{1,9},{2,10},{3,11},{4,12},{5,13},{6,14},{7,15},{8,0},{9,1},... | collective-permute-start | bytes 1769480 | tf_op jit(solution)/shard_map/ppermute | solution.py:604
  56.0 18.3 %collective-permute-start.7 = (bf16[384,768]{1,0:T(8,128)(2,1)}, bf16[384,768]{1,0:T(8,128)(2,1)}, u32[]{:S(2)}, u32[]{:S(2)}) collective-permute-start(bf16[384,768]{1,0:T(8,128)(2,1)} %pad_maximum_fusion.6.w0), channel_id=1, source_target_pairs={{0,16},{1,17},{2,18},{3,19},{4,20},{5,21},{6,22},{7,23},{8,24},{9,... | collective-permute-start | bytes 1769480 | tf_op jit(solution)/shard_map/ppermute | solution.py:604
  58.6 23.0 %collective-permute-start.8 = (bf16[384,768]{1,0:T(8,128)(2,1)}, bf16[384,768]{1,0:T(8,128)(2,1)}, u32[]{:S(2)}, u32[]{:S(2)}) collective-permute-start(bf16[384,768]{1,0:T(8,128)(2,1)} %pad_maximum_fusion.6.w0), channel_id=1, source_target_pairs={{0,24},{1,25},{2,26},{3,27},{4,28},{5,29},{6,30},{7,31},{8,16},{9,... | collective-permute-start | bytes 1769480 | tf_op jit(solution)/shard_map/ppermute | solution.py:604
  60.9 45.3 %collective-permute-start.10 = (bf16[768,768]{1,0:T(8,128)(2,1)}, bf16[768,768]{1,0:T(8,128)(2,1)S(1)}, u32[]{:S(2)}, u32[]{:S(2)}) collective-permute-start(bf16[768,768]{1,0:T(8,128)(2,1)} %dynamic-slice_bitcast_fusion.own), channel_id=1, source_target_pairs={{0,4},{1,5},{2,6},{3,7},{4,0},{5,1},{6,2},{7,3},{8,12},{9,13},{10,... | collective-permute-start | bytes 3538952 | tf_op jit(solution)/shard_map/ppermute | solution.py:604
  89.9 49.5 %collective-permute-start.9 = (bf16[448,768]{1,0:T(8,128)(2,1)}, bf16[448,768]{1,0:T(8,128)(2,1)S(1)}, u32[]{:S(2)}, u32[]{:S(2)}) collective-permute-start(bf16[448,768]{1,0:T(8,128)(2,1)} %get-tuple-element.89.mine), channel_id=1, source_target_pairs={{0,4},{1,5},{2,6},{3,7},{4,0},{5,1},{6,2},{7,3},{8,12},{9,13},{10,... | collective-permute-start | bytes 2064392 | tf_op jit(solution)/shard_map/ppermute | solution.py:604
  177.2 111.7 %reduce-scatter.6.cloned.1.call-start = ((), (), s32[]{:S(2)}) async-start(), calls=%async_computation.5 | async-start | bytes 2949120 | tf_op jit(solution)/shard_map/reduce_scatter | solution.py:740
  178.5 25.8 %collective-permute-start.15 = (bf16[448,768]{1,0:T(8,128)(2,1)S(1)}, bf16[448,768]{1,0:T(8,128)(2,1)S(1)}, u32[]{:S(2)}, u32[]{:S(2)}) collective-permute-start(bf16[448,768]{1,0:T(8,128)(2,1)S(1)} %copy-done.26), channel_id=1, source_target_pairs={{0,4},{1,5},{2,6},{3,7},{4,0},{5,1},{6,2},{7,3},{8,12},{9,13},{10,... | collective-permute-start | bytes 2064392 | tf_op jit(solution)/shard_map/ppermute | solution.py:604
  240.7 99.8 %reduce-scatter.8.cloned.1.call-start = ((), (), s32[]{:S(2)}) async-start(), calls=%async_computation.6 | async-start | bytes 3072000 | tf_op jit(solution)/shard_map/reduce_scatter | solution.py:740
  247.2 16.7 %collective-permute-start.18 = (bf16[672,768]{1,0:T(8,128)(2,1)}, bf16[672,768]{1,0:T(8,128)(2,1)S(1)}, u32[]{:S(2)}, u32[]{:S(2)}) collective-permute-start(bf16[672,768]{1,0:T(8,128)(2,1)} %pad_maximum_fusion.2), channel_id=1, source_target_pairs={{1,0},{3,2},{4,5},{6,7},{9,8},{11,10},{12,13},{14,15},{17,16},{19,... | collective-permute-start | bytes 3096584 | tf_op jit(solution)/shard_map/ppermute | solution.py:604
  264.6 24.2 %collective-permute-start.23 = (bf16[768,768]{1,0:T(8,128)(2,1)S(1)}, bf16[768,768]{1,0:T(8,128)(2,1)}, u32[]{:S(2)}, u32[]{:S(2)}) collective-permute-start(bf16[768,768]{1,0:T(8,128)(2,1)S(1)} %fusion.2), channel_id=1, source_target_pairs={{0,1},{2,3},{5,4},{7,6},{8,9},{10,11},{13,12},{15,14},{16,17},{18,... | collective-permute-start | bytes 3538952 | tf_op jit(solution)/shard_map/ppermute | solution.py:604
  288.9 28.9 %collective-permute-start.20 = (bf16[768,768]{1,0:T(8,128)(2,1)S(1)}, bf16[768,768]{1,0:T(8,128)(2,1)}, u32[]{:S(2)}, u32[]{:S(2)}) collective-permute-start(bf16[768,768]{1,0:T(8,128)(2,1)S(1)} %fusion.2), channel_id=1, source_target_pairs={{0,2},{2,0},{5,7},{7,5},{8,10},{10,8},{13,15},{15,13},{16,18},{18,... | collective-permute-start | bytes 3538952 | tf_op jit(solution)/shard_map/ppermute | solution.py:604
  295.4 43.6 %collective-permute-start.24 = (bf16[192,2304]{1,0:T(8,128)(2,1)S(1)}, bf16[192,2304]{1,0:T(8,128)(2,1)S(1)}, u32[]{:S(2)}, u32[]{:S(2)}) collective-permute-start(bf16[192,2304]{1,0:T(8,128)(2,1)S(1)} %slice.278), channel_id=1, source_target_pairs={{0,1},{1,0},{2,3},{3,2},{4,5},{5,4},{6,7},{7,6},{8,9},{9,8},{10,11... | collective-permute-start | bytes 2654216 | tf_op jit(solution)/shard_map/ppermute | solution.py:604
  317.8 30.9 %collective-permute-start.27 = (bf16[768,768]{1,0:T(8,128)(2,1)}, bf16[768,768]{1,0:T(8,128)(2,1)}, u32[]{:S(2)}, u32[]{:S(2)}) collective-permute-start(bf16[768,768]{1,0:T(8,128)(2,1)} %collective-permute-done.20), channel_id=1, source_target_pairs={{0,1},{2,3},{5,4},{7,6},{8,9},{10,11},{13,12},{15,14},{16,17},{18,... | collective-permute-start | bytes 3538952 | tf_op jit(solution)/shard_map/ppermute | solution.py:604
  321.5 56.2 %collective-permute-start.22 = (bf16[512,768]{1,0:T(8,128)(2,1)}, bf16[512,768]{1,0:T(8,128)(2,1)}, u32[]{:S(2)}, u32[]{:S(2)}) collective-permute-start(bf16[512,768]{1,0:T(8,128)(2,1)} %add_dynamic-update-slice_fusion), channel_id=1, source_target_pairs={{0,2},{2,0},{5,7},{7,5},{8,10},{10,8},{13,15},{15,13},{16,18},{18,... | collective-permute-start | bytes 2359304 | tf_op jit(solution)/shard_map/ppermute | solution.py:604
  324.7 66.7 %collective-permute-start.21 = (bf16[512,768]{1,0:T(8,128)(2,1)}, bf16[512,768]{1,0:T(8,128)(2,1)}, u32[]{:S(2)}, u32[]{:S(2)}) collective-permute-start(bf16[512,768]{1,0:T(8,128)(2,1)} %add_dynamic-update-slice_fusion), channel_id=1, source_target_pairs={{0,1},{2,3},{5,4},{7,6},{8,9},{10,11},{13,12},{15,14},{16,17},{18,... | collective-permute-start | bytes 2359304 | tf_op jit(solution)/shard_map/ppermute | solution.py:604
  339.2 33.2 %collective-permute-start.30 = (bf16[192,2304]{1,0:T(8,128)(2,1)S(1)}, bf16[192,2304]{1,0:T(8,128)(2,1)S(1)}, u32[]{:S(2)}, u32[]{:S(2)}) collective-permute-start(bf16[192,2304]{1,0:T(8,128)(2,1)S(1)} %add_convert_fusion.1), channel_id=1, source_target_pairs={{2,0},{3,1},{4,6},{5,7},{10,8},{11,9},{12,14},{13,15},{18,16},{19,... | collective-permute-start | bytes 2654216 | tf_op jit(solution)/shard_map/ppermute | solution.py:604
  341.5 29.4 %collective-permute-start.25 = (bf16[208,768]{1,0:T(8,128)(2,1)S(1)}, bf16[208,768]{1,0:T(8,128)(2,1)S(1)}, u32[]{:S(2)}, u32[]{:S(2)}) collective-permute-start(bf16[208,768]{1,0:T(8,128)(2,1)S(1)} %slice.234), channel_id=1, source_target_pairs={{0,1},{1,0},{2,3},{3,2},{4,5},{5,4},{6,7},{7,6},{8,9},{9,8},{10,11... | collective-permute-start | bytes 958472 | tf_op jit(solution)/shard_map/ppermute | solution.py:604
  371.1 14.9 %collective-permute-start.32 = (bf16[192,768]{1,0:T(8,128)(2,1)S(1)}, bf16[192,768]{1,0:T(8,128)(2,1)S(1)}, u32[]{:S(2)}, u32[]{:S(2)}) collective-permute-start(bf16[192,768]{1,0:T(8,128)(2,1)S(1)} %add_convert_fusion.2), channel_id=1, source_target_pairs={{2,0},{3,1},{4,6},{5,7},{10,8},{11,9},{12,14},{13,15},{18,16},{19,... | collective-permute-start | bytes 884744 | tf_op jit(solution)/shard_map/ppermute | solution.py:604
  376.3 20.5 %collective-permute-start.31 = (f32[96,2304]{1,0:T(8,128)S(1)}, f32[96,2304]{1,0:T(8,128)S(1)}, u32[]{:S(2)}, u32[]{:S(2)}) collective-permute-start(f32[96,2304]{1,0:T(8,128)S(1)} %slice.291), channel_id=1, source_target_pairs={{0,4},{1,5},{6,2},{7,3},{8,12},{9,13},{14,10},{15,11},{16,20},{17,... | collective-permute-start | bytes 2654216 | tf_op jit(solution)/shard_map/ppermute | solution.py:604
  377.6 14.2 %collective-permute-start.26 = (bf16[512,768]{1,0:T(8,128)(2,1)}, bf16[512,768]{1,0:T(8,128)(2,1)S(1)}, u32[]{:S(2)}, u32[]{:S(2)}) collective-permute-start(bf16[512,768]{1,0:T(8,128)(2,1)} %collective-permute-done.22), channel_id=1, source_target_pairs={{0,1},{2,3},{5,4},{7,6},{8,9},{10,11},{13,12},{15,14},{16,17},{18,... | collective-permute-start | bytes 2359304 | tf_op jit(solution)/shard_map/ppermute | solution.py:604
  (50 other events, 354.9 us)
Sparse Core Ops, SparseCore 0:
  11.2 120.2 all-gather.1
  177.3 55.1 reduce-scatter.3
  240.8 38.5 reduce-scatter.5
  289.0 38.2 reduce-scatter.7

commit v3 on v2

--- a/solution.py
+++ b/solution.py
@@ -514,8 +514,7 @@
     send_grads(scalars, whole, out, sems)
 
 
-def cross_grads(scalars, norm, frames, low, att, dq, dk, dv, vectors, out, low_vectors, whole, sems):
-    low_vectors[...] = vectors[...].astype(BF16)
+def cross_grads(scalars, norm, frames, low, att, dq, dk, dv, out, whole, sems):
     cols = att.shape[1] // 2
     parts = [halves(piece, cols) for piece in (dq, dk, dv)]
     for group in range(2):
@@ -523,10 +522,11 @@
         joined = jnp.concatenate([parts[1][group], parts[2][group]], axis=1)
         found = [mm(norm[...], parts[0][group], TN), mm(frames[...], joined, TN), mm(low[...], att[:, at], TN)]
         whole[group] = jnp.concatenate(found, axis=1).astype(BF16)
-    send_grads(scalars, whole, out, sems, low_vectors)
-
-
-def self_grads(scalars, norm, low, att, dq, dk, dv, out, whole, sems):
+    send_grads(scalars, whole, out, sems)
+
+
+def self_grads(scalars, norm, low, att, dq, dk, dv, vectors, out, low_vectors, whole, sems):
+    low_vectors[...] = vectors[...].astype(BF16)
     cols = att.shape[1] // 2
     parts = [halves(piece, cols) for piece in (dq, dk, dv)]
     for group in range(2):
@@ -534,7 +534,7 @@
         joined = jnp.concatenate([part[group] for part in parts], axis=1)
         found = [mm(norm[...], joined, TN), mm(low[...], att[:, at], TN)]
         whole[group] = jnp.concatenate(found, axis=1).astype(BF16)
-    send_grads(scalars, whole, out, sems)
+    send_grads(scalars, whole, out, sems, low_vectors)
 
 
 SMEM = pl.BlockSpec(memory_space=pltpu.SMEM)
@@ -799,100 +799,96 @@
 
     edge_shape = shape((swing, width), BF16)
     slice_shapes = [shape((tok_rows, width), BF16), edge_shape, edge_shape]
+    grads_cross = grads_of(
+        cross_grads, "cross_grads", 8, width, head_scratch,
+        low_two, frame_window, low_grad_two, low_cross, cq_grad, ck_grad, cv_grad,
+    )
+    kept, given = kernel_call(
+        partial(frame_backward, relay), "frame_backward", 7,
+        (scalars, after(ck_grad, grads_cross), cv_grad, rest_w),
+        [SMEM] + [VMEM] * 2 + [ANY],
+        [shape((frame_rows, width), BF16)] * 2,
+        scratch=[pltpu.VMEM((frames, width), F32)] + head_scratch,
+    )
     out_mid, out_pair, out_cross = kernel_call(
         finish_output, "finish_output", 3,
-        (scalars, resid_two, part_three, after(other_three, grad_two), out_bias),
+        (scalars, resid_two, part_three, after(other_three, kept), out_bias),
         [SMEM] + [VMEM] * 4,
         slice_shapes,
     )
+    half_sum = (kept.astype(F32) + swap(given).astype(F32)).astype(BF16)
+    half_sum = after(half_sum, out_mid)
+    to_pair = jnp.concatenate([half_sum[near:], out_pair], axis=0)
+    to_cross = jnp.concatenate([half_sum[:near], out_cross], axis=0)
+    from_pair = move(to_pair, pair_rule)
+    from_cross = move(to_cross, cross_rule)
+    cross_total = between_back(after(grads_cross, unit_total, to_pair, to_cross))
     grad_one, low_grad_one, low_self, sq_grad, sk_grad, sv_grad, back_one, sums_one, heads_one = kernel_call(
         self_backward, "self_backward", 12,
-        (scalars, resid_one, grad_two, back_two, after(swap(back_two), out_mid), ln_gain, self_q, self_k, self_v, self_o, self_den, *self_w),
+        (scalars, resid_one, grad_two, back_two, after(swap(back_two), to_pair, to_cross), ln_gain, self_q, self_k, self_v, self_o, self_den, *self_w),
         [SMEM] + [VMEM] * 10 + [ANY] * 4,
         [wide_f32, low_shape, att_shape, head_b, head_b, head_b, low_shape, sums_shape, heads_shape],
         scratch=drop_scratch + head_scratch,
-    )
-    kept, given = kernel_call(
-        partial(frame_backward, relay), "frame_backward", 7,
-        (scalars, after(ck_grad, back_one), cv_grad, rest_w),
-        [SMEM] + [VMEM] * 2 + [ANY],
-        [shape((frame_rows, width), BF16)] * 2,
-        scratch=[pltpu.VMEM((frames, width), F32)] + head_scratch,
-    )
-    in_mid, in_pair, in_cross, vectors = kernel_call(
-        input_backward, "input_backward", 4,
-        (scalars, hidden_rows, grad_one, back_one, after(swap(back_one), kept), ln_gain, sums_one, sums_two, heads_one, heads_two, unit_sums),
-        [SMEM] + [VMEM] * 10,
-        slice_shapes + [shape((16, width), F32)],
-    )
-    grads_self = grads_of(
-        self_grads, "self_grads", 5, width, head_scratch,
-        after(low_one, in_mid), low_grad_one, low_self, sq_grad, sk_grad, sv_grad,
-    )
-    self_total = between_back(after(grads_self, unit_total))
-    half_sum = (kept.astype(F32) + swap(given).astype(F32)).astype(BF16)
-    half_sum = after(half_sum, grads_self)
-    from_pair = move(jnp.concatenate([half_sum[near:], in_pair, out_pair], axis=0), pair_rule)
-    from_cross = move(jnp.concatenate([half_sum[:near], in_cross, out_cross], axis=0), cross_rule)
-    added = vectors.shape[0]
-    grads_cross = grads_of(
-        cross_grads, "cross_grads", 8, width, [pltpu.VMEM((added, width), BF16)] + head_scratch,
-        low_two, frame_window, low_grad_two, low_cross, after(cq_grad, half_sum), ck_grad, cv_grad, vectors,
-        added=added,
     )
     extra = jnp.where(
         odd == 1,
         jnp.concatenate([from_pair[:far], from_cross[:near]], axis=0),
         jnp.concatenate([from_cross[:near], from_pair[:far]], axis=0),
     )
-    frame_block = after(half_sum + extra, grads_cross)
-    token_rows = jnp.concatenate(
-        [
-            token_block(in_mid, from_pair[far:-swing], from_cross[near:-swing]),
-            token_block(out_mid, from_pair[-swing:], from_cross[-swing:]),
-        ],
-        axis=0,
-    )
-    frame_opposite = from_main(frame_block, 2)
-    frame_beside = from_main(frame_block, 1)
+    out_rows = token_block(out_mid, from_pair[far:], from_cross[near:])
+    copies_block = after(jnp.concatenate([half_sum + extra, out_rows], axis=0), back_one)
+    copies_opposite = from_main(copies_block, 2)
+    copies_beside = from_main(copies_block, 1)
+    in_mid, in_pair, in_cross, vectors = kernel_call(
+        input_backward, "input_backward", 4,
+        (scalars, hidden_rows, grad_one, back_one, after(swap(back_one), copies_block), ln_gain, sums_one, sums_two, heads_one, heads_two, unit_sums),
+        [SMEM] + [VMEM] * 10,
+        slice_shapes + [shape((16, width), F32)],
+    )
+    in_from_pair = move(in_pair, pair_rule)
+    in_from_cross = move(in_cross, cross_rule)
+    added = vectors.shape[0]
+    grads_self = grads_of(
+        self_grads, "self_grads", 5, width, [pltpu.VMEM((added, width), BF16)] + head_scratch,
+        after(low_one, in_mid), low_grad_one, low_self, sq_grad, sk_grad, sv_grad, vectors,
+        added=added,
+    )
+    in_rows = after(token_block(in_mid, in_from_pair, in_from_cross), grads_self)
     if relay:
-        cross_total = between_back(after(grads_cross, self_total, frame_beside))
+        self_total = between_back(after(grads_self, cross_total, in_rows, copies_beside))
     else:
-        parts = grads_cross.reshape(4, -1, width)[:, : width // 2].reshape(-1, width)
-        cross_total = jnp.concatenate(
-            [between_back(parts), jnp.zeros((added, width), BF16)], axis=0
-        )
-    early = jnp.concatenate([unit_total, self_total], axis=1)
-    early_across = move(after(early[block:], frame_beside), lambda a, z: (a, z ^ 1))
+        parts = grads_self.reshape(4, -1, width)[:, : width // 2].reshape(-1, width)
+        self_total = jnp.concatenate([between_back(parts), jnp.zeros((added, width), BF16)], axis=0)
+    in_opposite = from_main(in_rows, 2)
+    in_beside = from_main(in_rows, 1)
+    early = jnp.concatenate([unit_total, cross_total], axis=1)
+    early_across = move(early[block:], lambda a, z: (a, z ^ 1))
     early_paired = (early[:block].astype(F32) + early_across.astype(F32)).astype(BF16)
-    token_rows = after(token_rows, frame_opposite)
-    frame_third = from_main(frame_opposite, 1)
-    token_opposite = from_main(token_rows, 2)
-    token_beside = from_main(token_rows, 1)
+    copies_third = from_main(copies_opposite, 1)
     early_opposite = from_opposite(early_paired)
-    cross_total = after(cross_total, early_paired)
-    cross_across = move(cross_total[block:], lambda a, z: (a, z ^ 1))
-    cross_paired = (cross_total[:block].astype(F32) + cross_across[:block].astype(F32)).astype(BF16)
+    self_total = after(self_total, early_paired)
+    self_across = move(self_total[block:], lambda a, z: (a, z ^ 1))
+    self_paired = (self_total[:block].astype(F32) + self_across[:block].astype(F32)).astype(BF16)
     if relay:
-        vectors = cross_total[2 * block :].astype(F32) + cross_across[block:].astype(F32)
+        vectors = self_total[2 * block :].astype(F32) + self_across[block:].astype(F32)
         vectors = vectors + move(vectors, lambda a, z: (a, z ^ 2))
     else:
         vectors = lax.psum(lax.psum(vectors, "narrow"), "wide", axis_index_groups=groups)
-    token_third = from_main(after(token_opposite, cross_paired), 1)
-    cross_opposite = from_opposite(cross_paired)
-    grad_early = to_owner(early_paired, after(early_opposite, cross_paired))
-    grad_unit, grad_self = grad_early[:, : 2 * hidden_units], grad_early[:, 2 * hidden_units :]
-    grad_cross = to_owner(cross_paired, cross_opposite)
+    in_third = from_main(after(in_opposite, early_paired), 1)
+    self_opposite = from_opposite(self_paired)
+    grad_early = to_owner(early_paired, after(early_opposite, self_paired))
+    grad_unit, grad_cross = grad_early[:, : 2 * hidden_units], grad_early[:, 2 * hidden_units :]
+    grad_self = to_owner(self_paired, self_opposite)
 
     def copied(first, last, value, opposite, beside, third, dtype):
         near_copy = jnp.where(main, value[first:last], beside[first:last])
         far_copy = jnp.where(main, opposite[first:last], third[first:last])
         return per_batch(near_copy, far_copy, dtype)
 
-    encoded_grad = copied(0, frame_rows, frame_block, frame_opposite, frame_beside, frame_third, F32)
-    tokens = (token_rows, token_opposite, token_beside, token_third)
-    input_grad = copied(0, tok_rows, *tokens, F32)
-    output = copied(tok_rows, 2 * tok_rows, *tokens, BF16)
+    copies = (copies_block, copies_opposite, copies_beside, copies_third)
+    encoded_grad = copied(0, frame_rows, *copies, F32)
+    output = copied(frame_rows, frame_rows + tok_rows, *copies, BF16)
+    input_grad = copied(0, tok_rows, in_rows, in_opposite, in_beside, in_third, F32)
 
     def unpacked(grad):
         stack = jnp.stack([grad[:, head_cols * k : head_cols * (k + 1)] for k in range(3)])

time: 413 us -> 402 us (0.973)
  waiting for transfers between devices: 133 us -> 128 us
    ppermute x34 -> x36, waiting for transfers between devices: 107 us -> 101 us  [move(): return lax.ppermute(value, AXES, pairs_list)]
    unnamed x79 -> x69, local copies, waits for them, and re-layouts: 12.7 us -> 9.17 us
    ppermute x34 -> x36, starting transfers between devices: 88.9 us -> 85.4 us  [move(): return lax.ppermute(value, AXES, pairs_list)]
  transfers between devices with their start and end apart: 38 -> 40, of which waited for: 17 -> 18; matrix products, arithmetic and copies ran while one was open for 9% -> 9% of each run, Pallas kernels for 20% -> 21%
where the time goes in v3:
time: 402 us; the launch traced here: 395 us
  waiting for transfers between devices  128 us (32%)
  Pallas kernels  114 us (28%)
  starting transfers between devices  85.9 us (21%)
  local copies, waits for them, and re-layouts  25.1 us (6%)
  other arithmetic  24.8 us (6%)
  between operations  17.5 us (4%)
    pallas_call x12, Pallas kernels, kernel_call(): pl.pallas_call(kernel, out_shape=tuple(outs), in_specs=list(spaces), out_...  114 us
    ppermute x36, waiting for transfers between devices, move(): return lax.ppermute(value, AXES, pairs_list)  101 us
    ppermute x36, starting transfers between devices, move(): return lax.ppermute(value, AXES, pairs_list)  85.4 us
    all_gather x1, waiting for transfers between devices, body(): rest_w = lax.all_gather(rest_piece, AXES, axis=0, tiled=True)  25.4 us
    another operation x6, other arithmetic, per_batch(): jnp.stack([jnp.where(batch == 0, near_copy, far_copy), jnp.where(batch ==...  9.82 us
    unnamed x69, local copies, waits for them, and re-layouts  9.17 us
  transfers between devices with their start and end apart: 40, of which 18 were waited for; matrix products, arithmetic and copies ran while one was open for 9% of the time, Pallas kernels for 21%

profile of v3, /device:TPU:0, one launch (start us, length us, event | category | flops | bytes accessed | tf_op | source)
XLA Modules:
  0.0 395.2 jit_solution(12976519857787521520)
XLA Ops:
  22.3 6.0 %collective-permute-start.1 = (bf16[200,768]{1,0:T(8,128)(2,1)}, bf16[200,768]{1,0:T(8,128)(2,1)}, u32[]{:S(2)}, u32[]{:S(2)}) collective-permute-start(bf16[200,768]{1,0:T(8,128)(2,1)} %maximum_maximum_fusion), channel_id=1, source_target_pairs={{0,2},{1,3},{6,4},{7,5},{8,10},{9,11},{14,12},{15,13},{16,18},{17,... | collective-permute-start | bytes 921608 | tf_op jit(solution)/shard_map/ppermute | solution.py:604
  41.9 8.3 %collective-permute-done.2 = bf16[200,768]{1,0:T(8,128)(2,1)} collective-permute-done((bf16[200,768]{1,0:T(8,128)(2,1)S(1)}, bf16[200,768]{1,0:T(8,128)(2,1)}, u32[]{:S(2)}, u32[]{:S(2)}) %collective-permute-start.2) | collective-permute-done | bytes 307232 | tf_op jit(solution)/shard_map/ppermute | solution.py:604
  60.8 6.7 %collective-permute-start.10 = (bf16[768,768]{1,0:T(8,128)(2,1)}, bf16[768,768]{1,0:T(8,128)(2,1)S(1)}, u32[]{:S(2)}, u32[]{:S(2)}) collective-permute-start(bf16[768,768]{1,0:T(8,128)(2,1)} %dynamic-slice_bitcast_fusion.own), channel_id=1, source_target_pairs={{0,4},{1,5},{2,6},{3,7},{4,0},{5,1},{6,2},{7,3},{8,12},{9,13},{10,... | collective-permute-start | bytes 3538952 | tf_op jit(solution)/shard_map/ppermute | solution.py:604
  74.3 7.3 %collective-permute-done.8.w3 = bf16[384,768]{1,0:T(8,128)(2,1)} collective-permute-done((bf16[384,768]{1,0:T(8,128)(2,1)}, bf16[384,768]{1,0:T(8,128)(2,1)}, u32[]{:S(2)}, u32[]{:S(2)}) %collective-permute-start.8) | collective-permute-done | bytes 589856 | tf_op jit(solution)/shard_map/ppermute | solution.py:604
  81.6 8.3 %self_forward.1 = (bf16[448,768]{1,0:T(8,128)(2,1)}, bf16[448,768]{1,0:T(8,128)(2,1)}, bf16[3,448,128]{2,1,0:T(8,128)(2,1)}, bf16[3,448,128]{2,1,0:T(8,128)(2,1)...) custom-call(s32[8]{0:T(128)} %stack.107.scalars, ...), custom_call_target="tpu_custom_call" | custom-call | flops 8000000000 | bytes 1048576 | tf_op jit(solution)/shard_map/self_forward/pallas_call | solution.py:550
  89.9 15.4 %collective-permute-start.9 = (bf16[448,768]{1,0:T(8,128)(2,1)}, bf16[448,768]{1,0:T(8,128)(2,1)S(1)}, u32[]{:S(2)}, u32[]{:S(2)}) collective-permute-start(bf16[448,768]{1,0:T(8,128)(2,1)} %get-tuple-element.87.mine), channel_id=1, source_target_pairs={{0,4},{1,5},{2,6},{3,7},{4,0},{5,1},{6,2},{7,3},{8,12},{9,13},{10,... | collective-permute-start | bytes 2064392 | tf_op jit(solution)/shard_map/ppermute | solution.py:604
  106.1 25.4 %all-gather.2.cloned.1.call-done.w0 = bf16[3072,2304]{1,0:T(8,128)(2,1)} async-done(((bf16[96,2304]{1,0:T(8,128)(2,1)}), bf16[3072,2304]{1,0:T(8,128)(2,1)}) %all-gather.2.cloned.1.call-update) | async-done | bytes 14155792 | tf_op jit(solution)/shard_map/all_gather | solution.py:667
  131.5 7.9 %frame_project.1 = (bf16[1536,768]{1,0:T(8,128)(2,1)}, bf16[3,1536,128]{2,1,0:T(8,128)(2,1)}, bf16[3,1536,128]{2,1,0:T(8,128)(2,1)}) custom-call(s32[8]{0:T(128)} %stack.107.scalars, bf16[768,768]{1,0:T(8,128)(2,1)} %dynamic-slice_bitcast_fusion.own, bf16[768,768]{1,0:T(8,128)(2,1)} %copy-done.22, bf16[288,768]{1,0:T(8,128)(2,1)} %slice.259.halo, ...), custom_call_target="tpu_custom_call" | custom-call | flops 7000000000 | bytes 1048576 | tf_op jit(solution)/shard_map/frame_project/pallas_call | solution.py:550
  140.2 11.5 %cross_forward.1 = (f32[448,768]{1,0:T(8,128)}, bf16[448,768]{1,0:T(8,128)(2,1)}, bf16[3,448,128]{2,1,0:T(8,128)(2,1)}, f32[3,448,128]{2,1,0:T(8,128)}, f32[3,44...) custom-call(s32[8]{0:T(128)} %stack.107.scalars, bf16[448,768]{1,0:T(8,128)(2,1)} %get-tuple-element.86.hidden, ...), custom_call_target="tpu_custom_call" | custom-call | flops 11000000512 | bytes 1048576 | tf_op jit(solution)/shard_map/cross_forward/pallas_call | solution.py:550
  155.5 14.3 %unit_forward.1 = (f32[448,768]{1,0:T(8,128)}, bf16[448,768]{1,0:T(8,128)(2,1)}, bf16[448,768]{1,0:T(8,128)(2,1)}, bf16[448,1536]{1,0:T(8,128)(2,1)}, bf16[448,1...) custom-call(s32[8]{0:T(128)} %stack.107.scalars, ...), custom_call_target="tpu_custom_call" | custom-call | flops 14000000000 | bytes 1048576 | tf_op jit(solution)/shard_map/unit_forward/pallas_call | solution.py:550
  169.8 7.2 %unit_grads.1 = bf16[1536,1536]{1,0:T(8,128)(2,1)} custom-call(s32[8]{0:T(128)} %stack.107.scalars, bf16[448,768]{1,0:T(8,128)(2,1)} %get-tuple-element.98.norm, bf16[448,1536]{1,0:T(8,128)(2,1)} %get-tuple-element.99.pre, bf16[448,768]{1,0:T(8,128)(2,1)} %get-tuple-element.96.top.cotangent, bf16[448,1536]{1,0:T(8,128)(2,1)} %get-tuple-element.100.act), custom_call_target="tpu_custom_call" | custom-call | flops 8999999488 | bytes 1048576 | tf_op jit(solution)/shard_map/unit_grads/pallas_call | solution.py:550
  181.2 23.0 %cross_backward.1 = (f32[448,768]{1,0:T(8,128)}, bf16[448,768]{1,0:T(8,128)(2,1)}, bf16[448,384]{1,0:T(8,128)(2,1)}, bf16[3,448,128]{2,1,0:T(8,128)(2,1)}, bf16[...) custom-call(s32[8]{0:T(128)} %stack.107.scalars, ...), custom_call_target="tpu_custom_call" | custom-call | flops 20999999488 | bytes 1048576 | tf_op jit(solution)/shard_map/cross_backward/pallas_call | solution.py:550
  204.2 8.5 %cross_grads.1 = bf16[1536,768]{1,0:T(8,128)(2,1)} custom-call(s32[8]{0:T(128)} %stack.107.scalars, bf16[448,768]{1,0:T(8,128)(2,1)} %get-tuple-element.106.norm, bf16[1536,768]{1,0:T(8,128)(2,1)} %get-tuple-element.107.frames, bf16[448,768]{1,0:T(8,128)(2,1)} %get-tuple-element.108.low, bf16[448,384]{1,0:T(8,128)(2,1)} %get-tuple-element.109.att, ...), custom_call_target="tpu_custom_call" | custom-call | flops 8000000000 | bytes 1048576 | tf_op jit(solution)/shard_map/cross_grads/pallas_call | solution.py:550
  212.7 8.9 %frame_backward.1 = (bf16[768,768]{1,0:T(8,128)(2,1)}, bf16[768,768]{1,0:T(8,128)(2,1)}) custom-call(s32[8]{0:T(128)} %stack.107.scalars, bf16[3,1536,128]{2,1,0:T(8,128)(2,1)} %get-tuple-element.112.dk.dk_all, bf16[3,1536,128]{2,1,0:T(8,128)(2,1)} %get-tuple-element.111.dv.dv_all, bf16[3072,2304]{1,0:T(8,128)(2,1)} %all-gather.2.cloned.1.call-done.w0), custom_call_target="tpu_custom_call" | custom-call | flops 7000000000 | bytes 1048576 | tf_op jit(solution)/shard_map/frame_backward/pallas_call | solution.py:550
  235.0 12.0 %self_backward.1 = (f32[448,768]{1,0:T(8,128)}, bf16[448,768]{1,0:T(8,128)(2,1)}, bf16[448,384]{1,0:T(8,128)(2,1)}, bf16[3,448,128]{2,1,0:T(8,128)(2,1)}, bf16[3...) custom-call(s32[8]{0:T(128)} %stack.107.scalars, ...), custom_call_target="tpu_custom_call" | custom-call | flops 12000000000 | bytes 1048576 | tf_op jit(solution)/shard_map/self_backward/pallas_call | solution.py:550
  250.1 6.2 %collective-permute-start.19 = (bf16[1024,768]{1,0:T(8,128)(2,1)S(1)}, bf16[1024,768]{1,0:T(8,128)(2,1)S(1)}, u32[]{:S(2)}, u32[]{:S(2)}) collective-permute-start(bf16[1024,768]{1,0:T(8,128)(2,1)S(1)} %pad_maximum_fusion.1), channel_id=1, source_target_pairs={{0,1},{2,3},{5,4},{7,6},{8,9},{10,11},{13,12},{15,14},{16,17},{18,... | collective-permute-start | bytes 4718600 | tf_op jit(solution)/shard_map/ppermute | solution.py:604
  268.1 5.7 %self_grads.1 = bf16[1600,768]{1,0:T(8,128)(2,1)} custom-call(s32[8]{0:T(128)} %stack.107.scalars, bf16[448,768]{1,0:T(8,128)(2,1)} %get-tuple-element.142.norm, bf16[448,768]{1,0:T(8,128)(2,1)} %get-tuple-element.143.low, bf16[448,384]{1,0:T(8,128)(2,1)} %get-tuple-element.144.att, bf16[3,448,128]{2,1,0:T(8,128)(2,1)} %get-tuple-element.145.dq, ...), custom_call_target="tpu_custom_call" | custom-call | flops 5000000000 | bytes 1048576 | tf_op jit(solution)/shard_map/self_grads/pallas_call | solution.py:550
  273.8 9.2 %collective-permute-done.23 = bf16[96,768]{1,0:T(8,128)(2,1)} collective-permute-done((bf16[96,768]{1,0:T(8,128)(2,1)}, bf16[96,768]{1,0:T(8,128)(2,1)}, u32[]{:S(2)}, u32[]{:S(2)}) %collective-permute-start.23) | collective-permute-done | bytes 147488 | tf_op jit(solution)/shard_map/ppermute | solution.py:604
  284.8 7.8 %collective-permute-done.20 = bf16[1024,768]{1,0:T(8,128)(2,1)} collective-permute-done((bf16[1024,768]{1,0:T(8,128)(2,1)S(1)}, bf16[1024,768]{1,0:T(8,128)(2,1)}, u32[]{:S(2)}, u32[]{:S(2)}) %collective-permute-start.20) | collective-permute-done | bytes 1572896 | tf_op jit(solution)/shard_map/ppermute | solution.py:604
  297.5 6.6 %collective-permute-start.26 = (bf16[256,768]{1,0:T(8,128)(2,1)}, bf16[256,768]{1,0:T(8,128)(2,1)}, u32[]{:S(2)}, u32[]{:S(2)}) collective-permute-start(bf16[256,768]{1,0:T(8,128)(2,1)} %pad_maximum_fusion.8), channel_id=1, source_target_pairs={{0,2},{2,0},{5,7},{7,5},{8,10},{10,8},{13,15},{15,13},{16,18},{18,... | collective-permute-start | bytes 1179656 | tf_op jit(solution)/shard_map/ppermute | solution.py:604
  306.2 14.0 %collective-permute-done.21 = bf16[1024,768]{1,0:T(8,128)(2,1)} collective-permute-done((bf16[1024,768]{1,0:T(8,128)(2,1)}, bf16[1024,768]{1,0:T(8,128)(2,1)}, u32[]{:S(2)}, u32[]{:S(2)}) %collective-permute-start.21) | collective-permute-done | bytes 1572896 | tf_op jit(solution)/shard_map/ppermute | solution.py:604
  322.8 8.3 %collective-permute-done.27 = bf16[192,2304]{1,0:T(8,128)(2,1)} collective-permute-done((bf16[192,2304]{1,0:T(8,128)(2,1)}, bf16[192,2304]{1,0:T(8,128)(2,1)}, u32[]{:S(2)}, u32[]{:S(2)}) %collective-permute-start.27) | collective-permute-done | bytes 884768 | tf_op jit(solution)/shard_map/ppermute | solution.py:604
  347.5 10.8 %collective-permute-done.29 = bf16[208,768]{1,0:T(8,128)(2,1)S(1)} collective-permute-done((bf16[208,768]{1,0:T(8,128)(2,1)S(1)}, bf16[208,768]{1,0:T(8,128)(2,1)S(1)}, u32[]{:S(2)}, u32[]{:S(2)}) %collective-permute-start.29) | collective-permute-done | bytes 319520 | tf_op jit(solution)/shard_map/ppermute | solution.py:604
  359.8 14.8 %collective-permute-done.34 = bf16[192,2304]{1,0:T(8,128)(2,1)S(1)} collective-permute-done((bf16[192,2304]{1,0:T(8,128)(2,1)}, bf16[192,2304]{1,0:T(8,128)(2,1)S(1)}, u32[]{:S(2)}, u32[]{:S(2)}) %collective-permute-start.34) | collective-permute-done | bytes 884768 | tf_op jit(solution)/shard_map/ppermute | solution.py:604
  (217 shorter events, 123.5 us)
Async XLA Ops:
  7.2 124.3 %all-gather.2.cloned.1.call-start = ((), (), s32[]{:S(2)}) async-start(), calls=%async_computation.3 | async-start | bytes 14598144 | tf_op jit(solution)/shard_map/all_gather | solution.py:667
  11.1 221.3 %reduce-scatter.4.cloned.1.call-start = ((), (), s32[]{:S(2)}) async-start(), calls=%async_computation.4 | async-start | bytes 5898240 | tf_op jit(solution)/shard_map/reduce_scatter | solution.py:740
  12.3 15.9 %collective-permute-start.3 = (bf16[480,768]{1,0:T(8,128)(2,1)S(1)}, bf16[480,768]{1,0:T(8,128)(2,1)}, u32[]{:S(2)}, u32[]{:S(2)}) collective-permute-start(bf16[480,768]{1,0:T(8,128)(2,1)S(1)} %pad_maximum_fusion.5), channel_id=1, source_target_pairs={{4,8},{6,10},{9,5},{11,7},{12,16},{14,18},{17,13},{19,15},{20,24},... | collective-permute-start | bytes 2211848 | tf_op jit(solution)/shard_map/ppermute | solution.py:604
  28.2 23.8 %collective-permute-start.4 = (bf16[480,768]{1,0:T(8,128)(2,1)}, bf16[480,768]{1,0:T(8,128)(2,1)}, u32[]{:S(2)}, u32[]{:S(2)}) collective-permute-start(bf16[480,768]{1,0:T(8,128)(2,1)} %collective-permute-done.3), channel_id=1, source_target_pairs={{0,4},{2,6},{5,1},{7,3},{8,12},{10,14},{13,9},{15,11},{16,20},{18,... | collective-permute-start | bytes 2211848 | tf_op jit(solution)/shard_map/ppermute | solution.py:604
  36.5 13.7 %collective-permute-start.2 = (bf16[200,768]{1,0:T(8,128)(2,1)S(1)}, bf16[200,768]{1,0:T(8,128)(2,1)}, u32[]{:S(2)}, u32[]{:S(2)}) collective-permute-start(bf16[200,768]{1,0:T(8,128)(2,1)S(1)} %broadcast_select_fusion.3), channel_id=1, source_target_pairs={{0,1},{1,0},{2,3},{3,2},{4,5},{5,4},{6,7},{7,6},{8,9},{9,8},{10,11... | collective-permute-start | bytes 921608 | tf_op jit(solution)/shard_map/ppermute | solution.py:604
  53.3 21.0 %collective-permute-start.6 = (bf16[384,768]{1,0:T(8,128)(2,1)}, bf16[384,768]{1,0:T(8,128)(2,1)}, u32[]{:S(2)}, u32[]{:S(2)}) collective-permute-start(bf16[384,768]{1,0:T(8,128)(2,1)} %pad_maximum_fusion.6.w0), channel_id=1, source_target_pairs={{0,8},{1,9},{2,10},{3,11},{4,12},{5,13},{6,14},{7,15},{8,0},{9,1},... | collective-permute-start | bytes 1769480 | tf_op jit(solution)/shard_map/ppermute | solution.py:604
  56.0 18.3 %collective-permute-start.7 = (bf16[384,768]{1,0:T(8,128)(2,1)}, bf16[384,768]{1,0:T(8,128)(2,1)}, u32[]{:S(2)}, u32[]{:S(2)}) collective-permute-start(bf16[384,768]{1,0:T(8,128)(2,1)} %pad_maximum_fusion.6.w0), channel_id=1, source_target_pairs={{0,16},{1,17},{2,18},{3,19},{4,20},{5,21},{6,22},{7,23},{8,24},{9,... | collective-permute-start | bytes 1769480 | tf_op jit(solution)/shard_map/ppermute | solution.py:604
  58.6 23.0 %collective-permute-start.8 = (bf16[384,768]{1,0:T(8,128)(2,1)}, bf16[384,768]{1,0:T(8,128)(2,1)}, u32[]{:S(2)}, u32[]{:S(2)}) collective-permute-start(bf16[384,768]{1,0:T(8,128)(2,1)} %pad_maximum_fusion.6.w0), channel_id=1, source_target_pairs={{0,24},{1,25},{2,26},{3,27},{4,28},{5,29},{6,30},{7,31},{8,16},{9,... | collective-permute-start | bytes 1769480 | tf_op jit(solution)/shard_map/ppermute | solution.py:604
  60.8 45.2 %collective-permute-start.10 = (bf16[768,768]{1,0:T(8,128)(2,1)}, bf16[768,768]{1,0:T(8,128)(2,1)S(1)}, u32[]{:S(2)}, u32[]{:S(2)}) collective-permute-start(bf16[768,768]{1,0:T(8,128)(2,1)} %dynamic-slice_bitcast_fusion.own), channel_id=1, source_target_pairs={{0,4},{1,5},{2,6},{3,7},{4,0},{5,1},{6,2},{7,3},{8,12},{9,13},{10,... | collective-permute-start | bytes 3538952 | tf_op jit(solution)/shard_map/ppermute | solution.py:604
  89.9 49.5 %collective-permute-start.9 = (bf16[448,768]{1,0:T(8,128)(2,1)}, bf16[448,768]{1,0:T(8,128)(2,1)S(1)}, u32[]{:S(2)}, u32[]{:S(2)}) collective-permute-start(bf16[448,768]{1,0:T(8,128)(2,1)} %get-tuple-element.87.mine), channel_id=1, source_target_pairs={{0,4},{1,5},{2,6},{3,7},{4,0},{5,1},{6,2},{7,3},{8,12},{9,13},{10,... | collective-permute-start | bytes 2064392 | tf_op jit(solution)/shard_map/ppermute | solution.py:604
  177.1 107.7 %reduce-scatter.6.cloned.1.call-start = ((), (), s32[]{:S(2)}) async-start(), calls=%async_computation.5 | async-start | bytes 2949120 | tf_op jit(solution)/shard_map/reduce_scatter | solution.py:740
  232.4 111.5 %reduce-scatter.8.cloned.1.call-start = ((), (), s32[]{:S(2)}) async-start(), calls=%async_computation.6 | async-start | bytes 3072000 | tf_op jit(solution)/shard_map/reduce_scatter | solution.py:740
  232.6 16.7 %collective-permute-start.16 = (bf16[576,768]{1,0:T(8,128)(2,1)S(1)}, bf16[576,768]{1,0:T(8,128)(2,1)S(1)}, u32[]{:S(2)}, u32[]{:S(2)}) collective-permute-start(bf16[576,768]{1,0:T(8,128)(2,1)S(1)} %pad_maximum_fusion.3), channel_id=1, source_target_pairs={{1,0},{3,2},{4,5},{6,7},{9,8},{11,10},{12,13},{14,15},{17,16},{19,... | collective-permute-start | bytes 2654216 | tf_op jit(solution)/shard_map/ppermute | solution.py:604
  233.9 15.3 %collective-permute-start.17 = (bf16[384,768]{1,0:T(8,128)(2,1)S(1)}, bf16[384,768]{1,0:T(8,128)(2,1)S(1)}, u32[]{:S(2)}, u32[]{:S(2)}) collective-permute-start(bf16[384,768]{1,0:T(8,128)(2,1)S(1)} %pad_maximum_fusion.7), channel_id=1, source_target_pairs={{1,8},{3,10},{9,16},{11,18},{12,5},{14,7},{17,24},{19,26},{20,13},... | collective-permute-start | bytes 1769480 | tf_op jit(solution)/shard_map/ppermute | solution.py:604
  250.1 34.6 %collective-permute-start.19 = (bf16[1024,768]{1,0:T(8,128)(2,1)S(1)}, bf16[1024,768]{1,0:T(8,128)(2,1)S(1)}, u32[]{:S(2)}, u32[]{:S(2)}) collective-permute-start(bf16[1024,768]{1,0:T(8,128)(2,1)S(1)} %pad_maximum_fusion.1), channel_id=1, source_target_pairs={{0,1},{2,3},{5,4},{7,6},{8,9},{10,11},{13,12},{15,14},{16,17},{18,... | collective-permute-start | bytes 4718600 | tf_op jit(solution)/shard_map/ppermute | solution.py:604
  256.4 36.3 %collective-permute-start.20 = (bf16[1024,768]{1,0:T(8,128)(2,1)S(1)}, bf16[1024,768]{1,0:T(8,128)(2,1)}, u32[]{:S(2)}, u32[]{:S(2)}) collective-permute-start(bf16[1024,768]{1,0:T(8,128)(2,1)S(1)} %pad_maximum_fusion.1), channel_id=1, source_target_pairs={{0,2},{2,0},{5,7},{7,5},{8,10},{10,8},{13,15},{15,13},{16,18},{18,... | collective-permute-start | bytes 4718600 | tf_op jit(solution)/shard_map/ppermute | solution.py:604
  265.5 17.5 %collective-permute-start.23 = (bf16[96,768]{1,0:T(8,128)(2,1)}, bf16[96,768]{1,0:T(8,128)(2,1)}, u32[]{:S(2)}, u32[]{:S(2)}) collective-permute-start(bf16[96,768]{1,0:T(8,128)(2,1)} %get-tuple-element.139), channel_id=1, source_target_pairs={{1,0},{3,2},{4,5},{6,7},{9,8},{11,10},{12,13},{14,15},{17,16},{19,... | collective-permute-start | bytes 442376 | tf_op jit(solution)/shard_map/ppermute | solution.py:604
  266.8 16.2 %collective-permute-start.24 = (bf16[96,768]{1,0:T(8,128)(2,1)}, bf16[96,768]{1,0:T(8,128)(2,1)}, u32[]{:S(2)}, u32[]{:S(2)}) collective-permute-start(bf16[96,768]{1,0:T(8,128)(2,1)} %get-tuple-element.140), channel_id=1, source_target_pairs={{1,8},{3,10},{9,16},{11,18},{12,5},{14,7},{17,24},{19,26},{20,13},... | collective-permute-start | bytes 442376 | tf_op jit(solution)/shard_map/ppermute | solution.py:604
  292.7 27.6 %collective-permute-start.21 = (bf16[1024,768]{1,0:T(8,128)(2,1)}, bf16[1024,768]{1,0:T(8,128)(2,1)}, u32[]{:S(2)}, u32[]{:S(2)}) collective-permute-start(bf16[1024,768]{1,0:T(8,128)(2,1)} %collective-permute-done.20), channel_id=1, source_target_pairs={{0,1},{2,3},{5,4},{7,6},{8,9},{10,11},{13,12},{15,14},{16,17},{18,... | collective-permute-start | bytes 4718600 | tf_op jit(solution)/shard_map/ppermute | solution.py:604
  297.5 33.6 %collective-permute-start.27 = (bf16[192,2304]{1,0:T(8,128)(2,1)}, bf16[192,2304]{1,0:T(8,128)(2,1)}, u32[]{:S(2)}, u32[]{:S(2)}) collective-permute-start(bf16[192,2304]{1,0:T(8,128)(2,1)} %slice.269), channel_id=1, source_target_pairs={{0,1},{1,0},{2,3},{3,2},{4,5},{5,4},{6,7},{7,6},{8,9},{9,8},{10,11... | collective-permute-start | bytes 2654216 | tf_op jit(solution)/shard_map/ppermute | solution.py:604
  297.5 37.8 %collective-permute-start.26 = (bf16[256,768]{1,0:T(8,128)(2,1)}, bf16[256,768]{1,0:T(8,128)(2,1)}, u32[]{:S(2)}, u32[]{:S(2)}) collective-permute-start(bf16[256,768]{1,0:T(8,128)(2,1)} %pad_maximum_fusion.8), channel_id=1, source_target_pairs={{0,2},{2,0},{5,7},{7,5},{8,10},{10,8},{13,15},{15,13},{16,18},{18,... | collective-permute-start | bytes 1179656 | tf_op jit(solution)/shard_map/ppermute | solution.py:604
  304.2 40.9 %collective-permute-start.25 = (bf16[256,768]{1,0:T(8,128)(2,1)}, bf16[256,768]{1,0:T(8,128)(2,1)}, u32[]{:S(2)}, u32[]{:S(2)}) collective-permute-start(bf16[256,768]{1,0:T(8,128)(2,1)} %pad_maximum_fusion.8), channel_id=1, source_target_pairs={{0,1},{2,3},{5,4},{7,6},{8,9},{10,11},{13,12},{15,14},{16,17},{18,... | collective-permute-start | bytes 1179656 | tf_op jit(solution)/shard_map/ppermute | solution.py:604
  340.2 34.4 %collective-permute-start.34 = (bf16[192,2304]{1,0:T(8,128)(2,1)}, bf16[192,2304]{1,0:T(8,128)(2,1)S(1)}, u32[]{:S(2)}, u32[]{:S(2)}) collective-permute-start(bf16[192,2304]{1,0:T(8,128)(2,1)} %add_convert_fusion.1), channel_id=1, source_target_pairs={{2,0},{3,1},{4,6},{5,7},{10,8},{11,9},{12,14},{13,15},{18,16},{19,... | collective-permute-start | bytes 2654216 | tf_op jit(solution)/shard_map/ppermute | solution.py:604
  358.5 21.9 %collective-permute-start.32 = (bf16[192,768]{1,0:T(8,128)(2,1)S(1)}, bf16[192,768]{1,0:T(8,128)(2,1)S(1)}, u32[]{:S(2)}, u32[]{:S(2)}) collective-permute-start(bf16[192,768]{1,0:T(8,128)(2,1)S(1)} %add_convert_fusion.2), channel_id=1, source_target_pairs={{2,0},{3,1},{4,6},{5,7},{10,8},{11,9},{12,14},{13,15},{18,16},{19,... | collective-permute-start | bytes 884744 | tf_op jit(solution)/shard_map/ppermute | solution.py:604
  (48 other events, 311.6 us)
Sparse Core Ops, SparseCore 0:
  11.2 120.2 all-gather.1
  177.2 55.1 reduce-scatter.3
  235.5 43.6 reduce-scatter.5
  284.9 49.3 reduce-scatter.7

commit v4 on v3

--- a/solution.py
+++ b/solution.py
@@ -230,7 +230,7 @@
     part_out[...] = out_product(o_out, whole, cols).astype(BF16)
 
 
-CHUNK = 256
+CHUNK = 768
 
 
 def unit_forward(
@@ -449,14 +449,23 @@
     frames = dk_all.shape[1]
     near = (frames - size) * 3 // 8
     far = frames - size - near
-    keys = halves(dk_all, cols)
-    values = halves(dv_all, cols)
+    step = frames // 2
     for copy in copies:
         copy.wait()
-    for group in range(2):
-        joined = jnp.concatenate([keys[group], values[group]], axis=1)
-        part = mm(joined, whole[group, :, cols : 3 * cols], NT)
-        total[...] = part if group == 0 else total[...] + part
+
+    def one_part(j, carry):
+        at = pl.ds(pl.multiple_of(j * step, step), step)
+        keys = jnp.concatenate([dk_all[p, at, :] for p in range(pairs)], axis=1)
+        values = jnp.concatenate([dv_all[p, at, :] for p in range(pairs)], axis=1)
+        part = jnp.zeros((step, total.shape[1]), F32)
+        for group in range(2):
+            cut = slice(group * cols, (group + 1) * cols)
+            joined = jnp.concatenate([keys[:, cut], values[:, cut]], axis=1)
+            part = part + mm(joined, whole[group, :, cols : 3 * cols], NT)
+        total[at, :] = part
+        return carry
+
+    lax.fori_loop(0, 2, one_part, 0)
     odd = scalars[6]
     main = scalars[7] == 1
     lead = pl.multiple_of(jnp.where(odd == 0, near, far), 32)
@@ -507,33 +516,42 @@
 
 def unit_grads(scalars, norm, pre, top, act, out, whole, sems):
     units = pre.shape[1] // 2
+    found = mm(norm[...], pre[...], TN).astype(BF16)
     for group in range(2):
-        at = slice(group * units, (group + 1) * units)
-        whole[group, :, :units] = mm(norm[...], pre[:, at], TN).astype(BF16)
-        whole[group, :, units:] = mm(top[...], act[:, at], TN).astype(BF16)
+        whole[group, :, :units] = found[:, group * units : (group + 1) * units]
+    found = mm(top[...], act[...], TN).astype(BF16)
+    for group in range(2):
+        whole[group, :, units:] = found[:, group * units : (group + 1) * units]
     send_grads(scalars, whole, out, sems)
 
 
+def all_heads(refs):
+    return jnp.concatenate([refs[p] for p in range(refs.shape[0])], axis=1)
+
+
+def by_groups(found, whole):
+    for group in range(2):
+        parts = []
+        for piece in found:
+            size = piece.shape[1] // 2
+            parts.append(piece[:, group * size : (group + 1) * size])
+        whole[group] = jnp.concatenate(parts, axis=1).astype(BF16)
+
+
 def cross_grads(scalars, norm, frames, low, att, dq, dk, dv, out, whole, sems):
-    cols = att.shape[1] // 2
-    parts = [halves(piece, cols) for piece in (dq, dk, dv)]
-    for group in range(2):
-        at = slice(group * cols, (group + 1) * cols)
-        joined = jnp.concatenate([parts[1][group], parts[2][group]], axis=1)
-        found = [mm(norm[...], parts[0][group], TN), mm(frames[...], joined, TN), mm(low[...], att[:, at], TN)]
-        whole[group] = jnp.concatenate(found, axis=1).astype(BF16)
+    cols = att.shape[1]
+    pair = mm(frames[...], jnp.concatenate([all_heads(dk), all_heads(dv)], axis=1), TN)
+    found = [mm(norm[...], all_heads(dq), TN), pair[:, :cols], pair[:, cols:], mm(low[...], att[...], TN)]
+    by_groups(found, whole)
     send_grads(scalars, whole, out, sems)
 
 
 def self_grads(scalars, norm, low, att, dq, dk, dv, vectors, out, low_vectors, whole, sems):
     low_vectors[...] = vectors[...].astype(BF16)
-    cols = att.shape[1] // 2
-    parts = [halves(piece, cols) for piece in (dq, dk, dv)]
-    for group in range(2):
-        at = slice(group * cols, (group + 1) * cols)
-        joined = jnp.concatenate([part[group] for part in parts], axis=1)
-        found = [mm(norm[...], joined, TN), mm(low[...], att[:, at], TN)]
-        whole[group] = jnp.concatenate(found, axis=1).astype(BF16)
+    cols = att.shape[1]
+    three = mm(norm[...], jnp.concatenate([all_heads(dq), all_heads(dk), all_heads(dv)], axis=1), TN)
+    found = [three[:, :cols], three[:, cols : 2 * cols], three[:, 2 * cols :], mm(low[...], att[...], TN)]
+    by_groups(found, whole)
     send_grads(scalars, whole, out, sems, low_vectors)
 
 
@@ -554,7 +572,7 @@
         out_specs=tuple(out_spaces or [VMEM] * len(outs)),
         scratch_shapes=list(scratch),
         compiler_params=pltpu.CompilerParams(vmem_limit_bytes=56 * 1024 * 1024),
-        cost_estimate=pl.CostEstimate(flops=int(cost * 1e9), transcendentals=0, bytes_accessed=1 << 20),
+        cost_estimate=pl.CostEstimate(flops=int(cost * 2e9), transcendentals=0, bytes_accessed=1 << 20),
         name=name,
     )(*operands)
 

time: 402 us -> 395 us (0.983)
    pallas_call x12, Pallas kernels: 114 us -> 110 us  [kernel_call(): pl.pallas_call(kernel, out_shape=tuple(outs), in_specs=list(spaces), out_...]
    unnamed x69 -> x65, local copies, waits for them, and re-layouts: 9.17 us -> 7.81 us
  transfers between devices with their start and end apart: 40 -> 40, of which waited for: 18 -> 16; matrix products, arithmetic and copies ran while one was open for 9% -> 10% of each run, Pallas kernels for 21% -> 20%
where the time goes in v4:
time: 395 us; the launch traced here: 388 us
  waiting for transfers between devices  128 us (32%)
  Pallas kernels  110 us (28%)
  starting transfers between devices  82.1 us (21%)
  other arithmetic  25.6 us (6%)
  local copies, waits for them, and re-layouts  25.5 us (6%)
  between operations  17.4 us (4%)
    pallas_call x12, Pallas kernels, kernel_call(): pl.pallas_call(kernel, out_shape=tuple(outs), in_specs=list(spaces), out_...  110 us
    ppermute x36, waiting for transfers between devices, move(): return lax.ppermute(value, AXES, pairs_list)  96.9 us
    ppermute x36, starting transfers between devices, move(): return lax.ppermute(value, AXES, pairs_list)  81.5 us
    all_gather x1, waiting for transfers between devices, body(): rest_w = lax.all_gather(rest_piece, AXES, axis=0, tiled=True)  26.3 us
    another operation x6, other arithmetic, per_batch(): jnp.stack([jnp.where(batch == 0, near_copy, far_copy), jnp.where(batch ==...  9.82 us
  transfers between devices with their start and end apart: 40, of which 16 were waited for; matrix products, arithmetic and copies ran while one was open for 10% of the time, Pallas kernels for 20%

profile of v4, /device:TPU:0, one launch (start us, length us, event | category | flops | bytes accessed | tf_op | source)
XLA Modules:
  0.0 388.3 jit_solution(9071992718890545289)
XLA Ops:
  22.2 6.0 %collective-permute-start.1 = (bf16[200,768]{1,0:T(8,128)(2,1)}, bf16[200,768]{1,0:T(8,128)(2,1)}, u32[]{:S(2)}, u32[]{:S(2)}) collective-permute-start(bf16[200,768]{1,0:T(8,128)(2,1)} %maximum_maximum_fusion), channel_id=1, source_target_pairs={{0,2},{1,3},{6,4},{7,5},{8,10},{9,11},{14,12},{15,13},{16,18},{17,... | collective-permute-start | bytes 921608 | tf_op jit(solution)/shard_map/ppermute | solution.py:622
  36.4 5.4 %collective-permute-start.2 = (bf16[200,768]{1,0:T(8,128)(2,1)S(1)}, bf16[200,768]{1,0:T(8,128)(2,1)}, u32[]{:S(2)}, u32[]{:S(2)}) collective-permute-start(bf16[200,768]{1,0:T(8,128)(2,1)S(1)} %broadcast_select_fusion.3), channel_id=1, source_target_pairs={{0,1},{1,0},{2,3},{3,2},{4,5},{5,4},{6,7},{7,6},{8,9},{9,8},{10,11... | collective-permute-start | bytes 921608 | tf_op jit(solution)/shard_map/ppermute | solution.py:622
  41.9 8.3 %collective-permute-done.2 = bf16[200,768]{1,0:T(8,128)(2,1)} collective-permute-done((bf16[200,768]{1,0:T(8,128)(2,1)S(1)}, bf16[200,768]{1,0:T(8,128)(2,1)}, u32[]{:S(2)}, u32[]{:S(2)}) %collective-permute-start.2) | collective-permute-done | bytes 307232 | tf_op jit(solution)/shard_map/ppermute | solution.py:622
  60.5 6.7 %collective-permute-start.5 = (bf16[256,768]{1,0:T(8,128)(2,1)}, bf16[256,768]{1,0:T(8,128)(2,1)}, u32[]{:S(2)}, u32[]{:S(2)}) collective-permute-start(bf16[256,768]{1,0:T(8,128)(2,1)} %dynamic-slice_bitcast_fusion.3.own), channel_id=1, source_target_pairs={{0,4},{1,5},{2,6},{3,7},{4,0},{5,1},{6,2},{7,3},{8,12},{9,13},{10,... | collective-permute-start | bytes 1179656 | tf_op jit(solution)/shard_map/ppermute | solution.py:622
  75.7 5.9 %collective-permute-done.8.w3 = bf16[384,768]{1,0:T(8,128)(2,1)} collective-permute-done((bf16[384,768]{1,0:T(8,128)(2,1)}, bf16[384,768]{1,0:T(8,128)(2,1)}, u32[]{:S(2)}, u32[]{:S(2)}) %collective-permute-start.8) | collective-permute-done | bytes 589856 | tf_op jit(solution)/shard_map/ppermute | solution.py:622
  81.6 8.3 %self_forward.1 = (bf16[448,768]{1,0:T(8,128)(2,1)}, bf16[448,768]{1,0:T(8,128)(2,1)}, bf16[3,448,128]{2,1,0:T(8,128)(2,1)}, bf16[3,448,128]{2,1,0:T(8,128)(2,1)...) custom-call(s32[8]{0:T(128)} %stack.107.scalars, ...), custom_call_target="tpu_custom_call" | custom-call | flops 16000000000 | bytes 1048576 | tf_op jit(solution)/shard_map/self_forward/pallas_call | solution.py:568
  89.9 15.3 %collective-permute-start.9 = (bf16[448,768]{1,0:T(8,128)(2,1)}, bf16[448,768]{1,0:T(8,128)(2,1)S(1)}, u32[]{:S(2)}, u32[]{:S(2)}) collective-permute-start(bf16[448,768]{1,0:T(8,128)(2,1)} %get-tuple-element.87.mine), channel_id=1, source_target_pairs={{0,4},{1,5},{2,6},{3,7},{4,0},{5,1},{6,2},{7,3},{8,12},{9,13},{10,... | collective-permute-start | bytes 2064392 | tf_op jit(solution)/shard_map/ppermute | solution.py:622
  105.2 26.3 %all-gather.2.cloned.1.call-done.w0 = bf16[3072,2304]{1,0:T(8,128)(2,1)} async-done(((bf16[96,2304]{1,0:T(8,128)(2,1)}), bf16[3072,2304]{1,0:T(8,128)(2,1)}) %all-gather.2.cloned.1.call-update) | async-done | bytes 14155792 | tf_op jit(solution)/shard_map/all_gather | solution.py:685
  131.5 7.9 %frame_project.1 = (bf16[1536,768]{1,0:T(8,128)(2,1)}, bf16[3,1536,128]{2,1,0:T(8,128)(2,1)}, bf16[3,1536,128]{2,1,0:T(8,128)(2,1)}) custom-call(s32[8]{0:T(128)} %stack.107.scalars, bf16[768,768]{1,0:T(8,128)(2,1)} %dynamic-slice_bitcast_fusion.own, bf16[768,768]{1,0:T(8,128)(2,1)} %copy-done.21, bf16[288,768]{1,0:T(8,128)(2,1)} %slice.259.halo, ...), custom_call_target="tpu_custom_call" | custom-call | flops 14000000000 | bytes 1048576 | tf_op jit(solution)/shard_map/frame_project/pallas_call | solution.py:568
  140.2 11.5 %cross_forward.1 = (f32[448,768]{1,0:T(8,128)}, bf16[448,768]{1,0:T(8,128)(2,1)}, bf16[3,448,128]{2,1,0:T(8,128)(2,1)}, f32[3,448,128]{2,1,0:T(8,128)}, f32[3,44...) custom-call(s32[8]{0:T(128)} %stack.107.scalars, bf16[448,768]{1,0:T(8,128)(2,1)} %get-tuple-element.86.hidden, ...), custom_call_target="tpu_custom_call" | custom-call | flops 22000001024 | bytes 1048576 | tf_op jit(solution)/shard_map/cross_forward/pallas_call | solution.py:568
  155.5 12.7 %unit_forward.1 = (f32[448,768]{1,0:T(8,128)}, bf16[448,768]{1,0:T(8,128)(2,1)}, bf16[448,768]{1,0:T(8,128)(2,1)}, bf16[448,1536]{1,0:T(8,128)(2,1)}, bf16[448,1...) custom-call(s32[8]{0:T(128)} %stack.107.scalars, ...), custom_call_target="tpu_custom_call" | custom-call | flops 28000000000 | bytes 1048576 | tf_op jit(solution)/shard_map/unit_forward/pallas_call | solution.py:568
  168.2 7.2 %unit_grads.1 = bf16[1536,1536]{1,0:T(8,128)(2,1)} custom-call(s32[8]{0:T(128)} %stack.107.scalars, bf16[448,768]{1,0:T(8,128)(2,1)} %get-tuple-element.98.norm, bf16[448,1536]{1,0:T(8,128)(2,1)} %get-tuple-element.99.pre, bf16[448,768]{1,0:T(8,128)(2,1)} %get-tuple-element.96.top.cotangent, bf16[448,1536]{1,0:T(8,128)(2,1)} %get-tuple-element.100.act), custom_call_target="tpu_custom_call" | custom-call | flops 17999998976 | bytes 1048576 | tf_op jit(solution)/shard_map/unit_grads/pallas_call | solution.py:568
  179.5 22.7 %cross_backward.1 = (f32[448,768]{1,0:T(8,128)}, bf16[448,768]{1,0:T(8,128)(2,1)}, bf16[448,384]{1,0:T(8,128)(2,1)}, bf16[3,448,128]{2,1,0:T(8,128)(2,1)}, bf16[...) custom-call(s32[8]{0:T(128)} %stack.107.scalars, ...), custom_call_target="tpu_custom_call" | custom-call | flops 41999998976 | bytes 1048576 | tf_op jit(solution)/shard_map/cross_backward/pallas_call | solution.py:568
  202.3 7.6 %cross_grads.1 = bf16[1536,768]{1,0:T(8,128)(2,1)} custom-call(s32[8]{0:T(128)} %stack.107.scalars, bf16[448,768]{1,0:T(8,128)(2,1)} %get-tuple-element.106.norm, bf16[1536,768]{1,0:T(8,128)(2,1)} %get-tuple-element.107.frames, bf16[448,768]{1,0:T(8,128)(2,1)} %get-tuple-element.108.low, bf16[448,384]{1,0:T(8,128)(2,1)} %get-tuple-element.109.att, ...), custom_call_target="tpu_custom_call" | custom-call | flops 16000000000 | bytes 1048576 | tf_op jit(solution)/shard_map/cross_grads/pallas_call | solution.py:568
  209.8 8.4 %frame_backward.1 = (bf16[768,768]{1,0:T(8,128)(2,1)}, bf16[768,768]{1,0:T(8,128)(2,1)}) custom-call(s32[8]{0:T(128)} %stack.107.scalars, bf16[3,1536,128]{2,1,0:T(8,128)(2,1)} %get-tuple-element.112.dk.dk_all, bf16[3,1536,128]{2,1,0:T(8,128)(2,1)} %get-tuple-element.111.dv.dv_all, bf16[3072,2304]{1,0:T(8,128)(2,1)} %all-gather.2.cloned.1.call-done.w0), custom_call_target="tpu_custom_call" | custom-call | flops 14000000000 | bytes 1048576 | tf_op jit(solution)/shard_map/frame_backward/pallas_call | solution.py:568
  230.8 12.0 %self_backward.1 = (f32[448,768]{1,0:T(8,128)}, bf16[448,768]{1,0:T(8,128)(2,1)}, bf16[448,384]{1,0:T(8,128)(2,1)}, bf16[3,448,128]{2,1,0:T(8,128)(2,1)}, bf16[3...) custom-call(s32[8]{0:T(128)} %stack.107.scalars, ...), custom_call_target="tpu_custom_call" | custom-call | flops 24000000000 | bytes 1048576 | tf_op jit(solution)/shard_map/self_backward/pallas_call | solution.py:568
  259.3 5.1 %self_grads.1 = bf16[1600,768]{1,0:T(8,128)(2,1)} custom-call(s32[8]{0:T(128)} %stack.107.scalars, bf16[448,768]{1,0:T(8,128)(2,1)} %get-tuple-element.142.norm, bf16[448,768]{1,0:T(8,128)(2,1)} %get-tuple-element.143.low, bf16[448,384]{1,0:T(8,128)(2,1)} %get-tuple-element.144.att, bf16[3,448,128]{2,1,0:T(8,128)(2,1)} %get-tuple-element.145.dq, ...), custom_call_target="tpu_custom_call" | custom-call | flops 10000000000 | bytes 1048576 | tf_op jit(solution)/shard_map/self_grads/pallas_call | solution.py:568
  264.4 10.6 %collective-permute-done.23 = bf16[96,768]{1,0:T(8,128)(2,1)} collective-permute-done((bf16[96,768]{1,0:T(8,128)(2,1)}, bf16[96,768]{1,0:T(8,128)(2,1)}, u32[]{:S(2)}, u32[]{:S(2)}) %collective-permute-start.23) | collective-permute-done | bytes 147488 | tf_op jit(solution)/shard_map/ppermute | solution.py:622
  276.9 7.8 %collective-permute-done.20 = bf16[1024,768]{1,0:T(8,128)(2,1)} collective-permute-done((bf16[1024,768]{1,0:T(8,128)(2,1)S(1)}, bf16[1024,768]{1,0:T(8,128)(2,1)}, u32[]{:S(2)}, u32[]{:S(2)}) %collective-permute-start.20) | collective-permute-done | bytes 1572896 | tf_op jit(solution)/shard_map/ppermute | solution.py:622
  289.5 7.4 %collective-permute-start.26 = (bf16[256,768]{1,0:T(8,128)(2,1)}, bf16[256,768]{1,0:T(8,128)(2,1)}, u32[]{:S(2)}, u32[]{:S(2)}) collective-permute-start(bf16[256,768]{1,0:T(8,128)(2,1)} %pad_maximum_fusion.8), channel_id=1, source_target_pairs={{0,2},{2,0},{5,7},{7,5},{8,10},{10,8},{13,15},{15,13},{16,18},{18,... | collective-permute-start | bytes 1179656 | tf_op jit(solution)/shard_map/ppermute | solution.py:622
  299.0 14.0 %collective-permute-done.21 = bf16[1024,768]{1,0:T(8,128)(2,1)} collective-permute-done((bf16[1024,768]{1,0:T(8,128)(2,1)}, bf16[1024,768]{1,0:T(8,128)(2,1)}, u32[]{:S(2)}, u32[]{:S(2)}) %collective-permute-start.21) | collective-permute-done | bytes 1572896 | tf_op jit(solution)/shard_map/ppermute | solution.py:622
  315.6 7.6 %collective-permute-done.27 = bf16[192,2304]{1,0:T(8,128)(2,1)} collective-permute-done((bf16[192,2304]{1,0:T(8,128)(2,1)}, bf16[192,2304]{1,0:T(8,128)(2,1)}, u32[]{:S(2)}, u32[]{:S(2)}) %collective-permute-start.27) | collective-permute-done | bytes 884768 | tf_op jit(solution)/shard_map/ppermute | solution.py:622
  339.7 9.5 %collective-permute-done.29 = bf16[208,768]{1,0:T(8,128)(2,1)S(1)} collective-permute-done((bf16[208,768]{1,0:T(8,128)(2,1)S(1)}, bf16[208,768]{1,0:T(8,128)(2,1)S(1)}, u32[]{:S(2)}, u32[]{:S(2)}) %collective-permute-start.29) | collective-permute-done | bytes 319520 | tf_op jit(solution)/shard_map/ppermute | solution.py:622
  350.6 17.1 %collective-permute-done.34 = bf16[192,2304]{1,0:T(8,128)(2,1)S(1)} collective-permute-done((bf16[192,2304]{1,0:T(8,128)(2,1)}, bf16[192,2304]{1,0:T(8,128)(2,1)S(1)}, u32[]{:S(2)}, u32[]{:S(2)}) %collective-permute-start.34) | collective-permute-done | bytes 884768 | tf_op jit(solution)/shard_map/ppermute | solution.py:622
  (213 shorter events, 119.7 us)
Async XLA Ops:
  7.2 124.3 %all-gather.2.cloned.1.call-start = ((), (), s32[]{:S(2)}) async-start(), calls=%async_computation.3 | async-start | bytes 14598144 | tf_op jit(solution)/shard_map/all_gather | solution.py:685
  11.1 219.7 %reduce-scatter.4.cloned.1.call-start = ((), (), s32[]{:S(2)}) async-start(), calls=%async_computation.4 | async-start | bytes 5898240 | tf_op jit(solution)/shard_map/reduce_scatter | solution.py:758
  12.3 15.9 %collective-permute-start.3 = (bf16[480,768]{1,0:T(8,128)(2,1)S(1)}, bf16[480,768]{1,0:T(8,128)(2,1)}, u32[]{:S(2)}, u32[]{:S(2)}) collective-permute-start(bf16[480,768]{1,0:T(8,128)(2,1)S(1)} %pad_maximum_fusion.5), channel_id=1, source_target_pairs={{4,8},{6,10},{9,5},{11,7},{12,16},{14,18},{17,13},{19,15},{20,24},... | collective-permute-start | bytes 2211848 | tf_op jit(solution)/shard_map/ppermute | solution.py:622
  28.2 23.8 %collective-permute-start.4 = (bf16[480,768]{1,0:T(8,128)(2,1)}, bf16[480,768]{1,0:T(8,128)(2,1)}, u32[]{:S(2)}, u32[]{:S(2)}) collective-permute-start(bf16[480,768]{1,0:T(8,128)(2,1)} %collective-permute-done.3), channel_id=1, source_target_pairs={{0,4},{2,6},{5,1},{7,3},{8,12},{10,14},{13,9},{15,11},{16,20},{18,... | collective-permute-start | bytes 2211848 | tf_op jit(solution)/shard_map/ppermute | solution.py:622
  53.2 22.5 %collective-permute-start.6 = (bf16[384,768]{1,0:T(8,128)(2,1)}, bf16[384,768]{1,0:T(8,128)(2,1)}, u32[]{:S(2)}, u32[]{:S(2)}) collective-permute-start(bf16[384,768]{1,0:T(8,128)(2,1)} %pad_maximum_fusion.6.w0), channel_id=1, source_target_pairs={{0,8},{1,9},{2,10},{3,11},{4,12},{5,13},{6,14},{7,15},{8,0},{9,1},... | collective-permute-start | bytes 1769480 | tf_op jit(solution)/shard_map/ppermute | solution.py:622
  55.9 19.8 %collective-permute-start.7 = (bf16[384,768]{1,0:T(8,128)(2,1)}, bf16[384,768]{1,0:T(8,128)(2,1)}, u32[]{:S(2)}, u32[]{:S(2)}) collective-permute-start(bf16[384,768]{1,0:T(8,128)(2,1)} %pad_maximum_fusion.6.w0), channel_id=1, source_target_pairs={{0,16},{1,17},{2,18},{3,19},{4,20},{5,21},{6,22},{7,23},{8,24},{9,... | collective-permute-start | bytes 1769480 | tf_op jit(solution)/shard_map/ppermute | solution.py:622
  58.5 23.1 %collective-permute-start.8 = (bf16[384,768]{1,0:T(8,128)(2,1)}, bf16[384,768]{1,0:T(8,128)(2,1)}, u32[]{:S(2)}, u32[]{:S(2)}) collective-permute-start(bf16[384,768]{1,0:T(8,128)(2,1)} %pad_maximum_fusion.6.w0), channel_id=1, source_target_pairs={{0,24},{1,25},{2,26},{3,27},{4,28},{5,29},{6,30},{7,31},{8,16},{9,... | collective-permute-start | bytes 1769480 | tf_op jit(solution)/shard_map/ppermute | solution.py:622
  72.3 32.9 %collective-permute-start.10 = (bf16[768,768]{1,0:T(8,128)(2,1)}, bf16[768,768]{1,0:T(8,128)(2,1)S(1)}, u32[]{:S(2)}, u32[]{:S(2)}) collective-permute-start(bf16[768,768]{1,0:T(8,128)(2,1)} %dynamic-slice_bitcast_fusion.own), channel_id=1, source_target_pairs={{0,4},{1,5},{2,6},{3,7},{4,0},{5,1},{6,2},{7,3},{8,12},{9,13},{10,... | collective-permute-start | bytes 3538952 | tf_op jit(solution)/shard_map/ppermute | solution.py:622
  89.9 49.5 %collective-permute-start.9 = (bf16[448,768]{1,0:T(8,128)(2,1)}, bf16[448,768]{1,0:T(8,128)(2,1)S(1)}, u32[]{:S(2)}, u32[]{:S(2)}) collective-permute-start(bf16[448,768]{1,0:T(8,128)(2,1)} %get-tuple-element.87.mine), channel_id=1, source_target_pairs={{0,4},{1,5},{2,6},{3,7},{4,0},{5,1},{6,2},{7,3},{8,12},{9,13},{10,... | collective-permute-start | bytes 2064392 | tf_op jit(solution)/shard_map/ppermute | solution.py:622
  175.4 101.4 %reduce-scatter.6.cloned.1.call-start = ((), (), s32[]{:S(2)}) async-start(), calls=%async_computation.5 | async-start | bytes 2949120 | tf_op jit(solution)/shard_map/reduce_scatter | solution.py:758
  176.8 41.8 %collective-permute-start.15 = (bf16[448,768]{1,0:T(8,128)(2,1)S(1)}, bf16[448,768]{1,0:T(8,128)(2,1)S(1)}, u32[]{:S(2)}, u32[]{:S(2)}) collective-permute-start(bf16[448,768]{1,0:T(8,128)(2,1)S(1)} %copy-done.23), channel_id=1, source_target_pairs={{0,4},{1,5},{2,6},{3,7},{4,0},{5,1},{6,2},{7,3},{8,12},{9,13},{10,... | collective-permute-start | bytes 2064392 | tf_op jit(solution)/shard_map/ppermute | solution.py:622
  223.6 20.4 %collective-permute-start.16 = (bf16[576,768]{1,0:T(8,128)(2,1)S(1)}, bf16[576,768]{1,0:T(8,128)(2,1)S(1)}, u32[]{:S(2)}, u32[]{:S(2)}) collective-permute-start(bf16[576,768]{1,0:T(8,128)(2,1)S(1)} %pad_maximum_fusion.3), channel_id=1, source_target_pairs={{1,0},{3,2},{4,5},{6,7},{9,8},{11,10},{12,13},{14,15},{17,16},{19,... | collective-permute-start | bytes 2654216 | tf_op jit(solution)/shard_map/ppermute | solution.py:622
  225.8 18.2 %collective-permute-start.17 = (bf16[384,768]{1,0:T(8,128)(2,1)}, bf16[384,768]{1,0:T(8,128)(2,1)S(1)}, u32[]{:S(2)}, u32[]{:S(2)}) collective-permute-start(bf16[384,768]{1,0:T(8,128)(2,1)} %pad_maximum_fusion.7), channel_id=1, source_target_pairs={{1,8},{3,10},{9,16},{11,18},{12,5},{14,7},{17,24},{19,26},{20,13},... | collective-permute-start | bytes 1769480 | tf_op jit(solution)/shard_map/ppermute | solution.py:622
  230.8 105.4 %reduce-scatter.8.cloned.1.call-start = ((), (), s32[]{:S(2)}) async-start(), calls=%async_computation.6 | async-start | bytes 3072000 | tf_op jit(solution)/shard_map/reduce_scatter | solution.py:758
  244.9 32.0 %collective-permute-start.19 = (bf16[1024,768]{1,0:T(8,128)(2,1)S(1)}, bf16[1024,768]{1,0:T(8,128)(2,1)S(1)}, u32[]{:S(2)}, u32[]{:S(2)}) collective-permute-start(bf16[1024,768]{1,0:T(8,128)(2,1)S(1)} %pad_maximum_fusion.1), channel_id=1, source_target_pairs={{0,1},{2,3},{5,4},{7,6},{8,9},{10,11},{13,12},{15,14},{16,17},{18,... | collective-permute-start | bytes 4718600 | tf_op jit(solution)/shard_map/ppermute | solution.py:622
  248.4 36.3 %collective-permute-start.20 = (bf16[1024,768]{1,0:T(8,128)(2,1)S(1)}, bf16[1024,768]{1,0:T(8,128)(2,1)}, u32[]{:S(2)}, u32[]{:S(2)}) collective-permute-start(bf16[1024,768]{1,0:T(8,128)(2,1)S(1)} %pad_maximum_fusion.1), channel_id=1, source_target_pairs={{0,2},{2,0},{5,7},{7,5},{8,10},{10,8},{13,15},{15,13},{16,18},{18,... | collective-permute-start | bytes 4718600 | tf_op jit(solution)/shard_map/ppermute | solution.py:622
  256.6 18.4 %collective-permute-start.23 = (bf16[96,768]{1,0:T(8,128)(2,1)}, bf16[96,768]{1,0:T(8,128)(2,1)}, u32[]{:S(2)}, u32[]{:S(2)}) collective-permute-start(bf16[96,768]{1,0:T(8,128)(2,1)} %get-tuple-element.139), channel_id=1, source_target_pairs={{1,0},{3,2},{4,5},{6,7},{9,8},{11,10},{12,13},{14,15},{17,16},{19,... | collective-permute-start | bytes 442376 | tf_op jit(solution)/shard_map/ppermute | solution.py:622
  257.9 17.1 %collective-permute-start.24 = (bf16[96,768]{1,0:T(8,128)(2,1)}, bf16[96,768]{1,0:T(8,128)(2,1)}, u32[]{:S(2)}, u32[]{:S(2)}) collective-permute-start(bf16[96,768]{1,0:T(8,128)(2,1)} %get-tuple-element.140), channel_id=1, source_target_pairs={{1,8},{3,10},{9,16},{11,18},{12,5},{14,7},{17,24},{19,26},{20,13},... | collective-permute-start | bytes 442376 | tf_op jit(solution)/shard_map/ppermute | solution.py:622
  284.7 28.3 %collective-permute-start.21 = (bf16[1024,768]{1,0:T(8,128)(2,1)}, bf16[1024,768]{1,0:T(8,128)(2,1)}, u32[]{:S(2)}, u32[]{:S(2)}) collective-permute-start(bf16[1024,768]{1,0:T(8,128)(2,1)} %collective-permute-done.20), channel_id=1, source_target_pairs={{0,1},{2,3},{5,4},{7,6},{8,9},{10,11},{13,12},{15,14},{16,17},{18,... | collective-permute-start | bytes 4718600 | tf_op jit(solution)/shard_map/ppermute | solution.py:622
  289.5 33.6 %collective-permute-start.27 = (bf16[192,2304]{1,0:T(8,128)(2,1)}, bf16[192,2304]{1,0:T(8,128)(2,1)}, u32[]{:S(2)}, u32[]{:S(2)}) collective-permute-start(bf16[192,2304]{1,0:T(8,128)(2,1)} %slice.269), channel_id=1, source_target_pairs={{0,1},{1,0},{2,3},{3,2},{4,5},{5,4},{6,7},{7,6},{8,9},{9,8},{10,11... | collective-permute-start | bytes 2654216 | tf_op jit(solution)/shard_map/ppermute | solution.py:622
  289.5 37.8 %collective-permute-start.26 = (bf16[256,768]{1,0:T(8,128)(2,1)}, bf16[256,768]{1,0:T(8,128)(2,1)}, u32[]{:S(2)}, u32[]{:S(2)}) collective-permute-start(bf16[256,768]{1,0:T(8,128)(2,1)} %pad_maximum_fusion.8), channel_id=1, source_target_pairs={{0,2},{2,0},{5,7},{7,5},{8,10},{10,8},{13,15},{15,13},{16,18},{18,... | collective-permute-start | bytes 1179656 | tf_op jit(solution)/shard_map/ppermute | solution.py:622
  297.0 40.3 %collective-permute-start.25 = (bf16[256,768]{1,0:T(8,128)(2,1)}, bf16[256,768]{1,0:T(8,128)(2,1)}, u32[]{:S(2)}, u32[]{:S(2)}) collective-permute-start(bf16[256,768]{1,0:T(8,128)(2,1)} %pad_maximum_fusion.8), channel_id=1, source_target_pairs={{0,1},{2,3},{5,4},{7,6},{8,9},{10,11},{13,12},{15,14},{16,17},{18,... | collective-permute-start | bytes 1179656 | tf_op jit(solution)/shard_map/ppermute | solution.py:622
  332.4 35.3 %collective-permute-start.34 = (bf16[192,2304]{1,0:T(8,128)(2,1)}, bf16[192,2304]{1,0:T(8,128)(2,1)S(1)}, u32[]{:S(2)}, u32[]{:S(2)}) collective-permute-start(bf16[192,2304]{1,0:T(8,128)(2,1)} %add_convert_fusion.1), channel_id=1, source_target_pairs={{2,0},{3,1},{4,6},{5,7},{10,8},{11,9},{12,14},{13,15},{18,16},{19,... | collective-permute-start | bytes 2654216 | tf_op jit(solution)/shard_map/ppermute | solution.py:622
  349.3 24.2 %collective-permute-start.32 = (bf16[192,768]{1,0:T(8,128)(2,1)S(1)}, bf16[192,768]{1,0:T(8,128)(2,1)S(1)}, u32[]{:S(2)}, u32[]{:S(2)}) collective-permute-start(bf16[192,768]{1,0:T(8,128)(2,1)S(1)} %add_convert_fusion.2), channel_id=1, source_target_pairs={{2,0},{3,1},{4,6},{5,7},{10,8},{11,9},{12,14},{13,15},{18,16},{19,... | collective-permute-start | bytes 884744 | tf_op jit(solution)/shard_map/ppermute | solution.py:622
  (46 other events, 284.8 us)
Sparse Core Ops, SparseCore 0:
  11.2 120.2 all-gather.1
  175.6 55.1 reduce-scatter.3
  233.8 38.1 reduce-scatter.5
  277.0 48.5 reduce-scatter.7

commit v5 on v4

--- a/solution.py
+++ b/solution.py
@@ -767,8 +767,8 @@
 
     def to_owner(paired, opposite):
         summed = paired.astype(F32) + opposite.astype(F32)
-        passed = move(summed[shard:], lambda a, z: (a ^ 1, z) if a % 2 == z // 2 else None)
-        return jnp.where(home, summed[:shard], passed)
+        passed = move(summed[shard:].astype(BF16), lambda a, z: (a ^ 1, z) if a % 2 == z // 2 else None)
+        return jnp.where(home, summed[:shard], passed.astype(F32))
 
     def grads_of(kernel, name, cost, size, scratch, *operands, added=0):
         return kernel_call(

time: 395 us -> 394 us (level)
  transfers between devices with their start and end apart: 40 -> 40, of which waited for: 16 -> 17; matrix products, arithmetic and copies ran while one was open for 10% -> 10% of each run, Pallas kernels for 20% -> 20%
where the time goes in v5:
time: 394 us; the launch traced here: 388 us
  waiting for transfers between devices  128 us (32%)
  Pallas kernels  110 us (28%)
  starting transfers between devices  81.7 us (21%)
  other arithmetic  25.5 us (6%)
  local copies, waits for them, and re-layouts  24.7 us (6%)
  between operations  17.4 us (4%)
    pallas_call x12, Pallas kernels, kernel_call(): pl.pallas_call(kernel, out_shape=tuple(outs), in_specs=list(spaces), out_...  110 us
    ppermute x36, waiting for transfers between devices, move(): return lax.ppermute(value, AXES, pairs_list)  97.5 us
    ppermute x36, starting transfers between devices, move(): return lax.ppermute(value, AXES, pairs_list)  81.1 us
    all_gather x1, waiting for transfers between devices, body(): rest_w = lax.all_gather(rest_piece, AXES, axis=0, tiled=True)  26.3 us
    another operation x6, other arithmetic, per_batch(): jnp.stack([jnp.where(batch == 0, near_copy, far_copy), jnp.where(batch ==...  9.82 us
  transfers between devices with their start and end apart: 40, of which 17 were waited for; matrix products, arithmetic and copies ran while one was open for 10% of the time, Pallas kernels for 20%

profile of v5, /device:TPU:0, one launch (start us, length us, event | category | flops | bytes accessed | tf_op | source)
XLA Modules:
  0.0 387.7 jit_solution(14346933295896700999)
XLA Ops:
  22.2 6.0 %collective-permute-start.1 = (bf16[200,768]{1,0:T(8,128)(2,1)}, bf16[200,768]{1,0:T(8,128)(2,1)}, u32[]{:S(2)}, u32[]{:S(2)}) collective-permute-start(bf16[200,768]{1,0:T(8,128)(2,1)} %maximum_maximum_fusion), channel_id=1, source_target_pairs={{0,2},{1,3},{6,4},{7,5},{8,10},{9,11},{14,12},{15,13},{16,18},{17,... | collective-permute-start | bytes 921608 | tf_op jit(solution)/shard_map/ppermute | solution.py:622
  36.4 5.4 %collective-permute-start.2 = (bf16[200,768]{1,0:T(8,128)(2,1)S(1)}, bf16[200,768]{1,0:T(8,128)(2,1)}, u32[]{:S(2)}, u32[]{:S(2)}) collective-permute-start(bf16[200,768]{1,0:T(8,128)(2,1)S(1)} %broadcast_select_fusion.3), channel_id=1, source_target_pairs={{0,1},{1,0},{2,3},{3,2},{4,5},{5,4},{6,7},{7,6},{8,9},{9,8},{10,11... | collective-permute-start | bytes 921608 | tf_op jit(solution)/shard_map/ppermute | solution.py:622
  41.9 8.3 %collective-permute-done.2 = bf16[200,768]{1,0:T(8,128)(2,1)} collective-permute-done((bf16[200,768]{1,0:T(8,128)(2,1)S(1)}, bf16[200,768]{1,0:T(8,128)(2,1)}, u32[]{:S(2)}, u32[]{:S(2)}) %collective-permute-start.2) | collective-permute-done | bytes 307232 | tf_op jit(solution)/shard_map/ppermute | solution.py:622
  60.5 6.7 %collective-permute-start.5 = (bf16[256,768]{1,0:T(8,128)(2,1)}, bf16[256,768]{1,0:T(8,128)(2,1)}, u32[]{:S(2)}, u32[]{:S(2)}) collective-permute-start(bf16[256,768]{1,0:T(8,128)(2,1)} %dynamic-slice_bitcast_fusion.3.own), channel_id=1, source_target_pairs={{0,4},{1,5},{2,6},{3,7},{4,0},{5,1},{6,2},{7,3},{8,12},{9,13},{10,... | collective-permute-start | bytes 1179656 | tf_op jit(solution)/shard_map/ppermute | solution.py:622
  75.7 5.9 %collective-permute-done.8.w3 = bf16[384,768]{1,0:T(8,128)(2,1)} collective-permute-done((bf16[384,768]{1,0:T(8,128)(2,1)}, bf16[384,768]{1,0:T(8,128)(2,1)}, u32[]{:S(2)}, u32[]{:S(2)}) %collective-permute-start.8) | collective-permute-done | bytes 589856 | tf_op jit(solution)/shard_map/ppermute | solution.py:622
  81.6 8.3 %self_forward.1 = (bf16[448,768]{1,0:T(8,128)(2,1)}, bf16[448,768]{1,0:T(8,128)(2,1)}, bf16[3,448,128]{2,1,0:T(8,128)(2,1)}, bf16[3,448,128]{2,1,0:T(8,128)(2,1)...) custom-call(s32[8]{0:T(128)} %stack.107.scalars, ...), custom_call_target="tpu_custom_call" | custom-call | flops 16000000000 | bytes 1048576 | tf_op jit(solution)/shard_map/self_forward/pallas_call | solution.py:568
  89.9 15.3 %collective-permute-start.9 = (bf16[448,768]{1,0:T(8,128)(2,1)}, bf16[448,768]{1,0:T(8,128)(2,1)S(1)}, u32[]{:S(2)}, u32[]{:S(2)}) collective-permute-start(bf16[448,768]{1,0:T(8,128)(2,1)} %get-tuple-element.87.mine), channel_id=1, source_target_pairs={{0,4},{1,5},{2,6},{3,7},{4,0},{5,1},{6,2},{7,3},{8,12},{9,13},{10,... | collective-permute-start | bytes 2064392 | tf_op jit(solution)/shard_map/ppermute | solution.py:622
  105.2 26.3 %all-gather.2.cloned.1.call-done.w0 = bf16[3072,2304]{1,0:T(8,128)(2,1)} async-done(((bf16[96,2304]{1,0:T(8,128)(2,1)}), bf16[3072,2304]{1,0:T(8,128)(2,1)}) %all-gather.2.cloned.1.call-update) | async-done | bytes 14155792 | tf_op jit(solution)/shard_map/all_gather | solution.py:685
  131.5 7.9 %frame_project.1 = (bf16[1536,768]{1,0:T(8,128)(2,1)}, bf16[3,1536,128]{2,1,0:T(8,128)(2,1)}, bf16[3,1536,128]{2,1,0:T(8,128)(2,1)}) custom-call(s32[8]{0:T(128)} %stack.107.scalars, bf16[768,768]{1,0:T(8,128)(2,1)} %dynamic-slice_bitcast_fusion.own, bf16[768,768]{1,0:T(8,128)(2,1)} %copy-done.19, bf16[288,768]{1,0:T(8,128)(2,1)} %slice.261.halo, ...), custom_call_target="tpu_custom_call" | custom-call | flops 14000000000 | bytes 1048576 | tf_op jit(solution)/shard_map/frame_project/pallas_call | solution.py:568
  140.2 11.5 %cross_forward.1 = (f32[448,768]{1,0:T(8,128)}, bf16[448,768]{1,0:T(8,128)(2,1)}, bf16[3,448,128]{2,1,0:T(8,128)(2,1)}, f32[3,448,128]{2,1,0:T(8,128)}, f32[3,44...) custom-call(s32[8]{0:T(128)} %stack.107.scalars, bf16[448,768]{1,0:T(8,128)(2,1)} %get-tuple-element.86.hidden, ...), custom_call_target="tpu_custom_call" | custom-call | flops 22000001024 | bytes 1048576 | tf_op jit(solution)/shard_map/cross_forward/pallas_call | solution.py:568
  155.5 12.7 %unit_forward.1 = (f32[448,768]{1,0:T(8,128)}, bf16[448,768]{1,0:T(8,128)(2,1)}, bf16[448,768]{1,0:T(8,128)(2,1)}, bf16[448,1536]{1,0:T(8,128)(2,1)}, bf16[448,1...) custom-call(s32[8]{0:T(128)} %stack.107.scalars, ...), custom_call_target="tpu_custom_call" | custom-call | flops 28000000000 | bytes 1048576 | tf_op jit(solution)/shard_map/unit_forward/pallas_call | solution.py:568
  168.2 7.2 %unit_grads.1 = bf16[1536,1536]{1,0:T(8,128)(2,1)} custom-call(s32[8]{0:T(128)} %stack.107.scalars, bf16[448,768]{1,0:T(8,128)(2,1)} %get-tuple-element.98.norm, bf16[448,1536]{1,0:T(8,128)(2,1)} %get-tuple-element.99.pre, bf16[448,768]{1,0:T(8,128)(2,1)} %get-tuple-element.96.top.cotangent, bf16[448,1536]{1,0:T(8,128)(2,1)} %get-tuple-element.100.act), custom_call_target="tpu_custom_call" | custom-call | flops 17999998976 | bytes 1048576 | tf_op jit(solution)/shard_map/unit_grads/pallas_call | solution.py:568
  179.5 22.7 %cross_backward.1 = (f32[448,768]{1,0:T(8,128)}, bf16[448,768]{1,0:T(8,128)(2,1)}, bf16[448,384]{1,0:T(8,128)(2,1)}, bf16[3,448,128]{2,1,0:T(8,128)(2,1)}, bf16[...) custom-call(s32[8]{0:T(128)} %stack.107.scalars, ...), custom_call_target="tpu_custom_call" | custom-call | flops 41999998976 | bytes 1048576 | tf_op jit(solution)/shard_map/cross_backward/pallas_call | solution.py:568
  202.2 7.6 %cross_grads.1 = bf16[1536,768]{1,0:T(8,128)(2,1)} custom-call(s32[8]{0:T(128)} %stack.107.scalars, bf16[448,768]{1,0:T(8,128)(2,1)} %get-tuple-element.106.norm, bf16[1536,768]{1,0:T(8,128)(2,1)} %get-tuple-element.107.frames, bf16[448,768]{1,0:T(8,128)(2,1)} %get-tuple-element.108.low, bf16[448,384]{1,0:T(8,128)(2,1)} %get-tuple-element.109.att, ...), custom_call_target="tpu_custom_call" | custom-call | flops 16000000000 | bytes 1048576 | tf_op jit(solution)/shard_map/cross_grads/pallas_call | solution.py:568
  209.8 8.4 %frame_backward.1 = (bf16[768,768]{1,0:T(8,128)(2,1)}, bf16[768,768]{1,0:T(8,128)(2,1)}) custom-call(s32[8]{0:T(128)} %stack.107.scalars, bf16[3,1536,128]{2,1,0:T(8,128)(2,1)} %get-tuple-element.112.dk.dk_all, bf16[3,1536,128]{2,1,0:T(8,128)(2,1)} %get-tuple-element.111.dv.dv_all, bf16[3072,2304]{1,0:T(8,128)(2,1)} %all-gather.2.cloned.1.call-done.w0), custom_call_target="tpu_custom_call" | custom-call | flops 14000000000 | bytes 1048576 | tf_op jit(solution)/shard_map/frame_backward/pallas_call | solution.py:568
  230.8 12.0 %self_backward.1 = (f32[448,768]{1,0:T(8,128)}, bf16[448,768]{1,0:T(8,128)(2,1)}, bf16[448,384]{1,0:T(8,128)(2,1)}, bf16[3,448,128]{2,1,0:T(8,128)(2,1)}, bf16[3...) custom-call(s32[8]{0:T(128)} %stack.107.scalars, ...), custom_call_target="tpu_custom_call" | custom-call | flops 24000000000 | bytes 1048576 | tf_op jit(solution)/shard_map/self_backward/pallas_call | solution.py:568
  259.2 5.1 %self_grads.1 = bf16[1600,768]{1,0:T(8,128)(2,1)} custom-call(s32[8]{0:T(128)} %stack.107.scalars, bf16[448,768]{1,0:T(8,128)(2,1)} %get-tuple-element.142.norm, bf16[448,768]{1,0:T(8,128)(2,1)} %get-tuple-element.143.low, bf16[448,384]{1,0:T(8,128)(2,1)} %get-tuple-element.144.att, bf16[3,448,128]{2,1,0:T(8,128)(2,1)} %get-tuple-element.145.dq, ...), custom_call_target="tpu_custom_call" | custom-call | flops 10000000000 | bytes 1048576 | tf_op jit(solution)/shard_map/self_grads/pallas_call | solution.py:568
  264.3 10.6 %collective-permute-done.23 = bf16[96,768]{1,0:T(8,128)(2,1)} collective-permute-done((bf16[96,768]{1,0:T(8,128)(2,1)}, bf16[96,768]{1,0:T(8,128)(2,1)}, u32[]{:S(2)}, u32[]{:S(2)}) %collective-permute-start.23) | collective-permute-done | bytes 147488 | tf_op jit(solution)/shard_map/ppermute | solution.py:622
  276.8 7.8 %collective-permute-done.20 = bf16[1024,768]{1,0:T(8,128)(2,1)} collective-permute-done((bf16[1024,768]{1,0:T(8,128)(2,1)S(1)}, bf16[1024,768]{1,0:T(8,128)(2,1)}, u32[]{:S(2)}, u32[]{:S(2)}) %collective-permute-start.20) | collective-permute-done | bytes 1572896 | tf_op jit(solution)/shard_map/ppermute | solution.py:622
  289.5 7.4 %collective-permute-start.26 = (bf16[256,768]{1,0:T(8,128)(2,1)}, bf16[256,768]{1,0:T(8,128)(2,1)}, u32[]{:S(2)}, u32[]{:S(2)}) collective-permute-start(bf16[256,768]{1,0:T(8,128)(2,1)} %pad_maximum_fusion.8), channel_id=1, source_target_pairs={{0,2},{2,0},{5,7},{7,5},{8,10},{10,8},{13,15},{15,13},{16,18},{18,... | collective-permute-start | bytes 1179656 | tf_op jit(solution)/shard_map/ppermute | solution.py:622
  299.0 14.0 %collective-permute-done.21 = bf16[1024,768]{1,0:T(8,128)(2,1)} collective-permute-done((bf16[1024,768]{1,0:T(8,128)(2,1)}, bf16[1024,768]{1,0:T(8,128)(2,1)}, u32[]{:S(2)}, u32[]{:S(2)}) %collective-permute-start.21) | collective-permute-done | bytes 1572896 | tf_op jit(solution)/shard_map/ppermute | solution.py:622
  315.5 7.6 %collective-permute-done.27 = bf16[192,2304]{1,0:T(8,128)(2,1)} collective-permute-done((bf16[192,2304]{1,0:T(8,128)(2,1)}, bf16[192,2304]{1,0:T(8,128)(2,1)}, u32[]{:S(2)}, u32[]{:S(2)}) %collective-permute-start.27) | collective-permute-done | bytes 884768 | tf_op jit(solution)/shard_map/ppermute | solution.py:622
  339.7 9.5 %collective-permute-done.29 = bf16[208,768]{1,0:T(8,128)(2,1)S(1)} collective-permute-done((bf16[208,768]{1,0:T(8,128)(2,1)S(1)}, bf16[208,768]{1,0:T(8,128)(2,1)S(1)}, u32[]{:S(2)}, u32[]{:S(2)}) %collective-permute-start.29) | collective-permute-done | bytes 319520 | tf_op jit(solution)/shard_map/ppermute | solution.py:622
  350.6 17.0 %collective-permute-done.34 = bf16[192,2304]{1,0:T(8,128)(2,1)S(1)} collective-permute-done((bf16[192,2304]{1,0:T(8,128)(2,1)}, bf16[192,2304]{1,0:T(8,128)(2,1)S(1)}, u32[]{:S(2)}, u32[]{:S(2)}) %collective-permute-start.34) | collective-permute-done | bytes 884768 | tf_op jit(solution)/shard_map/ppermute | solution.py:622
  (209 shorter events, 119.1 us)
Async XLA Ops:
  7.2 124.3 %all-gather.2.cloned.1.call-start = ((), (), s32[]{:S(2)}) async-start(), calls=%async_computation.3 | async-start | bytes 14598144 | tf_op jit(solution)/shard_map/all_gather | solution.py:685
  11.1 219.7 %reduce-scatter.4.cloned.1.call-start = ((), (), s32[]{:S(2)}) async-start(), calls=%async_computation.4 | async-start | bytes 5898240 | tf_op jit(solution)/shard_map/reduce_scatter | solution.py:758
  12.3 15.9 %collective-permute-start.3 = (bf16[480,768]{1,0:T(8,128)(2,1)S(1)}, bf16[480,768]{1,0:T(8,128)(2,1)}, u32[]{:S(2)}, u32[]{:S(2)}) collective-permute-start(bf16[480,768]{1,0:T(8,128)(2,1)S(1)} %pad_maximum_fusion.5), channel_id=1, source_target_pairs={{4,8},{6,10},{9,5},{11,7},{12,16},{14,18},{17,13},{19,15},{20,24},... | collective-permute-start | bytes 2211848 | tf_op jit(solution)/shard_map/ppermute | solution.py:622
  28.2 23.8 %collective-permute-start.4 = (bf16[480,768]{1,0:T(8,128)(2,1)}, bf16[480,768]{1,0:T(8,128)(2,1)}, u32[]{:S(2)}, u32[]{:S(2)}) collective-permute-start(bf16[480,768]{1,0:T(8,128)(2,1)} %collective-permute-done.3), channel_id=1, source_target_pairs={{0,4},{2,6},{5,1},{7,3},{8,12},{10,14},{13,9},{15,11},{16,20},{18,... | collective-permute-start | bytes 2211848 | tf_op jit(solution)/shard_map/ppermute | solution.py:622
  53.2 22.5 %collective-permute-start.6 = (bf16[384,768]{1,0:T(8,128)(2,1)}, bf16[384,768]{1,0:T(8,128)(2,1)}, u32[]{:S(2)}, u32[]{:S(2)}) collective-permute-start(bf16[384,768]{1,0:T(8,128)(2,1)} %pad_maximum_fusion.6.w0), channel_id=1, source_target_pairs={{0,8},{1,9},{2,10},{3,11},{4,12},{5,13},{6,14},{7,15},{8,0},{9,1},... | collective-permute-start | bytes 1769480 | tf_op jit(solution)/shard_map/ppermute | solution.py:622
  55.9 19.8 %collective-permute-start.7 = (bf16[384,768]{1,0:T(8,128)(2,1)}, bf16[384,768]{1,0:T(8,128)(2,1)}, u32[]{:S(2)}, u32[]{:S(2)}) collective-permute-start(bf16[384,768]{1,0:T(8,128)(2,1)} %pad_maximum_fusion.6.w0), channel_id=1, source_target_pairs={{0,16},{1,17},{2,18},{3,19},{4,20},{5,21},{6,22},{7,23},{8,24},{9,... | collective-permute-start | bytes 1769480 | tf_op jit(solution)/shard_map/ppermute | solution.py:622
  58.5 23.1 %collective-permute-start.8 = (bf16[384,768]{1,0:T(8,128)(2,1)}, bf16[384,768]{1,0:T(8,128)(2,1)}, u32[]{:S(2)}, u32[]{:S(2)}) collective-permute-start(bf16[384,768]{1,0:T(8,128)(2,1)} %pad_maximum_fusion.6.w0), channel_id=1, source_target_pairs={{0,24},{1,25},{2,26},{3,27},{4,28},{5,29},{6,30},{7,31},{8,16},{9,... | collective-permute-start | bytes 1769480 | tf_op jit(solution)/shard_map/ppermute | solution.py:622
  72.3 32.9 %collective-permute-start.10 = (bf16[768,768]{1,0:T(8,128)(2,1)}, bf16[768,768]{1,0:T(8,128)(2,1)S(1)}, u32[]{:S(2)}, u32[]{:S(2)}) collective-permute-start(bf16[768,768]{1,0:T(8,128)(2,1)} %dynamic-slice_bitcast_fusion.own), channel_id=1, source_target_pairs={{0,4},{1,5},{2,6},{3,7},{4,0},{5,1},{6,2},{7,3},{8,12},{9,13},{10,... | collective-permute-start | bytes 3538952 | tf_op jit(solution)/shard_map/ppermute | solution.py:622
  89.9 49.5 %collective-permute-start.9 = (bf16[448,768]{1,0:T(8,128)(2,1)}, bf16[448,768]{1,0:T(8,128)(2,1)S(1)}, u32[]{:S(2)}, u32[]{:S(2)}) collective-permute-start(bf16[448,768]{1,0:T(8,128)(2,1)} %get-tuple-element.87.mine), channel_id=1, source_target_pairs={{0,4},{1,5},{2,6},{3,7},{4,0},{5,1},{6,2},{7,3},{8,12},{9,13},{10,... | collective-permute-start | bytes 2064392 | tf_op jit(solution)/shard_map/ppermute | solution.py:622
  175.4 101.4 %reduce-scatter.6.cloned.1.call-start = ((), (), s32[]{:S(2)}) async-start(), calls=%async_computation.5 | async-start | bytes 2949120 | tf_op jit(solution)/shard_map/reduce_scatter | solution.py:758
  176.7 41.8 %collective-permute-start.15 = (bf16[448,768]{1,0:T(8,128)(2,1)S(1)}, bf16[448,768]{1,0:T(8,128)(2,1)S(1)}, u32[]{:S(2)}, u32[]{:S(2)}) collective-permute-start(bf16[448,768]{1,0:T(8,128)(2,1)S(1)} %copy-done.21), channel_id=1, source_target_pairs={{0,4},{1,5},{2,6},{3,7},{4,0},{5,1},{6,2},{7,3},{8,12},{9,13},{10,... | collective-permute-start | bytes 2064392 | tf_op jit(solution)/shard_map/ppermute | solution.py:622
  223.6 20.4 %collective-permute-start.16 = (bf16[576,768]{1,0:T(8,128)(2,1)S(1)}, bf16[576,768]{1,0:T(8,128)(2,1)S(1)}, u32[]{:S(2)}, u32[]{:S(2)}) collective-permute-start(bf16[576,768]{1,0:T(8,128)(2,1)S(1)} %pad_maximum_fusion.3), channel_id=1, source_target_pairs={{1,0},{3,2},{4,5},{6,7},{9,8},{11,10},{12,13},{14,15},{17,16},{19,... | collective-permute-start | bytes 2654216 | tf_op jit(solution)/shard_map/ppermute | solution.py:622
  225.8 18.1 %collective-permute-start.17 = (bf16[384,768]{1,0:T(8,128)(2,1)}, bf16[384,768]{1,0:T(8,128)(2,1)S(1)}, u32[]{:S(2)}, u32[]{:S(2)}) collective-permute-start(bf16[384,768]{1,0:T(8,128)(2,1)} %pad_maximum_fusion.7), channel_id=1, source_target_pairs={{1,8},{3,10},{9,16},{11,18},{12,5},{14,7},{17,24},{19,26},{20,13},... | collective-permute-start | bytes 1769480 | tf_op jit(solution)/shard_map/ppermute | solution.py:622
  230.8 105.3 %reduce-scatter.8.cloned.1.call-start = ((), (), s32[]{:S(2)}) async-start(), calls=%async_computation.6 | async-start | bytes 3072000 | tf_op jit(solution)/shard_map/reduce_scatter | solution.py:758
  244.8 31.9 %collective-permute-start.19 = (bf16[1024,768]{1,0:T(8,128)(2,1)S(1)}, bf16[1024,768]{1,0:T(8,128)(2,1)S(1)}, u32[]{:S(2)}, u32[]{:S(2)}) collective-permute-start(bf16[1024,768]{1,0:T(8,128)(2,1)S(1)} %pad_maximum_fusion.1), channel_id=1, source_target_pairs={{0,1},{2,3},{5,4},{7,6},{8,9},{10,11},{13,12},{15,14},{16,17},{18,... | collective-permute-start | bytes 4718600 | tf_op jit(solution)/shard_map/ppermute | solution.py:622
  248.3 36.3 %collective-permute-start.20 = (bf16[1024,768]{1,0:T(8,128)(2,1)S(1)}, bf16[1024,768]{1,0:T(8,128)(2,1)}, u32[]{:S(2)}, u32[]{:S(2)}) collective-permute-start(bf16[1024,768]{1,0:T(8,128)(2,1)S(1)} %pad_maximum_fusion.1), channel_id=1, source_target_pairs={{0,2},{2,0},{5,7},{7,5},{8,10},{10,8},{13,15},{15,13},{16,18},{18,... | collective-permute-start | bytes 4718600 | tf_op jit(solution)/shard_map/ppermute | solution.py:622
  256.6 18.4 %collective-permute-start.23 = (bf16[96,768]{1,0:T(8,128)(2,1)}, bf16[96,768]{1,0:T(8,128)(2,1)}, u32[]{:S(2)}, u32[]{:S(2)}) collective-permute-start(bf16[96,768]{1,0:T(8,128)(2,1)} %get-tuple-element.139), channel_id=1, source_target_pairs={{1,0},{3,2},{4,5},{6,7},{9,8},{11,10},{12,13},{14,15},{17,16},{19,... | collective-permute-start | bytes 442376 | tf_op jit(solution)/shard_map/ppermute | solution.py:622
  257.9 17.1 %collective-permute-start.24 = (bf16[96,768]{1,0:T(8,128)(2,1)}, bf16[96,768]{1,0:T(8,128)(2,1)}, u32[]{:S(2)}, u32[]{:S(2)}) collective-permute-start(bf16[96,768]{1,0:T(8,128)(2,1)} %get-tuple-element.140), channel_id=1, source_target_pairs={{1,8},{3,10},{9,16},{11,18},{12,5},{14,7},{17,24},{19,26},{20,13},... | collective-permute-start | bytes 442376 | tf_op jit(solution)/shard_map/ppermute | solution.py:622
  284.6 28.3 %collective-permute-start.21 = (bf16[1024,768]{1,0:T(8,128)(2,1)}, bf16[1024,768]{1,0:T(8,128)(2,1)}, u32[]{:S(2)}, u32[]{:S(2)}) collective-permute-start(bf16[1024,768]{1,0:T(8,128)(2,1)} %collective-permute-done.20), channel_id=1, source_target_pairs={{0,1},{2,3},{5,4},{7,6},{8,9},{10,11},{13,12},{15,14},{16,17},{18,... | collective-permute-start | bytes 4718600 | tf_op jit(solution)/shard_map/ppermute | solution.py:622
  289.5 33.6 %collective-permute-start.27 = (bf16[192,2304]{1,0:T(8,128)(2,1)}, bf16[192,2304]{1,0:T(8,128)(2,1)}, u32[]{:S(2)}, u32[]{:S(2)}) collective-permute-start(bf16[192,2304]{1,0:T(8,128)(2,1)} %slice.271), channel_id=1, source_target_pairs={{0,1},{1,0},{2,3},{3,2},{4,5},{5,4},{6,7},{7,6},{8,9},{9,8},{10,11... | collective-permute-start | bytes 2654216 | tf_op jit(solution)/shard_map/ppermute | solution.py:622
  289.5 37.8 %collective-permute-start.26 = (bf16[256,768]{1,0:T(8,128)(2,1)}, bf16[256,768]{1,0:T(8,128)(2,1)}, u32[]{:S(2)}, u32[]{:S(2)}) collective-permute-start(bf16[256,768]{1,0:T(8,128)(2,1)} %pad_maximum_fusion.8), channel_id=1, source_target_pairs={{0,2},{2,0},{5,7},{7,5},{8,10},{10,8},{13,15},{15,13},{16,18},{18,... | collective-permute-start | bytes 1179656 | tf_op jit(solution)/shard_map/ppermute | solution.py:622
  296.9 40.3 %collective-permute-start.25 = (bf16[256,768]{1,0:T(8,128)(2,1)}, bf16[256,768]{1,0:T(8,128)(2,1)}, u32[]{:S(2)}, u32[]{:S(2)}) collective-permute-start(bf16[256,768]{1,0:T(8,128)(2,1)} %pad_maximum_fusion.8), channel_id=1, source_target_pairs={{0,1},{2,3},{5,4},{7,6},{8,9},{10,11},{13,12},{15,14},{16,17},{18,... | collective-permute-start | bytes 1179656 | tf_op jit(solution)/shard_map/ppermute | solution.py:622
  332.3 35.3 %collective-permute-start.34 = (bf16[192,2304]{1,0:T(8,128)(2,1)}, bf16[192,2304]{1,0:T(8,128)(2,1)S(1)}, u32[]{:S(2)}, u32[]{:S(2)}) collective-permute-start(bf16[192,2304]{1,0:T(8,128)(2,1)} %add_convert_fusion.1), channel_id=1, source_target_pairs={{2,0},{3,1},{4,6},{5,7},{10,8},{11,9},{12,14},{13,15},{18,16},{19,... | collective-permute-start | bytes 2654216 | tf_op jit(solution)/shard_map/ppermute | solution.py:622
  349.3 25.9 %collective-permute-start.32 = (bf16[192,768]{1,0:T(8,128)(2,1)S(1)}, bf16[192,768]{1,0:T(8,128)(2,1)S(1)}, u32[]{:S(2)}, u32[]{:S(2)}) collective-permute-start(bf16[192,768]{1,0:T(8,128)(2,1)S(1)} %add_convert_fusion.2), channel_id=1, source_target_pairs={{2,0},{3,1},{4,6},{5,7},{10,8},{11,9},{12,14},{13,15},{18,16},{19,... | collective-permute-start | bytes 884744 | tf_op jit(solution)/shard_map/ppermute | solution.py:622
  (44 other events, 276.1 us)
Sparse Core Ops, SparseCore 0:
  11.2 120.2 all-gather.1
  175.5 55.1 reduce-scatter.3
  233.8 38.1 reduce-scatter.5
  276.9 48.5 reduce-scatter.7
